TPU v7x, 32 devices: a whole 2x2x4 slice. The times are simulated.
32 devices in a mesh: gx: 8 (over z, core), gy: 4 (over y, x).
Axes of the slice: x: 2, y: 2, z: 4, core: 2. Of those that a mesh axis runs over, the one named last changes fastest.
Arguments:
- iti: float32 [8, 4, 2, 512, 512], P('gx', 'gy'), may hold values from -3 to 3
- side: int32 [8, 4], P('gx', 'gy'), may hold values from 0 to 1, as said below
- owner: int32 [8, 4, 4], P('gx', 'gy'), may hold values from 0 to 3, each once within a row
Outputs:
- panels: float32 [8, 4, 2, 4, 96, 768], P('gx', 'gy')
Inputs may be any that keep to these rules, and one draw needn't show every extreme that they name: `side`: boxes (i, j) and (i + 4, j) are the two siblings of one parent and have different sides. `owner`: for each box the owners of its panels are all different.
All inputs are finite; a program needn't handle non-finite values.
Results may differ from a plain program's by a relative error of at most 0.0003.
Values sent between devices are 32-bit elements; how exact they have to be, the bound alone decides.
No kernel may reach another device: no remote copies, remote signals or barrier semaphores. Data moves between devices by JAX's collectives and lax.ppermute only.
A program may use at most 64 MiB of HBM per device.

v0:
```python
import math

import jax
import jax.numpy as jnp
from jax import lax
from jax.sharding import PartitionSpec as P

SWEEPS = 15


def from_partner(x, axis, bit):
    return lax.ppermute(x, axis, [(i, i ^ 1 << bit) for i in range(lax.axis_size(axis))])


def cprod(left, right):
    highest = lax.Precision.HIGHEST
    real_real = jnp.dot(left[0], right[0], precision=highest, preferred_element_type=jnp.float32)
    imag_imag = jnp.dot(left[1], right[1], precision=highest, preferred_element_type=jnp.float32)
    real_imag = jnp.dot(left[0], right[1], precision=highest, preferred_element_type=jnp.float32)
    imag_real = jnp.dot(left[1], right[0], precision=highest, preferred_element_type=jnp.float32)
    return jnp.stack([real_real - imag_imag, real_imag + imag_real])


def series_sum(interface, start):
    total = start
    power = interface
    levels = (SWEEPS + 1).bit_length() - 1
    for level in range(levels):
        total = total + cprod(power, total)
        if level + 1 < levels:
            power = cprod(power, power)
    return total


def on_device(iti, side, owner):
    ownmap = iti[0, 0]
    edge = ownmap.shape[-1] // 4
    ext = 3 * edge
    bit_index = lax.axis_size("gx").bit_length() - 2
    partner = from_partner(ownmap[:, ext:, :], "gx", bit_index)
    p_ss = partner[:, :, ext:]
    p_se = partner[:, :, :ext]
    interface = cprod(p_ss, ownmap[:, ext:, ext:])
    own_cols = cprod(p_ss, ownmap[:, ext:, :ext])
    flag = side[0, 0] == 1
    west_start = jnp.where(flag, p_se, own_cols)
    east_start = jnp.where(flag, own_cols, p_se)
    exterior = ownmap[:, :ext, :ext]
    zero = jnp.zeros_like(exterior)
    west_base = jnp.where(flag, zero, exterior)
    east_base = jnp.where(flag, exterior, zero)
    coupling = ownmap[:, :ext, ext:]
    weight = math.sqrt(edge)
    groups = lax.axis_size("gy")
    rows_each = ext // groups
    places = jnp.arange(groups, dtype=jnp.int32)
    match = (owner[0, 0][:, None] == places[None, :]).astype(jnp.int32)
    inverse = jnp.sum(places[:, None] * match, axis=0)
    merged = (
        jnp.concatenate([west_base, east_base], axis=-1)
        + cprod(coupling, series_sum(interface, jnp.concatenate([west_start, east_start], axis=-1)))
    ) * weight
    split = merged.reshape(2, groups, rows_each, merged.shape[-1])
    sent = jnp.take(split, inverse, axis=1)
    received = lax.all_to_all(sent, "gy", split_axis=1, concat_axis=1, tiled=True)
    return received[None, None]


def solution(mesh):
    in_specs = (P("gx", "gy", None, None, None), P("gx", "gy"), P("gx", "gy", None))
    out_specs = P("gx", "gy", None, None, None, None)
    return jax.shard_map(
        on_device, mesh=mesh, in_specs=in_specs, out_specs=out_specs, check_vma=False
    )
```

profile of v0, /device:TPU:8, one launch (start us, length us, event | category | flops | bytes accessed | tf_op | source)
XLA Modules:
  0.0 81.5 jit_solution(10900105465341544035)
XLA Ops:
  0.0 1.2 %slice.121 = f32[2,128,512]{2,1,0:T(8,128)S(1)} slice(f32[2,512,512]{2,1,0:T(8,128)} %bitcast.155), slice={[0:2], [384:512], [0:512]} | slice | bytes 1048576 | tf_op jit(solution)/shard_map/slice | solution.py:40
  1.2 2.7 %collective-permute-start = (f32[2,128,512]{2,1,0:T(8,128)S(1)}, f32[2,128,512]{2,1,0:T(8,128)S(1)}, u32[]{:S(2)}, u32[]{:S(2)}) collective-permute-start(f32[2,128,512]{2,1,0:T(8,128)S(1)} %slice.121), channel_id=1, source_target_pairs={{0,16},{4,20},{8,24},{12,28},{16,0},{20,4},{24,8},{28,12},{1,17},{... | collective-permute-start | bytes 1572872 | tf_op jit(solution)/shard_map/ppermute | solution.py:12
  4.5 0.7 select_reduce_fusion
  5.3 1.4 %slice_select_fusion.1 = (f32[2,384,384]{2,1,0:T(8,128)S(1)}, f32[2,384,384]{2,1,0:T(8,128)S(1)}) fusion(f32[2,512,512]{2,1,0:T(8,128)} %bitcast.156, pred[]{:T(512)} %bitcast.1), kind=kLoop, calls=%fused_computation.35 | loop fusion | flops 589824 | bytes 3538945 | tf_op jit(solution)/shard_map/jit(_where)/select_n | solution.py:50
  6.8 19.4 %collective-permute-done = f32[2,128,512]{2,1,0:T(8,128)S(1)} collective-permute-done((f32[2,128,512]{2,1,0:T(8,128)S(1)}, f32[2,128,512]{2,1,0:T(8,128)S(1)}, u32[]{:S(2)}, u32[]{:S(2)}) %collective-permute-start) | collective-permute-done | bytes 524320 | tf_op jit(solution)/shard_map/ppermute | solution.py:12
  26.2 0.3 fusion.25
  26.5 0.3 fusion.24
  26.8 0.2 fusion.27
  27.0 0.3 fusion.10
  27.4 0.3 fusion.9
  27.7 0.2 convolution_subtract_fusion.9
  28.0 0.5 fusion.32
  28.5 0.5 fusion.28
  28.9 0.2 fusion.39
  29.1 0.2 fusion.26
  29.3 0.2 convolution_add_fusion.9
  29.8 0.5 fusion.8
  30.2 0.5 fusion.7
  30.7 0.2 convolution_subtract_fusion.8
  31.1 0.5 fusion.16
  31.5 0.5 fusion.17
  32.0 0.2 fusion.41
  32.2 0.2 convolution_add_fusion.8
  32.6 0.5 fusion.6
  33.1 0.5 fusion.5
  33.6 0.2 convolution_subtract_fusion.7
  33.9 0.5 fusion.18
  34.4 0.5 fusion.19
  34.9 0.2 fusion.43
  35.1 0.2 convolution_add_fusion.7
  35.3 0.2 fusion.44
  35.5 0.5 fusion.4
  36.0 0.5 fusion.3
  36.5 0.2 convolution_subtract_fusion.6
  36.8 0.5 fusion.20
  37.3 0.5 fusion.21
  37.8 0.2 convolution_add_fusion.6
  38.0 0.5 fusion.2
  38.4 0.5 fusion.1
  39.1 1.1 %fusion.22 = f32[768,384]{0,1:T(8,128)S(1)} fusion(f32[2,128,768]{2,1,0:T(8,128)S(1)} %maximum_add_fusion.3, f32[2,512,512]{2,1,0:T(8,128)S(1)} %bitcast.165), kind=kOutput, calls=%fused_computation.64 | convolution fusion | flops 452984832 | bytes 1769472 | tf_op jit(solution)/shard_map/dot_general | solution.py:17
  40.2 1.3 %fusion.23 = f32[768,384]{0,1:T(8,128)S(1)} fusion(f32[2,128,768]{2,1,0:T(8,128)S(1)} %maximum_add_fusion.3, f32[2,512,512]{2,1,0:T(8,128)S(1)} %bitcast.166), kind=kOutput, calls=%fused_computation.65 | convolution fusion | flops 452984832 | bytes 1769472 | tf_op jit(solution)/shard_map/dot_general | solution.py:19
  41.5 1.1 %convolution_subtract_fusion = f32[768,384]{0,1:T(8,128)S(1)} fusion(f32[768,384]{0,1:T(8,128)S(1)} %fusion.22, f32[2,128,768]{2,1,0:T(8,128)S(1)} %maximum_add_fusion.3, f32[2,512,512]{2,1,0:T(8,128)S(1)} %bitcast.167), kind=kOutput, calls=%fused_computation.5 | convolution fusion | flops 453279744 | bytes 2949120 | tf_op jit(solution)/shard_map/dot_general | solution.py:18
  42.7 1.1 %convolution_add_fusion = f32[768,384]{0,1:T(8,128)S(1)} fusion(f32[768,384]{0,1:T(8,128)S(1)} %fusion.23, f32[2,128,768]{2,1,0:T(8,128)S(1)} %maximum_add_fusion.3, f32[2,512,512]{2,1,0:T(8,128)S(1)} %bitcast.168), kind=kOutput, calls=%fused_computation.4 | convolution fusion | flops 453279744 | bytes 2949120 | tf_op jit(solution)/shard_map/dot_general | solution.py:20
  43.8 0.3 fusion
  44.0 2.1 %gather_fusion = f32[4,2,96,768]{3,2,1,0:T(8,128)} fusion(f32[2,4,96,768]{3,2,1,0:T(8,128)S(1)} %fusion, s32[1024]{0:T(1024)S(1)} %pad_clamp_fusion), kind=kCustom, calls=%fused_computation | custom fusion | bytes 4718608 | tf_op jit(solution)/shard_map/jit(_take)/gather | solution.py:64
  46.1 1.9 %select_bitcast_fusion = f32[2,4,96,768]{3,2,0,1:T(8,128)S(1)} fusion(f32[4,2,96,768]{3,2,1,0:T(8,128)} %gather_fusion, pred[4]{0:T(512)(128)(4,1)S(1)} %compare_and_fusion), kind=kLoop, calls=%fused_computation.3 | loop fusion | flops 589824 | bytes 4718596 | tf_op jit(solution)/shard_map/jit(_take)/select_n | solution.py:64
  48.1 31.9 %all_to_all.5 = f32[2,4,96,768]{3,2,0,1:T(8,128)S(1)} all-to-all(f32[2,4,96,768]{3,2,0,1:T(8,128)S(1)} %select_bitcast_fusion), channel_id=1, replica_groups=mesh['gx'=8,'gy'=4] {'gy'}, dimensions={1} | all-to-all | bytes 4718592 | tf_op jit(solution)/shard_map/all_to_all | solution.py:65
  80.0 1.6 %copy.5 = f32[1,1,2,4,96,768]{5,4,3,2,1,0:T(8,128)} copy(f32[1,1,2,4,96,768]{5,4,2,3,1,0:T(8,128)S(1)} %bitcast.154) | data formatting | bytes 4718592 | tf_op jit(solution)/shard_map/broadcast_in_dim | solution.py:66
  (12 shorter events, 1.0 us)
Async XLA Ops:
  0.0 26.2 %copy-start = (f32[1,1,2,512,512]{4,3,2,1,0:T(8,128)S(1)}, f32[1,1,2,512,512]{4,3,2,1,0:T(8,128)}, u32[]{:S(2)}) copy-start(f32[1,1,2,512,512]{4,3,2,1,0:T(8,128)} %param.3) | copy-start | bytes 6291460
  1.2 25.0 %collective-permute-start = (f32[2,128,512]{2,1,0:T(8,128)S(1)}, f32[2,128,512]{2,1,0:T(8,128)S(1)}, u32[]{:S(2)}, u32[]{:S(2)}) collective-permute-start(f32[2,128,512]{2,1,0:T(8,128)S(1)} %slice.121), channel_id=1, source_target_pairs={{0,16},{4,20},{8,24},{12,28},{16,0},{20,4},{24,8},{28,12},{1,17},{... | collective-permute-start | bytes 1572872 | tf_op jit(solution)/shard_map/ppermute | solution.py:12
where the time goes:
time: 83.1 us; the launch traced here: 81.5 us
  blocking collectives  31.9 us (38%)
  waiting for transfers between devices  19.4 us (23%)
  matrix products  16.6 us (20%)
  other arithmetic  4.99 us (6%)
  local copies, waits for them, and re-layouts  4.89 us (6%)
  starting transfers between devices  2.65 us (3%)
  between operations  1.03 us (1%)
    all_to_all x1, blocking collectives, on_device(): lax.all_to_all(sent, 'gy', split_axis=1, concat_axis=1, tiled=True)  31.9 us
    ppermute x1, waiting for transfers between devices, from_partner(): lax.ppermute(x, axis, [(i, i ^ 1 << bit) for i in range(lax.axis_size(axi...  19.4 us
    dot_general x10, matrix products, cprod(): jnp.dot(left[0], right[1], precision=highest, preferred_element_type=jnp....  4.3 us
    dot_general x10, matrix products, cprod(): jnp.dot(left[1], right[0], precision=highest, preferred_element_type=jnp....  4.12 us
    dot_general x10, matrix products, cprod(): jnp.dot(left[1], right[1], precision=highest, preferred_element_type=jnp....  4.12 us
    dot_general x10, matrix products, cprod(): jnp.dot(left[0], right[0], precision=highest, preferred_element_type=jnp....  4.1 us
    ppermute x1, starting transfers between devices, from_partner(): lax.ppermute(x, axis, [(i, i ^ 1 << bit) for i in range(lax.axis_size(axi...  2.65 us
    gather x1, local copies, waits for them, and re-layouts, on_device(): sent = jnp.take(split, inverse, axis=1)  2.1 us
  transfers between devices with their start and end apart: 1, of which 1 were waited for; matrix products, arithmetic and copies ran while one was open for 3% of the time, Pallas kernels for 0%

commit v1 on v0

v1 whole, which is shorter than its diff:
```python
import functools
import math

import jax
import jax.numpy as jnp
from jax import lax
from jax.experimental import pallas as pl
from jax.experimental.pallas import tpu as pltpu
from jax.sharding import PartitionSpec as P

SWEEPS = 15
VMEM = pl.BlockSpec(memory_space=pltpu.VMEM)
SMEM = pl.BlockSpec(memory_space=pltpu.SMEM)
ANY = pl.BlockSpec(memory_space=pl.ANY)


def limit(mib):
    return pltpu.CompilerParams(vmem_limit_bytes=mib << 20)


def permute(x, axis, offset):
    return lax.ppermute(x, axis, [(i, i ^ offset) for i in range(lax.axis_size(axis))])


def halves(x):
    high = x.astype(jnp.bfloat16)
    return high, (x - high.astype(jnp.float32)).astype(jnp.bfloat16)


def matmul(left, right):
    dot = functools.partial(jnp.dot, preferred_element_type=jnp.float32)
    return dot(left[0], right[0]) + (dot(left[1], right[0]) + dot(left[0], right[1]))


def rows_of(ref, rows, cols):
    return jnp.concatenate([ref[0, rows, cols], ref[1, rows, cols]], axis=1)


def embed(x):
    half = x.shape[1] // 2
    real, imag = x[:, :half], x[:, half:]
    return halves(jnp.concatenate([x, jnp.concatenate([-imag, real], axis=1)], axis=0))


def panel_of(owner_ref, dest, groups):
    index = jnp.int32(0)
    for p in range(groups):
        index = jnp.where(owner_ref[p] == dest, jnp.int32(p), index)
    return index


def own_half_kernel(edge, ext, groups, owner_ref, iti_ref, qss_ref, high_ref, low_ref, *out_refs):
    rows_each = ext // groups
    me = lax.axis_index("gy")
    starts = [pl.multiple_of(panel_of(owner_ref, me ^ k, groups) * rows_each, 8) for k in range(groups)]
    weight = math.sqrt(edge)
    shared = slice(ext, ext + edge)
    rss = embed(rows_of(iti_ref, shared, shared))
    qss = halves(rows_of(qss_ref, slice(None), slice(None)))
    power = matmul(qss, rss)
    total = jnp.concatenate([rows_of(iti_ref, pl.ds(s, rows_each), shared) for s in starts], axis=0)
    rse = embed(rows_of(iti_ref, shared, slice(0, ext)))
    own_cols = embed(matmul(qss, rse))
    levels = (SWEEPS + 1).bit_length() - 1
    for level in range(levels):
        right = embed(power)
        if level + 1 < levels:
            power = matmul(halves(power), right)
        total = total + matmul(halves(total), right)
    total = halves(total)
    high_ref[...] = total[0]
    low_ref[...] = total[1]
    half = matmul(total, own_cols)
    for k in range(groups):
        for c in range(2):
            block = half[k * rows_each : (k + 1) * rows_each, c * ext : (c + 1) * ext]
            out_refs[k][c] = (iti_ref[c, pl.ds(starts[k], rows_each), 0:ext] + block) * weight


def other_half_kernel(edge, groups, high_ref, low_ref, qse_ref, *out_refs):
    rows_each = high_ref.shape[0] // groups
    weight = math.sqrt(edge)
    cols = qse_ref.shape[-1]
    half = matmul((high_ref[...], low_ref[...]), embed(rows_of(qse_ref, slice(None), slice(None))))
    for k in range(groups):
        for c in range(2):
            out_refs[k][c] = half[k * rows_each : (k + 1) * rows_each, c * cols : (c + 1) * cols] * weight


def store_kernel(groups, ext, first, side_refs, block_refs, out_ref, sems):
    me = lax.axis_index("gy")
    copies = []
    for k in range(groups):
        side = (side_refs[k][0] == 1).astype(jnp.int32)
        own = side * ext
        col = pl.multiple_of(own if first is None else (ext - own) + first, 128)
        rows, cols = block_refs[k].shape[1:]
        for c in range(2):
            copy = pltpu.make_async_copy(
                block_refs[k].at[c], out_ref.at[c, me ^ k, :, pl.ds(col, cols)], sems.at[k, c]
            )
            copy.start()
            copies.append(copy)
    for copy in copies:
        copy.wait()


def store(sides, blocks, first, ext, out=None):
    groups = len(blocks)
    rows = blocks[0].shape[1]
    shape = jax.ShapeDtypeStruct((2, groups, rows, 2 * ext), jnp.float32)

    def kernel(*refs):
        out_ref, sems = refs[-2:]
        store_kernel(groups, ext, first, refs[:groups], refs[groups : 2 * groups], out_ref, sems)

    args = [*sides, *blocks] + ([] if out is None else [out])
    return pl.pallas_call(
        kernel,
        out_shape=shape,
        in_specs=[SMEM] * groups + [VMEM] * groups + ([] if out is None else [ANY]),
        out_specs=ANY,
        compiler_params=limit(4),
        scratch_shapes=[pltpu.SemaphoreType.DMA((groups, 2))],
        input_output_aliases={} if out is None else {2 * groups: 0},
    )(*args)


def on_device(iti, side, owner):
    ownmap = iti[0, 0]
    edge = ownmap.shape[-1] // 4
    ext = 3 * edge
    groups = lax.axis_size("gy")
    rows_each = ext // groups
    across = lax.axis_size("gx") // 2
    mine = side[0]
    sides = [mine] + [permute(mine, "gy", k) for k in range(1, groups)]
    qss = permute(ownmap[:, ext:, ext:], "gx", across)
    cuts = [(0, 2 * edge), (2 * edge, ext)]
    qse = []
    gate = qss
    for lo, hi in cuts:
        part, gate = lax.optimization_barrier((ownmap[:, ext:, lo:hi], gate))
        gate = permute(part, "gx", across)
        qse.append(gate)
    panel = jax.ShapeDtypeStruct((2, rows_each, ext), jnp.float32)
    factor = jax.ShapeDtypeStruct((ext, 2 * edge), jnp.bfloat16)
    high, low, *blocks = pl.pallas_call(
        functools.partial(own_half_kernel, edge, ext, groups),
        out_shape=[factor, factor] + [panel] * groups,
        in_specs=[SMEM, VMEM, VMEM],
        out_specs=[VMEM] * (2 + groups),
        compiler_params=limit(24),
    )(owner[0, 0], ownmap, qss)
    blocks = [blocks[0]] + [permute(blocks[k], "gy", k) for k in range(1, groups)]
    out = store(sides, blocks, None, ext)
    for (lo, hi), part in zip(cuts, qse):
        panel = jax.ShapeDtypeStruct((2, rows_each, hi - lo), jnp.float32)
        blocks = pl.pallas_call(
            functools.partial(other_half_kernel, edge, groups),
            out_shape=[panel] * groups,
            in_specs=[VMEM] * 3,
            out_specs=[VMEM] * groups,
            compiler_params=limit(16),
        )(high, low, part)
        blocks = [blocks[0]] + [permute(blocks[k], "gy", k) for k in range(1, groups)]
        out = store(sides, blocks, lo, ext, out)
    return out[None, None]


def solution(mesh):
    in_specs = (P("gx", "gy", None, None, None), P("gx", "gy"), P("gx", "gy", None))
    out_specs = P("gx", "gy", None, None, None, None)
    return jax.shard_map(
        on_device, mesh=mesh, in_specs=in_specs, out_specs=out_specs, check_vma=False
    )
```

time: 83.1 us -> 59.7 us (0.72); the launches traced: 81.5 us -> 59.4 us
  blocking collectives: 31.9 us -> 0 us
  starting transfers between devices: 2.65 us -> 23.4 us
  matrix products: 16.6 us -> 0 us
  Pallas kernels: 0 us -> 12.2 us
  other arithmetic: 4.99 us -> 0 us
    all_to_all x1 -> x0, blocking collectives: 31.9 us -> none  [on_device(): lax.all_to_all(sent, 'gy', split_axis=1, concat_axis=1, tiled=True)]
    ppermute x1 -> x15, starting transfers between devices: 2.65 us -> 23.4 us  [permute(): lax.ppermute(x, axis, [(i, i ^ offset) for i in range(lax.axis_size(axis))])]
    dot_general x40 -> x0, matrix products: 16.6 us -> none  [the longest x10 4.3 us: cprod(): jnp.dot(left[0], right[1], precision=highest, preferred_element_type=jnp....]
    pallas_call x0 -> x6, Pallas kernels: none -> 12.2 us  [the longest x3 8.45 us: store(): pl.pallas_call(kernel, out_shape=shape, in_specs=[SMEM] * groups + [VMEM]...]
    select_n x4 -> x0, other arithmetic: 3.44 us -> none  [the longest x2 1.93 us: on_device(): sent = jnp.take(split, inverse, axis=1)]
    unnamed x2 -> x4, local copies, waits for them, and re-layouts: 0.01 us -> 2.25 us
    gather x1 -> x0, local copies, waits for them, and re-layouts: 2.1 us -> none  [on_device(): sent = jnp.take(split, inverse, axis=1)]
    broadcast_in_dim x1 -> x0, local copies, waits for them, and re-layouts: 1.56 us -> none  [on_device(): return received[None, None]]
  transfers between devices with their start and end apart: 1 -> 15, of which waited for: 1 -> 5; matrix products, arithmetic and copies ran while one was open for 3% -> 2% of each run, Pallas kernels for 0% -> 16%
where the time goes in v1:
time: 59.7 us; the launch traced here: 59.4 us
  starting transfers between devices  23.4 us (39%)
  waiting for transfers between devices  18.9 us (32%)
  Pallas kernels  12.2 us (20%)
  local copies, waits for them, and re-layouts  4.21 us (7%)
  between operations  0.76 us (1%)
    ppermute x15, starting transfers between devices, permute(): lax.ppermute(x, axis, [(i, i ^ offset) for i in range(lax.axis_size(axis))])  23.4 us
    ppermute x15, waiting for transfers between devices, permute(): lax.ppermute(x, axis, [(i, i ^ offset) for i in range(lax.axis_size(axis))])  18.9 us
    pallas_call x3, Pallas kernels, store(): pl.pallas_call(kernel, out_shape=shape, in_specs=[SMEM] * groups + [VMEM]...  8.45 us
    pallas_call x1, Pallas kernels, on_device(): pl.pallas_call(functools.partial(own_half_kernel, edge, ext, groups), out...  2.93 us
    unnamed x4, local copies, waits for them, and re-layouts  2.25 us
    slice x2, local copies, waits for them, and re-layouts, on_device(): part, gate = lax.optimization_barrier((ownmap[:, ext:, lo:hi], gate))  1.96 us
  transfers between devices with their start and end apart: 15, of which 5 were waited for; matrix products, arithmetic and copies ran while one was open for 2% of the time, Pallas kernels for 16%

profile of v1, /device:TPU:8, one launch (start us, length us, event | category | flops | bytes accessed | tf_op | source)
XLA Modules:
  0.0 59.4 jit_solution(16652579231721341467)
XLA Ops:
  0.0 1.0 %fusion = (f32[2,128,128]{2,1,0:T(8,128)S(1)}, f32[2,128,128]{2,1,0:T(8,128)S(1)}) fusion(f32[2,512,512]{2,1,0:T(8,128)} %bitcast.7), kind=kLoop, calls=%fused_computation | loop fusion | bytes 524288 | tf_op jit(solution)/shard_map/slice | solution.py:143
  1.0 2.7 %collective-permute-start.3 = (f32[2,128,128]{2,1,0:T(8,128)S(1)}, f32[2,128,128]{2,1,0:T(8,128)S(1)}, u32[]{:S(2)}, u32[]{:S(2)}) collective-permute-start(f32[2,128,128]{2,1,0:T(8,128)S(1)} %get-tuple-element.38), channel_id=1, source_target_pairs={{0,16},{4,20},{8,24},{12,28},{16,0},{20,4},{24,8},{28,12},{1,17},{... | collective-permute-start | bytes 393224 | tf_op jit(solution)/shard_map/ppermute | solution.py:22
  3.6 1.0 %slice.14 = f32[2,128,256]{2,1,0:T(8,128)S(1)} slice(f32[2,512,512]{2,1,0:T(8,128)} %bitcast.8), slice={[0:2], [384:512], [0:256]} | slice | bytes 524288 | tf_op jit(solution)/shard_map/slice | solution.py:143
  4.6 4.5 %collective-permute-done.3.qss_ref = f32[2,128,128]{2,1,0:T(8,128)S(1)} collective-permute-done((f32[2,128,128]{2,1,0:T(8,128)S(1)}, f32[2,128,128]{2,1,0:T(8,128)S(1)}, u32[]{:S(2)}, u32[]{:S(2)}) %collective-permute-start.3) | collective-permute-done | bytes 131104 | tf_op jit(solution)/shard_map/ppermute | solution.py:22
  9.1 3.4 %collective-permute-start.4 = (f32[2,128,256]{2,1,0:T(8,128)S(1)}, f32[2,128,256]{2,1,0:T(8,128)S(1)}, u32[]{:S(2)}, u32[]{:S(2)}) collective-permute-start(f32[2,128,256]{2,1,0:T(8,128)S(1)} %slice.14), channel_id=1, source_target_pairs={{0,16},{4,20},{8,24},{12,28},{16,0},{20,4},{24,8},{28,12},{1,17},{... | collective-permute-start | bytes 786440 | tf_op jit(solution)/shard_map/ppermute | solution.py:22
  12.5 0.0 copy-start
  12.5 1.6 %copy-done = f32[1,1,2,512,512]{4,3,2,1,0:T(8,128)S(1)} copy-done((f32[1,1,2,512,512]{4,3,2,1,0:T(8,128)S(1)}, f32[1,1,2,512,512]{4,3,2,1,0:T(8,128)}, u32[]{:S(2)}) %copy-start) | copy-done | bytes 2097176
  14.1 0.0 copy-start.1
  14.1 0.7 %copy-done.1 = s32[1,1,4]{2,1,0:T(1,128)S(1)} copy-done((s32[1,1,4]{2,1,0:T(1,128)S(1)}, s32[1,1,4]{2,1,0:T(1,128)}, u32[]{:S(2)}) %copy-start.1) | copy-done | bytes 40
  14.7 2.9 %shard_map.37 = (bf16[384,256]{1,0:T(8,128)(2,1)S(1)}, bf16[384,256]{1,0:T(8,128)(2,1)S(1)}, f32[2,96,384]{2,1,0:T(8,128)S(1)}, f32[2,96,384]{2,1,0:T(8,128)S(1)...) custom-call(s32[4]{0:T(128)S(1)} %bitcast.10, f32[2,512,512]{2,1,0:T(8,128)S(1)} %bitcast.9, ...), custom_call_target="tpu_custom_call" | custom-call | tf_op jit(solution)/shard_map/pallas_call | solution.py:148
  17.7 1.6 %collective-permute-start.12 = (f32[2,96,384]{2,1,0:T(8,128)S(1)}, f32[2,96,384]{2,1,0:T(8,128)S(1)}, u32[]{:S(2)}, u32[]{:S(2)}) collective-permute-start(f32[2,96,384]{2,1,0:T(8,128)S(1)} %get-tuple-element.34), channel_id=1, source_target_pairs={{0,1},{1,0},{2,3},{3,2},{4,5},{5,4},{6,7},{7,6},{8,9},{9,8},{10,11... | collective-permute-start | bytes 884744 | tf_op jit(solution)/shard_map/ppermute | solution.py:22
  19.2 1.5 %collective-permute-start.13 = (f32[2,96,384]{2,1,0:T(8,128)S(1)}, f32[2,96,384]{2,1,0:T(8,128)S(1)}, u32[]{:S(2)}, u32[]{:S(2)}) collective-permute-start(f32[2,96,384]{2,1,0:T(8,128)S(1)} %get-tuple-element.35), channel_id=1, source_target_pairs={{0,2},{1,3},{2,0},{3,1},{4,6},{5,7},{6,4},{7,5},{8,10},{9,11},{10,... | collective-permute-start | bytes 884744 | tf_op jit(solution)/shard_map/ppermute | solution.py:22
  20.7 0.5 collective-permute-start.14
  21.2 0.0 collective-permute-done.4.qse_ref
  21.2 2.9 %collective-permute-start.5 = (f32[2,128,128]{2,1,0:T(8,128)S(1)}, f32[2,128,128]{2,1,0:T(8,128)S(1)}, u32[]{:S(2)}, u32[]{:S(2)}) collective-permute-start(f32[2,128,128]{2,1,0:T(8,128)S(1)} %get-tuple-element.24), channel_id=1, source_target_pairs={{0,16},{4,20},{8,24},{12,28},{16,0},{20,4},{24,8},{28,12},{1,17},{... | collective-permute-start | bytes 393224 | tf_op jit(solution)/shard_map/ppermute | solution.py:22
  24.1 2.2 %collective-permute-start.2 = (s32[1]{0:T(128)}, s32[1]{0:T(128)}, u32[]{:S(2)}, u32[]{:S(2)}) collective-permute-start(s32[1]{0:T(128)} %bitcast), channel_id=1, source_target_pairs={{0,3},{1,2},{2,1},{3,0},{4,7},{5,6},{6,5},{7,4},{8,11},{9,10},{10,... | collective-permute-start | bytes 20 | tf_op jit(solution)/shard_map/ppermute | solution.py:22
  26.4 0.5 shard_map.39
  26.8 7.0 %collective-permute-done.2.refs_3_ = s32[1]{0:T(128)} collective-permute-done((s32[1]{0:T(128)}, s32[1]{0:T(128)}, u32[]{:S(2)}, u32[]{:S(2)}) %collective-permute-start.2) | collective-permute-done | bytes 36 | tf_op jit(solution)/shard_map/ppermute | solution.py:22
  33.8 0.5 collective-permute-start.1
  34.3 3.1 %collective-permute-done.1.refs_2_ = s32[1]{0:T(128)} collective-permute-done((s32[1]{0:T(128)}, s32[1]{0:T(128)}, u32[]{:S(2)}, u32[]{:S(2)}) %collective-permute-start.1) | collective-permute-done | bytes 36 | tf_op jit(solution)/shard_map/ppermute | solution.py:22
  37.5 1.4 %collective-permute-start = (s32[1]{0:T(128)}, s32[1]{0:T(128)}, u32[]{:S(2)}, u32[]{:S(2)}) collective-permute-start(s32[1]{0:T(128)} %bitcast), channel_id=1, source_target_pairs={{0,1},{1,0},{2,3},{3,2},{4,5},{5,4},{6,7},{7,6},{8,9},{9,8},{10,11... | collective-permute-start | bytes 20 | tf_op jit(solution)/shard_map/ppermute | solution.py:22
  38.9 2.4 %collective-permute-done.refs_1_ = s32[1]{0:T(128)} collective-permute-done((s32[1]{0:T(128)}, s32[1]{0:T(128)}, u32[]{:S(2)}, u32[]{:S(2)}) %collective-permute-start) | collective-permute-done | bytes 36 | tf_op jit(solution)/shard_map/ppermute | solution.py:22
  41.3 1.4 %collective-permute-start.9 = (f32[2,96,256]{2,1,0:T(8,128)S(1)}, f32[2,96,256]{2,1,0:T(8,128)S(1)}, u32[]{:S(2)}, u32[]{:S(2)}) collective-permute-start(f32[2,96,256]{2,1,0:T(8,128)S(1)} %get-tuple-element.30), channel_id=1, source_target_pairs={{0,1},{1,0},{2,3},{3,2},{4,5},{5,4},{6,7},{7,6},{8,9},{9,8},{10,11... | collective-permute-start | bytes 589832 | tf_op jit(solution)/shard_map/ppermute | solution.py:22
  42.7 0.0 collective-permute-done.12.refs_5_
  42.7 0.6 %collective-permute-start.10 = (f32[2,96,256]{2,1,0:T(8,128)S(1)}, f32[2,96,256]{2,1,0:T(8,128)S(1)}, u32[]{:S(2)}, u32[]{:S(2)}) collective-permute-start(f32[2,96,256]{2,1,0:T(8,128)S(1)} %get-tuple-element.31), channel_id=1, source_target_pairs={{0,2},{1,3},{2,0},{3,1},{4,6},{5,7},{6,4},{7,5},{8,10},{9,11},{10,... | collective-permute-start | bytes 589832 | tf_op jit(solution)/shard_map/ppermute | solution.py:22
  43.3 0.0 collective-permute-done.5.qse_ref
  43.3 1.5 %collective-permute-start.11 = (f32[2,96,256]{2,1,0:T(8,128)S(1)}, f32[2,96,256]{2,1,0:T(8,128)S(1)}, u32[]{:S(2)}, u32[]{:S(2)}) collective-permute-start(f32[2,96,256]{2,1,0:T(8,128)S(1)} %get-tuple-element.32), channel_id=1, source_target_pairs={{0,3},{1,2},{2,1},{3,0},{4,7},{5,6},{6,5},{7,4},{8,11},{9,10},{10,... | collective-permute-start | bytes 589832 | tf_op jit(solution)/shard_map/ppermute | solution.py:22
  44.8 0.3 shard_map.38
  45.1 0.0 collective-permute-done.13.refs_6_
  45.1 1.5 %collective-permute-start.6 = (f32[2,96,128]{2,1,0:T(8,128)S(1)}, f32[2,96,128]{2,1,0:T(8,128)S(1)}, u32[]{:S(2)}, u32[]{:S(2)}) collective-permute-start(f32[2,96,128]{2,1,0:T(8,128)S(1)} %get-tuple-element.26), channel_id=1, source_target_pairs={{0,1},{1,0},{2,3},{3,2},{4,5},{5,4},{6,7},{7,6},{8,9},{9,8},{10,11... | collective-permute-start | bytes 294920 | tf_op jit(solution)/shard_map/ppermute | solution.py:22
  46.6 0.0 collective-permute-done.14.refs_7_
  46.6 0.6 %collective-permute-start.7 = (f32[2,96,128]{2,1,0:T(8,128)S(1)}, f32[2,96,128]{2,1,0:T(8,128)S(1)}, u32[]{:S(2)}, u32[]{:S(2)}) collective-permute-start(f32[2,96,128]{2,1,0:T(8,128)S(1)} %get-tuple-element.27), channel_id=1, source_target_pairs={{0,2},{1,3},{2,0},{3,1},{4,6},{5,7},{6,4},{7,5},{8,10},{9,11},{10,... | collective-permute-start | bytes 294920 | tf_op jit(solution)/shard_map/ppermute | solution.py:22
  47.2 1.9 %collective-permute-done.9.refs_5_ = f32[2,96,256]{2,1,0:T(8,128)S(1)} collective-permute-done((f32[2,96,256]{2,1,0:T(8,128)S(1)}, f32[2,96,256]{2,1,0:T(8,128)S(1)}, u32[]{:S(2)}, u32[]{:S(2)}) %collective-permute-start.9) | collective-permute-done | bytes 196640 | tf_op jit(solution)/shard_map/ppermute | solution.py:22
  49.0 1.2 %collective-permute-start.8 = (f32[2,96,128]{2,1,0:T(8,128)S(1)}, f32[2,96,128]{2,1,0:T(8,128)S(1)}, u32[]{:S(2)}, u32[]{:S(2)}) collective-permute-start(f32[2,96,128]{2,1,0:T(8,128)S(1)} %get-tuple-element.28), channel_id=1, source_target_pairs={{0,3},{1,2},{2,1},{3,0},{4,7},{5,6},{6,5},{7,4},{8,11},{9,10},{10,... | collective-permute-start | bytes 294920 | tf_op jit(solution)/shard_map/ppermute | solution.py:22
  50.9 3.0 %shard_map.40.refs_8_ = f32[2,4,96,768]{3,2,1,0:T(8,128)} custom-call(s32[1]{0:T(128)} %bitcast.4.refs_0_, s32[1]{0:T(128)} %collective-permute-done.refs_1_, s32[1]{0:T(128)} %collective-permute-done.1.refs_2_, s32[1]{0:T(128)} %collective-permute-done.2.refs_3_, f32[2,96,384]{2,1,0:T(8,128)S(1)} %get-tuple-element.33.refs_4_, ...), custom_call_target="tpu_custom_call" | custom-call | tf_op jit(solution)/shard_map/pallas_call | solution.py:118
  53.9 0.0 collective-permute-done.10.refs_6_
  53.9 0.0 collective-permute-done.11.refs_7_
  53.9 2.8 %shard_map.41.refs_8_ = f32[2,4,96,768]{3,2,1,0:T(8,128)} custom-call(s32[1]{0:T(128)} %bitcast.5.refs_0_, s32[1]{0:T(128)} %collective-permute-done.refs_1_, s32[1]{0:T(128)} %collective-permute-done.1.refs_2_, s32[1]{0:T(128)} %collective-permute-done.2.refs_3_, f32[2,96,256]{2,1,0:T(8,128)S(1)} %get-tuple-element.29.refs_4_, ...), custom_call_target="tpu_custom_call", output_to_operand_aliasing={{}: (8, {})} | custom-call | tf_op jit(solution)/shard_map/pallas_call | solution.py:118
  56.7 0.0 collective-permute-done.6.refs_5_
  56.7 0.0 collective-permute-done.7.refs_6_
  56.7 0.0 collective-permute-done.8.refs_7_
  56.8 2.7 %shard_map.42 = f32[2,4,96,768]{3,2,1,0:T(8,128)} custom-call(s32[1]{0:T(128)} %bitcast.6.refs_0_, s32[1]{0:T(128)} %collective-permute-done.refs_1_, s32[1]{0:T(128)} %collective-permute-done.1.refs_2_, s32[1]{0:T(128)} %collective-permute-done.2.refs_3_, f32[2,96,128]{2,1,0:T(8,128)S(1)} %get-tuple-element.25.refs_4_, ...), custom_call_target="tpu_custom_call", output_to_operand_aliasing={{}: (8, {})} | custom-call | tf_op jit(solution)/shard_map/pallas_call | solution.py:118
Async XLA Ops:
  1.0 8.1 %collective-permute-start.3 = (f32[2,128,128]{2,1,0:T(8,128)S(1)}, f32[2,128,128]{2,1,0:T(8,128)S(1)}, u32[]{:S(2)}, u32[]{:S(2)}) collective-permute-start(f32[2,128,128]{2,1,0:T(8,128)S(1)} %get-tuple-element.38), channel_id=1, source_target_pairs={{0,16},{4,20},{8,24},{12,28},{16,0},{20,4},{24,8},{28,12},{1,17},{... | collective-permute-start | bytes 393224 | tf_op jit(solution)/shard_map/ppermute | solution.py:22
  9.1 12.1 %collective-permute-start.4 = (f32[2,128,256]{2,1,0:T(8,128)S(1)}, f32[2,128,256]{2,1,0:T(8,128)S(1)}, u32[]{:S(2)}, u32[]{:S(2)}) collective-permute-start(f32[2,128,256]{2,1,0:T(8,128)S(1)} %slice.14), channel_id=1, source_target_pairs={{0,16},{4,20},{8,24},{12,28},{16,0},{20,4},{24,8},{28,12},{1,17},{... | collective-permute-start | bytes 786440 | tf_op jit(solution)/shard_map/ppermute | solution.py:22
  12.5 1.6 %copy-start = (f32[1,1,2,512,512]{4,3,2,1,0:T(8,128)S(1)}, f32[1,1,2,512,512]{4,3,2,1,0:T(8,128)}, u32[]{:S(2)}) copy-start(f32[1,1,2,512,512]{4,3,2,1,0:T(8,128)} %param.3) | copy-start | bytes 6291460
  14.1 0.7 %copy-start.1 = (s32[1,1,4]{2,1,0:T(1,128)S(1)}, s32[1,1,4]{2,1,0:T(1,128)}, u32[]{:S(2)}) copy-start(s32[1,1,4]{2,1,0:T(1,128)} %param.5) | copy-start | bytes 52
  17.7 25.0 %collective-permute-start.12 = (f32[2,96,384]{2,1,0:T(8,128)S(1)}, f32[2,96,384]{2,1,0:T(8,128)S(1)}, u32[]{:S(2)}, u32[]{:S(2)}) collective-permute-start(f32[2,96,384]{2,1,0:T(8,128)S(1)} %get-tuple-element.34), channel_id=1, source_target_pairs={{0,1},{1,0},{2,3},{3,2},{4,5},{5,4},{6,7},{7,6},{8,9},{9,8},{10,11... | collective-permute-start | bytes 884744 | tf_op jit(solution)/shard_map/ppermute | solution.py:22
  19.2 25.9 %collective-permute-start.13 = (f32[2,96,384]{2,1,0:T(8,128)S(1)}, f32[2,96,384]{2,1,0:T(8,128)S(1)}, u32[]{:S(2)}, u32[]{:S(2)}) collective-permute-start(f32[2,96,384]{2,1,0:T(8,128)S(1)} %get-tuple-element.35), channel_id=1, source_target_pairs={{0,2},{1,3},{2,0},{3,1},{4,6},{5,7},{6,4},{7,5},{8,10},{9,11},{10,... | collective-permute-start | bytes 884744 | tf_op jit(solution)/shard_map/ppermute | solution.py:22
  20.7 25.8 %collective-permute-start.14 = (f32[2,96,384]{2,1,0:T(8,128)S(1)}, f32[2,96,384]{2,1,0:T(8,128)S(1)}, u32[]{:S(2)}, u32[]{:S(2)}) collective-permute-start(f32[2,96,384]{2,1,0:T(8,128)S(1)} %get-tuple-element.36), channel_id=1, source_target_pairs={{0,3},{1,2},{2,1},{3,0},{4,7},{5,6},{6,5},{7,4},{8,11},{9,10},{10,... | collective-permute-start | bytes 884744 | tf_op jit(solution)/shard_map/ppermute | solution.py:22
  21.2 22.1 %collective-permute-start.5 = (f32[2,128,128]{2,1,0:T(8,128)S(1)}, f32[2,128,128]{2,1,0:T(8,128)S(1)}, u32[]{:S(2)}, u32[]{:S(2)}) collective-permute-start(f32[2,128,128]{2,1,0:T(8,128)S(1)} %get-tuple-element.24), channel_id=1, source_target_pairs={{0,16},{4,20},{8,24},{12,28},{16,0},{20,4},{24,8},{28,12},{1,17},{... | collective-permute-start | bytes 393224 | tf_op jit(solution)/shard_map/ppermute | solution.py:22
  24.1 9.7 %collective-permute-start.2 = (s32[1]{0:T(128)}, s32[1]{0:T(128)}, u32[]{:S(2)}, u32[]{:S(2)}) collective-permute-start(s32[1]{0:T(128)} %bitcast), channel_id=1, source_target_pairs={{0,3},{1,2},{2,1},{3,0},{4,7},{5,6},{6,5},{7,4},{8,11},{9,10},{10,... | collective-permute-start | bytes 20 | tf_op jit(solution)/shard_map/ppermute | solution.py:22
  33.8 3.7 %collective-permute-start.1 = (s32[1]{0:T(128)}, s32[1]{0:T(128)}, u32[]{:S(2)}, u32[]{:S(2)}) collective-permute-start(s32[1]{0:T(128)} %bitcast), channel_id=1, source_target_pairs={{0,2},{1,3},{2,0},{3,1},{4,6},{5,7},{6,4},{7,5},{8,10},{9,11},{10,... | collective-permute-start | bytes 20 | tf_op jit(solution)/shard_map/ppermute | solution.py:22
  37.5 3.8 %collective-permute-start = (s32[1]{0:T(128)}, s32[1]{0:T(128)}, u32[]{:S(2)}, u32[]{:S(2)}) collective-permute-start(s32[1]{0:T(128)} %bitcast), channel_id=1, source_target_pairs={{0,1},{1,0},{2,3},{3,2},{4,5},{5,4},{6,7},{7,6},{8,9},{9,8},{10,11... | collective-permute-start | bytes 20 | tf_op jit(solution)/shard_map/ppermute | solution.py:22
  41.3 7.8 %collective-permute-start.9 = (f32[2,96,256]{2,1,0:T(8,128)S(1)}, f32[2,96,256]{2,1,0:T(8,128)S(1)}, u32[]{:S(2)}, u32[]{:S(2)}) collective-permute-start(f32[2,96,256]{2,1,0:T(8,128)S(1)} %get-tuple-element.30), channel_id=1, source_target_pairs={{0,1},{1,0},{2,3},{3,2},{4,5},{5,4},{6,7},{7,6},{8,9},{9,8},{10,11... | collective-permute-start | bytes 589832 | tf_op jit(solution)/shard_map/ppermute | solution.py:22
  42.7 11.2 %collective-permute-start.10 = (f32[2,96,256]{2,1,0:T(8,128)S(1)}, f32[2,96,256]{2,1,0:T(8,128)S(1)}, u32[]{:S(2)}, u32[]{:S(2)}) collective-permute-start(f32[2,96,256]{2,1,0:T(8,128)S(1)} %get-tuple-element.31), channel_id=1, source_target_pairs={{0,2},{1,3},{2,0},{3,1},{4,6},{5,7},{6,4},{7,5},{8,10},{9,11},{10,... | collective-permute-start | bytes 589832 | tf_op jit(solution)/shard_map/ppermute | solution.py:22
  43.3 10.6 %collective-permute-start.11 = (f32[2,96,256]{2,1,0:T(8,128)S(1)}, f32[2,96,256]{2,1,0:T(8,128)S(1)}, u32[]{:S(2)}, u32[]{:S(2)}) collective-permute-start(f32[2,96,256]{2,1,0:T(8,128)S(1)} %get-tuple-element.32), channel_id=1, source_target_pairs={{0,3},{1,2},{2,1},{3,0},{4,7},{5,6},{6,5},{7,4},{8,11},{9,10},{10,... | collective-permute-start | bytes 589832 | tf_op jit(solution)/shard_map/ppermute | solution.py:22
  45.1 11.6 %collective-permute-start.6 = (f32[2,96,128]{2,1,0:T(8,128)S(1)}, f32[2,96,128]{2,1,0:T(8,128)S(1)}, u32[]{:S(2)}, u32[]{:S(2)}) collective-permute-start(f32[2,96,128]{2,1,0:T(8,128)S(1)} %get-tuple-element.26), channel_id=1, source_target_pairs={{0,1},{1,0},{2,3},{3,2},{4,5},{5,4},{6,7},{7,6},{8,9},{9,8},{10,11... | collective-permute-start | bytes 294920 | tf_op jit(solution)/shard_map/ppermute | solution.py:22
  46.6 10.2 %collective-permute-start.7 = (f32[2,96,128]{2,1,0:T(8,128)S(1)}, f32[2,96,128]{2,1,0:T(8,128)S(1)}, u32[]{:S(2)}, u32[]{:S(2)}) collective-permute-start(f32[2,96,128]{2,1,0:T(8,128)S(1)} %get-tuple-element.27), channel_id=1, source_target_pairs={{0,2},{1,3},{2,0},{3,1},{4,6},{5,7},{6,4},{7,5},{8,10},{9,11},{10,... | collective-permute-start | bytes 294920 | tf_op jit(solution)/shard_map/ppermute | solution.py:22
  49.0 7.7 %collective-permute-start.8 = (f32[2,96,128]{2,1,0:T(8,128)S(1)}, f32[2,96,128]{2,1,0:T(8,128)S(1)}, u32[]{:S(2)}, u32[]{:S(2)}) collective-permute-start(f32[2,96,128]{2,1,0:T(8,128)S(1)} %get-tuple-element.28), channel_id=1, source_target_pairs={{0,3},{1,2},{2,1},{3,0},{4,7},{5,6},{6,5},{7,4},{8,11},{9,10},{10,... | collective-permute-start | bytes 294920 | tf_op jit(solution)/shard_map/ppermute | solution.py:22

commit v2 on v0

v2 whole, which is shorter than its diff:
```python
import functools
import math

import jax
import jax.numpy as jnp
from jax import lax
from jax.experimental import pallas as pl
from jax.experimental.pallas import tpu as pltpu
from jax.sharding import PartitionSpec as P


SWEEPS = 15
LEVELS = (SWEEPS + 1).bit_length() - 1
PIECES = 2
VMEM = pl.BlockSpec(memory_space=pltpu.VMEM)
SMEM = pl.BlockSpec(memory_space=pltpu.SMEM)
HBM = pl.BlockSpec(memory_space=pltpu.MemorySpace.HBM)


def limit(mib):
    return pltpu.CompilerParams(vmem_limit_bytes=mib << 20)


def f32(*shape):
    return jax.ShapeDtypeStruct(shape, jnp.float32)


def bf16(*shape):
    return jax.ShapeDtypeStruct(shape, jnp.bfloat16)


def permute(x, axis, offset):
    return lax.ppermute(x, axis, [(i, i ^ offset) for i in range(lax.axis_size(axis))])


def exchange(blocks):
    received = [blocks[0]]
    for k in range(1, len(blocks)):
        received.append(permute(blocks[k], "gy", k))
    return received


def call(kernel, **options):
    def run(*args):
        return pl.pallas_call(kernel, **options)(*args)

    return run


def halves(x):
    high = x.astype(jnp.bfloat16)
    return high, (x - high.astype(jnp.float32)).astype(jnp.bfloat16)


def matmul(left, right):
    dot = functools.partial(jnp.dot, preferred_element_type=jnp.float32)
    return dot(left[0], right[0]) + (dot(left[1], right[0]) + dot(left[0], right[1]))


def embed(real, imag):
    top = jnp.concatenate([real, imag], axis=1)
    return halves(jnp.concatenate([top, jnp.concatenate([-imag, real], axis=1)], axis=0))


def split_embed(x):
    half = x.shape[1] // 2
    return embed(x[:, :half], x[:, half:])


def panel_of(owner_ref, dest, groups):
    index = jnp.int32(0)
    for p in range(groups):
        index = jnp.where(owner_ref[p] == dest, jnp.int32(p), index)
    return index


def prepare_kernel(edge, ext, groups, cuts, owner_ref, iti_ref, *refs):
    parts, refs = refs[: len(cuts)], refs[len(cuts) :]
    base_ref, res_ref, res_high, res_low, rss_high, rss_low, rse_high, rse_low, shared_ref, sems = refs
    rows_each = ext // groups
    me = lax.axis_index("gy")
    pending = []

    def fetch(src, dst):
        copy = pltpu.make_async_copy(src, dst, sems.at[len(pending)])
        copy.start()
        pending.append(1)
        return copy

    shared = fetch(iti_ref.at[:, ext:, :], shared_ref)
    blocks, others = [], []
    for k in range(groups):
        start = pl.multiple_of(panel_of(owner_ref, me ^ k, groups) * rows_each, 8)
        rows = pl.ds(k * rows_each, rows_each)
        for c in range(2):
            blocks.append(fetch(iti_ref.at[c, pl.ds(start, rows_each), ext:], res_ref.at[rows, c * edge : (c + 1) * edge]))
            others.append(fetch(iti_ref.at[c, pl.ds(start, rows_each), :ext], base_ref.at[c, rows, :]))
    for (lo, hi), part in zip(cuts, parts):
        others.append(fetch(iti_ref.at[:, ext:, lo:hi], part))
    shared.wait()
    rss_high[...], rss_low[...] = embed(shared_ref[0, :, ext:], shared_ref[1, :, ext:])
    rse_high[...], rse_low[...] = embed(shared_ref[0, :, :ext], shared_ref[1, :, :ext])
    for copy in blocks:
        copy.wait()
    res_high[...], res_low[...] = halves(res_ref[...])
    for copy in others:
        copy.wait()


def factor_kernel(edge, ext, rows, qss_ref, base_ref, res_ref, res_high, res_low, rss_high, rss_low, rse_high, rse_low, *refs):
    pow_high, pow_low, cols_high, cols_low, far_high, far_low, out_ref = refs
    qss = halves(jnp.concatenate([qss_ref[0], qss_ref[1]], axis=1))
    power = matmul(qss, (rss_high[...], rss_low[...]))
    total = res_ref[ext - rows :]
    left = res_high[ext - rows :], res_low[ext - rows :]
    for level in range(LEVELS):
        right = split_embed(power)
        pow_high[level], pow_low[level] = right
        if level + 1 < LEVELS:
            both = matmul([jnp.concatenate(pair, axis=0) for pair in zip(halves(power), left)], right)
            power = both[:edge]
            total = total + both[edge:]
        else:
            total = total + matmul(left, right)
        left = halves(total)
    far_high[...], far_low[...] = left
    cols = split_embed(matmul(qss, (rse_high[...], rse_low[...])))
    cols_high[...], cols_low[...] = cols
    finish(edge, ext, [out_ref], matmul(left, cols), base_ref, ext - rows)


def finish(edge, ext, out_refs, half, base_ref, start):
    weight = math.sqrt(edge)
    rows = half.shape[0] // len(out_refs)
    for n, out_ref in enumerate(out_refs):
        for c in range(2):
            block = half[n * rows : (n + 1) * rows, c * ext : (c + 1) * ext]
            out_ref[c] = (base_ref[c, start + n * rows : start + (n + 1) * rows, :] + block) * weight


def own_half_kernel(edge, ext, rows, base_ref, res_ref, res_high, res_low, pow_high, pow_low, cols_high, cols_low, *refs):
    high_ref, low_ref, *out_refs = refs
    total = res_ref[: ext - rows]
    left = res_high[: ext - rows], res_low[: ext - rows]
    for level in range(LEVELS):
        total = total + matmul(left, (pow_high[level], pow_low[level]))
        left = halves(total)
    high_ref[...], low_ref[...] = left
    if out_refs:
        finish(edge, ext, out_refs, matmul([x[rows:] for x in left], (cols_high[...], cols_low[...])), base_ref, rows)


def mine_kernel(edge, ext, rows, base_ref, high_ref, low_ref, cols_high, cols_low, out_ref):
    half = matmul((high_ref[:rows], low_ref[:rows]), (cols_high[...], cols_low[...]))
    finish(edge, ext, [out_ref], half, base_ref, 0)


def other_half_kernel(edge, groups, high_ref, low_ref, far_high, far_low, qse_ref, *out_refs):
    weight = math.sqrt(edge)
    rows = far_high.shape[0]
    cols = qse_ref.shape[-1]
    left = [jnp.concatenate([a[...], b[...]], axis=0) for a, b in ((high_ref, far_high), (low_ref, far_low))]
    half = matmul(left, embed(qse_ref[0], qse_ref[1]))
    for k in range(groups):
        for c in range(2):
            out_refs[k][c] = half[k * rows : (k + 1) * rows, c * cols : (c + 1) * cols] * weight


def store(sides, parts, ext, out=None):
    groups = len(sides)
    count = groups * len(parts)
    rows = parts[0][1][0].shape[1]

    def kernel(*refs):
        out_ref, sems = refs[-2:]
        me = lax.axis_index("gy")
        copies = []
        for k in range(groups):
            own = (jnp.max(refs[k][...]) > 0.5).astype(jnp.int32) * ext
            for n, (first, _) in enumerate(parts):
                block = refs[groups + n * groups + k]
                col = pl.multiple_of(own if first is None else ext - own + first, 128)
                for c in range(2):
                    dst = out_ref.at[c, me ^ k, :, pl.ds(col, block.shape[-1])]
                    copy = pltpu.make_async_copy(block.at[c], dst, sems.at[2 * (n * groups + k) + c])
                    copy.start()
                    copies.append(copy)
        for copy in copies:
            copy.wait()

    args = [*sides, *(b for _, blocks in parts for b in blocks)] + ([] if out is None else [out])
    return call(
        kernel,
        out_shape=f32(2, groups, rows, 2 * ext),
        in_specs=[VMEM] * (groups + count) + ([] if out is None else [HBM]),
        out_specs=HBM,
        scratch_shapes=[pltpu.SemaphoreType.DMA((2 * count,))],
        input_output_aliases={} if out is None else {groups + count: 0},
        compiler_params=limit(4),
    )(*args)


def on_device(iti, side, owner):
    ownmap = iti[0, 0]
    edge = ownmap.shape[-1] // 4
    ext = 3 * edge
    groups = lax.axis_size("gy")
    rows_each = ext // groups
    across = lax.axis_size("gx") // 2
    cuts = [(0 * edge, 2 * edge), (2 * edge, 3 * edge)]
    assert len(cuts) == PIECES
    qss = permute(ownmap[:, ext:, ext:], "gx", across)
    *pieces, base, res, res_high, res_low, rss_high, rss_low, rse_high, rse_low = call(
        functools.partial(prepare_kernel, edge, ext, groups, cuts),
        out_shape=[f32(2, edge, hi - lo) for lo, hi in cuts]
        + [f32(2, ext, ext), f32(ext, 2 * edge), bf16(ext, 2 * edge), bf16(ext, 2 * edge)]
        + [bf16(2 * edge, 2 * edge)] * 2
        + [bf16(2 * edge, 2 * ext)] * 2,
        in_specs=[SMEM, HBM],
        out_specs=[VMEM] * (8 + len(cuts)),
        scratch_shapes=[pltpu.VMEM((2, edge, 4 * edge), jnp.float32), pltpu.SemaphoreType.DMA((1 + 4 * groups + len(cuts),))],
        compiler_params=limit(12),
    )(owner[0, 0], ownmap)
    pow_high, pow_low, cols_high, cols_low, far_high, far_low, farthest = call(
        functools.partial(factor_kernel, edge, ext, rows_each),
        out_shape=[bf16(LEVELS, 2 * edge, 2 * edge)] * 2
        + [bf16(2 * edge, 2 * ext)] * 2
        + [bf16(rows_each, 2 * edge)] * 2
        + [f32(2, rows_each, ext)],
        in_specs=[VMEM] * 9,
        out_specs=[VMEM] * 7,
        compiler_params=limit(16),
    )(qss, base, res, res_high, res_low, rss_high, rss_low, rse_high, rse_low)
    qse = []
    for piece in pieces:
        if qse:
            piece, qse[-1] = lax.optimization_barrier((piece, qse[-1]))
        else:
            piece, far_high = lax.optimization_barrier((piece, far_high))
        qse.append(permute(piece, "gx", across))
    high, low, *own = call(
        functools.partial(own_half_kernel, edge, ext, rows_each),
        out_shape=[bf16(ext - rows_each, 2 * edge)] * 2 + [f32(2, rows_each, ext)] * (groups - 2),
        in_specs=[VMEM] * 8,
        out_specs=[VMEM] * groups,
        compiler_params=limit(16),
    )(base, res, res_high, res_low, pow_high, pow_low, cols_high, cols_low)
    mine = call(
        functools.partial(mine_kernel, edge, ext, rows_each),
        out_shape=f32(2, rows_each, ext),
        in_specs=[VMEM] * 5,
        out_specs=VMEM,
        compiler_params=limit(16),
    )(base, high, low, cols_high, cols_low)
    own = [mine, *own, farthest]
    own = exchange(own)
    flag = jnp.full((8, 128), side[0, 0].astype(jnp.float32))
    flag, high = lax.optimization_barrier((flag, high))
    sides = exchange([flag] * groups)
    parts = []
    for (lo, hi), part in zip(cuts, qse):
        blocks = call(
            functools.partial(other_half_kernel, edge, groups),
            out_shape=[f32(2, rows_each, hi - lo)] * groups,
            in_specs=[VMEM] * 5,
            out_specs=[VMEM] * groups,
            compiler_params=limit(12),
        )(high, low, far_high, far_low, part)
        parts.append((lo, exchange(blocks)))
    out = store(sides, [(None, own), *parts[:-1]], ext)
    out = store(sides, parts[-1:], ext, out)
    return out[None, None]


def solution(mesh):
    in_specs = (P("gx", "gy", None, None, None), P("gx", "gy"), P("gx", "gy", None))
    out_specs = P("gx", "gy", None, None, None, None)
    return jax.shard_map(on_device, mesh=mesh, in_specs=in_specs, out_specs=out_specs, check_vma=False)
```

time: 83.1 us -> 54.6 us (0.66); the launches traced: 81.5 us -> 54.4 us
  blocking collectives: 31.9 us -> 0 us
  starting transfers between devices: 2.65 us -> 23.1 us
  matrix products: 16.6 us -> 0 us
  Pallas kernels: 0 us -> 8.25 us
  other arithmetic: 4.99 us -> 0 us
  local copies, waits for them, and re-layouts: 4.89 us -> 3.17 us
    all_to_all x1 -> x0, blocking collectives: 31.9 us -> none  [on_device(): lax.all_to_all(sent, 'gy', split_axis=1, concat_axis=1, tiled=True)]
    ppermute x1 -> x15, starting transfers between devices: 2.65 us -> 23.1 us  [permute(): lax.ppermute(x, axis, [(i, i ^ offset) for i in range(lax.axis_size(axis))])]
    dot_general x40 -> x0, matrix products: 16.6 us -> none  [the longest x10 4.3 us: cprod(): jnp.dot(left[0], right[1], precision=highest, preferred_element_type=jnp....]
    pallas_call x0 -> x8, Pallas kernels: none -> 8.25 us  [run(): return pl.pallas_call(kernel, **options)(*args)]
    select_n x4 -> x0, other arithmetic: 3.44 us -> none  [the longest x2 1.93 us: on_device(): sent = jnp.take(split, inverse, axis=1)]
    unnamed x2 -> x4, local copies, waits for them, and re-layouts: 0.01 us -> 2.25 us
    gather x1 -> x0, local copies, waits for them, and re-layouts: 2.1 us -> none  [on_device(): sent = jnp.take(split, inverse, axis=1)]
    broadcast_in_dim x1, local copies, waits for them, and re-layouts: 1.56 us -> 0.01 us  [on_device(): flag = jnp.full((8, 128), side[0, 0].astype(jnp.float32))]
  transfers between devices with their start and end apart: 1 -> 15, of which waited for: 1 -> 8; matrix products, arithmetic and copies ran while one was open for 3% -> 0% of each run, Pallas kernels for 0% -> 10%
where the time goes in v2:
time: 54.6 us; the launch traced here: 54.4 us
  starting transfers between devices  23.1 us (42%)
  waiting for transfers between devices  19.1 us (35%)
  Pallas kernels  8.25 us (15%)
  local copies, waits for them, and re-layouts  3.17 us (6%)
  between operations  0.76 us (1%)
    ppermute x15, starting transfers between devices, permute(): lax.ppermute(x, axis, [(i, i ^ offset) for i in range(lax.axis_size(axis))])  23.1 us
    ppermute x15, waiting for transfers between devices, permute(): lax.ppermute(x, axis, [(i, i ^ offset) for i in range(lax.axis_size(axis))])  19.1 us
    pallas_call x8, Pallas kernels, run(): return pl.pallas_call(kernel, **options)(*args)  8.25 us
    unnamed x4, local copies, waits for them, and re-layouts  2.25 us
  transfers between devices with their start and end apart: 15, of which 8 were waited for; matrix products, arithmetic and copies ran while one was open for 0% of the time, Pallas kernels for 10%

profile of v2, /device:TPU:8, one launch (start us, length us, event | category | flops | bytes accessed | tf_op | source)
XLA Modules:
  0.0 54.4 jit_solution(11700003298561467571)
XLA Ops:
  0.0 0.9 %slice.4 = f32[2,128,128]{2,1,0:T(8,128)S(1)} slice(f32[2,512,512]{2,1,0:T(8,128)} %bitcast.4), slice={[0:2], [384:512], [384:512]} | slice | bytes 262144 | tf_op jit(solution)/shard_map/slice | solution.py:212
  0.9 2.7 %collective-permute-start = (f32[2,128,128]{2,1,0:T(8,128)S(1)}, f32[2,128,128]{2,1,0:T(8,128)S(1)}, u32[]{:S(2)}, u32[]{:S(2)}) collective-permute-start(f32[2,128,128]{2,1,0:T(8,128)S(1)} %slice.4), channel_id=1, source_target_pairs={{0,16},{4,20},{8,24},{12,28},{16,0},{20,4},{24,8},{28,12},{1,17},{... | collective-permute-start | bytes 393224 | tf_op jit(solution)/shard_map/ppermute | solution.py:33
  3.6 0.0 copy-start
  3.6 1.6 %copy-done = f32[1,1,2,512,512]{4,3,2,1,0:T(8,128)S(1)} copy-done((f32[1,1,2,512,512]{4,3,2,1,0:T(8,128)S(1)}, f32[1,1,2,512,512]{4,3,2,1,0:T(8,128)}, u32[]{:S(2)}) %copy-start) | copy-done | bytes 2097176
  5.2 0.0 copy-start.1
  5.2 0.7 %copy-done.1 = s32[1,1,4]{2,1,0:T(1,128)S(1)} copy-done((s32[1,1,4]{2,1,0:T(1,128)S(1)}, s32[1,1,4]{2,1,0:T(1,128)}, u32[]{:S(2)}) %copy-start.1) | copy-done | bytes 40
  5.8 1.3 %shard_map.37 = (f32[2,128,256]{2,1,0:T(8,128)S(1)}, f32[2,128,128]{2,1,0:T(8,128)S(1)}, f32[2,384,384]{2,1,0:T(8,128)S(1)}, f32[384,256]{1,0:T(8,128)S(1)}, bf1...) custom-call(s32[4]{0:T(128)S(1)} %bitcast.6, ...), custom_call_target="tpu_custom_call" | custom-call | tf_op jit(solution)/shard_map/pallas_call | solution.py:45
  7.1 1.9 %collective-permute-done.qss_ref = f32[2,128,128]{2,1,0:T(8,128)S(1)} collective-permute-done((f32[2,128,128]{2,1,0:T(8,128)S(1)}, f32[2,128,128]{2,1,0:T(8,128)S(1)}, u32[]{:S(2)}, u32[]{:S(2)}) %collective-permute-start) | collective-permute-done | bytes 131104 | tf_op jit(solution)/shard_map/ppermute | solution.py:33
  9.0 1.8 %shard_map.38 = (bf16[4,256,256]{2,1,0:T(8,128)(2,1)S(1)}, bf16[4,256,256]{2,1,0:T(8,128)(2,1)S(1)}, bf16[256,768]{1,0:T(8,128)(2,1)S(1)}, bf16[256,768]{1,0:T(8...) custom-call(f32[2,128,128]{2,1,0:T(8,128)S(1)} %collective-permute-done.qss_ref,, ...), custom_call_target="tpu_custom_call" | custom-call | tf_op jit(solution)/shard_map/pallas_call | solution.py:45
  10.9 3.4 %collective-permute-start.4 = (f32[2,128,256]{2,1,0:T(8,128)S(1)}, f32[2,128,256]{2,1,0:T(8,128)S(1)}, u32[]{:S(2)}, u32[]{:S(2)}) collective-permute-start(f32[2,128,256]{2,1,0:T(8,128)S(1)} %get-tuple-element.61), channel_id=1, source_target_pairs={{0,16},{4,20},{8,24},{12,28},{16,0},{20,4},{24,8},{28,12},{1,17},{... | collective-permute-start | bytes 786440 | tf_op jit(solution)/shard_map/ppermute | solution.py:33
  14.3 1.5 %shard_map.39 = (bf16[288,256]{1,0:T(8,128)(2,1)S(1)}, bf16[288,256]{1,0:T(8,128)(2,1)S(1)}, f32[2,96,384]{2,1,0:T(8,128)S(1)}, f32[2,96,384]{2,1,0:T(8,128)S(1)}) custom-call(f32[2,384,384]{2,1,0:T(8,128)S(1)} %get-tuple-element.40.base_ref, f32[384,256]{1,0:T(8,128)S(1)} %get-tuple-element.41.res_ref, bf16[384,256]{1,0:T(8,128)(2,1)S(1)} %get-tuple-element.42.res_high, ...), custom_call_target="tpu_custom_call" | custom-call | tf_op jit(solution)/shard_map/pallas_call | solution.py:45
  15.9 1.6 %collective-permute-start.10 = (f32[2,96,384]{2,1,0:T(8,128)S(1)}, f32[2,96,384]{2,1,0:T(8,128)S(1)}, u32[]{:S(2)}, u32[]{:S(2)}) collective-permute-start(f32[2,96,384]{2,1,0:T(8,128)S(1)} %get-tuple-element.68), channel_id=1, source_target_pairs={{0,2},{1,3},{2,0},{3,1},{4,6},{5,7},{6,4},{7,5},{8,10},{9,11},{10,... | collective-permute-start | bytes 884744 | tf_op jit(solution)/shard_map/ppermute | solution.py:33
  17.4 1.5 %collective-permute-start.9 = (f32[2,96,384]{2,1,0:T(8,128)S(1)}, f32[2,96,384]{2,1,0:T(8,128)S(1)}, u32[]{:S(2)}, u32[]{:S(2)}) collective-permute-start(f32[2,96,384]{2,1,0:T(8,128)S(1)} %get-tuple-element.67), channel_id=1, source_target_pairs={{0,1},{1,0},{2,3},{3,2},{4,5},{5,4},{6,7},{7,6},{8,9},{9,8},{10,11... | collective-permute-start | bytes 884744 | tf_op jit(solution)/shard_map/ppermute | solution.py:33
  18.9 0.5 collective-permute-start.11
  19.4 3.2 %collective-permute-done.4.qse_ref = f32[2,128,256]{2,1,0:T(8,128)S(1)} collective-permute-done((f32[2,128,256]{2,1,0:T(8,128)S(1)}, f32[2,128,256]{2,1,0:T(8,128)S(1)}, u32[]{:S(2)}, u32[]{:S(2)}) %collective-permute-start.4) | collective-permute-done | bytes 262176 | tf_op jit(solution)/shard_map/ppermute | solution.py:33
  22.6 3.4 %collective-permute-start.5 = (f32[2,128,128]{2,1,0:T(8,128)S(1)}, f32[2,128,128]{2,1,0:T(8,128)S(1)}, u32[]{:S(2)}, u32[]{:S(2)}) collective-permute-start(f32[2,128,128]{2,1,0:T(8,128)S(1)} %get-tuple-element.62), channel_id=1, source_target_pairs={{0,16},{4,20},{8,24},{12,28},{16,0},{20,4},{24,8},{28,12},{1,17},{... | collective-permute-start | bytes 393224 | tf_op jit(solution)/shard_map/ppermute | solution.py:33
  26.6 1.3 %collective-permute-start.1 = (f32[8,128]{1,0:T(8,128)S(1)}, f32[8,128]{1,0:T(8,128)S(1)}, u32[]{:S(2)}, u32[]{:S(2)}) collective-permute-start(f32[8,128]{1,0:T(8,128)S(1)} %broadcast_in_dim.6.refs_0_), channel_id=1, source_target_pairs={{0,1},{1,0},{2,3},{3,2},{4,5},{5,4},{6,7},{7,6},{8,9},{9,8},{10,11... | collective-permute-start | bytes 12296 | tf_op jit(solution)/shard_map/ppermute | solution.py:33
  28.0 4.3 %collective-permute-done.1.refs_1_ = f32[8,128]{1,0:T(8,128)S(1)} collective-permute-done((f32[8,128]{1,0:T(8,128)S(1)}, f32[8,128]{1,0:T(8,128)S(1)}, u32[]{:S(2)}, u32[]{:S(2)}) %collective-permute-start.1) | collective-permute-done | bytes 4128 | tf_op jit(solution)/shard_map/ppermute | solution.py:33
  32.2 0.5 collective-permute-start.2
  32.7 3.1 %collective-permute-done.2.refs_2_ = f32[8,128]{1,0:T(8,128)S(1)} collective-permute-done((f32[8,128]{1,0:T(8,128)S(1)}, f32[8,128]{1,0:T(8,128)S(1)}, u32[]{:S(2)}, u32[]{:S(2)}) %collective-permute-start.2) | collective-permute-done | bytes 4128 | tf_op jit(solution)/shard_map/ppermute | solution.py:33
  35.8 1.4 %collective-permute-start.3 = (f32[8,128]{1,0:T(8,128)S(1)}, f32[8,128]{1,0:T(8,128)S(1)}, u32[]{:S(2)}, u32[]{:S(2)}) collective-permute-start(f32[8,128]{1,0:T(8,128)S(1)} %broadcast_in_dim.6.refs_0_), channel_id=1, source_target_pairs={{0,3},{1,2},{2,1},{3,0},{4,7},{5,6},{6,5},{7,4},{8,11},{9,10},{10,... | collective-permute-start | bytes 12296 | tf_op jit(solution)/shard_map/ppermute | solution.py:33
  37.3 0.5 shard_map.42
  37.8 2.6 %collective-permute-done.3.refs_3_ = f32[8,128]{1,0:T(8,128)S(1)} collective-permute-done((f32[8,128]{1,0:T(8,128)S(1)}, f32[8,128]{1,0:T(8,128)S(1)}, u32[]{:S(2)}, u32[]{:S(2)}) %collective-permute-start.3) | collective-permute-done | bytes 4128 | tf_op jit(solution)/shard_map/ppermute | solution.py:33
  40.4 1.5 %collective-permute-start.12 = (f32[2,96,256]{2,1,0:T(8,128)S(1)}, f32[2,96,256]{2,1,0:T(8,128)S(1)}, u32[]{:S(2)}, u32[]{:S(2)}) collective-permute-start(f32[2,96,256]{2,1,0:T(8,128)S(1)} %get-tuple-element.72), channel_id=1, source_target_pairs={{0,1},{1,0},{2,3},{3,2},{4,5},{5,4},{6,7},{7,6},{8,9},{9,8},{10,11... | collective-permute-start | bytes 589832 | tf_op jit(solution)/shard_map/ppermute | solution.py:33
  41.9 0.0 collective-permute-done.10.refs_6_
  41.9 0.5 collective-permute-start.13
  42.4 0.0 collective-permute-done.5.qse_ref
  42.4 1.5 %collective-permute-start.14 = (f32[2,96,256]{2,1,0:T(8,128)S(1)}, f32[2,96,256]{2,1,0:T(8,128)S(1)}, u32[]{:S(2)}, u32[]{:S(2)}) collective-permute-start(f32[2,96,256]{2,1,0:T(8,128)S(1)} %get-tuple-element.74), channel_id=1, source_target_pairs={{0,3},{1,2},{2,1},{3,0},{4,7},{5,6},{6,5},{7,4},{8,11},{9,10},{10,... | collective-permute-start | bytes 589832 | tf_op jit(solution)/shard_map/ppermute | solution.py:33
  43.9 0.3 shard_map.40
  44.2 0.0 collective-permute-done.9.refs_5_
  44.2 1.6 %collective-permute-start.6 = (f32[2,96,128]{2,1,0:T(8,128)S(1)}, f32[2,96,128]{2,1,0:T(8,128)S(1)}, u32[]{:S(2)}, u32[]{:S(2)}) collective-permute-start(f32[2,96,128]{2,1,0:T(8,128)S(1)} %get-tuple-element.64), channel_id=1, source_target_pairs={{0,1},{1,0},{2,3},{3,2},{4,5},{5,4},{6,7},{7,6},{8,9},{9,8},{10,11... | collective-permute-start | bytes 294920 | tf_op jit(solution)/shard_map/ppermute | solution.py:33
  45.8 0.0 collective-permute-done.11.refs_7_
  45.8 0.5 collective-permute-start.7
  46.3 1.7 %collective-permute-done.12.refs_9_ = f32[2,96,256]{2,1,0:T(8,128)S(1)} collective-permute-done((f32[2,96,256]{2,1,0:T(8,128)S(1)}, f32[2,96,256]{2,1,0:T(8,128)S(1)}, u32[]{:S(2)}, u32[]{:S(2)}) %collective-permute-start.12) | collective-permute-done | bytes 196640 | tf_op jit(solution)/shard_map/ppermute | solution.py:33
  48.0 1.2 %collective-permute-start.8 = (f32[2,96,128]{2,1,0:T(8,128)S(1)}, f32[2,96,128]{2,1,0:T(8,128)S(1)}, u32[]{:S(2)}, u32[]{:S(2)}) collective-permute-start(f32[2,96,128]{2,1,0:T(8,128)S(1)} %get-tuple-element.66), channel_id=1, source_target_pairs={{0,3},{1,2},{2,1},{3,0},{4,7},{5,6},{6,5},{7,4},{8,11},{9,10},{10,... | collective-permute-start | bytes 294920 | tf_op jit(solution)/shard_map/ppermute | solution.py:33
  49.2 0.3 shard_map.41.refs_4_
  49.5 1.5 %collective-permute-done.13.refs_10_ = f32[2,96,256]{2,1,0:T(8,128)S(1)} collective-permute-done((f32[2,96,256]{2,1,0:T(8,128)S(1)}, f32[2,96,256]{2,1,0:T(8,128)S(1)}, u32[]{:S(2)}, u32[]{:S(2)}) %collective-permute-start.13) | collective-permute-done | bytes 196640 | tf_op jit(solution)/shard_map/ppermute | solution.py:33
  51.0 0.0 collective-permute-done.14.refs_11_
  51.0 1.5 %shard_map.43.refs_8_ = f32[2,4,96,768]{3,2,1,0:T(8,128)} custom-call(f32[8,128]{1,0:T(8,128)S(1)} %broadcast_in_dim.6.refs_0_, f32[8,128]{1,0:T(8,128)S(1)} %collective-permute-done.1.refs_1_, f32[8,128]{1,0:T(8,128)S(1)} %collective-permute-done.2.refs_2_, f32[8,128]{1,0:T(8,128)S(1)} %collective-permute-done.3.refs_3_, ...), custom_call_target="tpu_custom_call" | custom-call | tf_op jit(solution)/shard_map/pallas_call | solution.py:45
  52.5 0.0 collective-permute-done.6.refs_5_
  52.5 0.0 collective-permute-done.7.refs_6_
  52.5 0.9 %collective-permute-done.8.refs_7_ = f32[2,96,128]{2,1,0:T(8,128)S(1)} collective-permute-done((f32[2,96,128]{2,1,0:T(8,128)S(1)}, f32[2,96,128]{2,1,0:T(8,128)S(1)}, u32[]{:S(2)}, u32[]{:S(2)}) %collective-permute-start.8) | collective-permute-done | bytes 98336 | tf_op jit(solution)/shard_map/ppermute | solution.py:33
  53.5 0.9 %shard_map.44 = f32[2,4,96,768]{3,2,1,0:T(8,128)} custom-call(f32[8,128]{1,0:T(8,128)S(1)} %broadcast_in_dim.6.refs_0_, f32[8,128]{1,0:T(8,128)S(1)} %collective-permute-done.1.refs_1_, f32[8,128]{1,0:T(8,128)S(1)} %collective-permute-done.2.refs_2_, f32[8,128]{1,0:T(8,128)S(1)} %collective-permute-done.3.refs_3_, ...), custom_call_target="tpu_custom_call", output_to_operand_aliasing={{}: (8, {})} | custom-call | tf_op jit(solution)/shard_map/pallas_call | solution.py:45
  (1 shorter events, 0.0 us)
Async XLA Ops:
  0.9 8.1 %collective-permute-start = (f32[2,128,128]{2,1,0:T(8,128)S(1)}, f32[2,128,128]{2,1,0:T(8,128)S(1)}, u32[]{:S(2)}, u32[]{:S(2)}) collective-permute-start(f32[2,128,128]{2,1,0:T(8,128)S(1)} %slice.4), channel_id=1, source_target_pairs={{0,16},{4,20},{8,24},{12,28},{16,0},{20,4},{24,8},{28,12},{1,17},{... | collective-permute-start | bytes 393224 | tf_op jit(solution)/shard_map/ppermute | solution.py:33
  3.6 1.6 %copy-start = (f32[1,1,2,512,512]{4,3,2,1,0:T(8,128)S(1)}, f32[1,1,2,512,512]{4,3,2,1,0:T(8,128)}, u32[]{:S(2)}) copy-start(f32[1,1,2,512,512]{4,3,2,1,0:T(8,128)} %param.3) | copy-start | bytes 6291460
  5.2 0.7 %copy-start.1 = (s32[1,1,4]{2,1,0:T(1,128)S(1)}, s32[1,1,4]{2,1,0:T(1,128)}, u32[]{:S(2)}) copy-start(s32[1,1,4]{2,1,0:T(1,128)} %param.5) | copy-start | bytes 52
  10.9 11.7 %collective-permute-start.4 = (f32[2,128,256]{2,1,0:T(8,128)S(1)}, f32[2,128,256]{2,1,0:T(8,128)S(1)}, u32[]{:S(2)}, u32[]{:S(2)}) collective-permute-start(f32[2,128,256]{2,1,0:T(8,128)S(1)} %get-tuple-element.61), channel_id=1, source_target_pairs={{0,16},{4,20},{8,24},{12,28},{16,0},{20,4},{24,8},{28,12},{1,17},{... | collective-permute-start | bytes 786440 | tf_op jit(solution)/shard_map/ppermute | solution.py:33
  15.9 26.0 %collective-permute-start.10 = (f32[2,96,384]{2,1,0:T(8,128)S(1)}, f32[2,96,384]{2,1,0:T(8,128)S(1)}, u32[]{:S(2)}, u32[]{:S(2)}) collective-permute-start(f32[2,96,384]{2,1,0:T(8,128)S(1)} %get-tuple-element.68), channel_id=1, source_target_pairs={{0,2},{1,3},{2,0},{3,1},{4,6},{5,7},{6,4},{7,5},{8,10},{9,11},{10,... | collective-permute-start | bytes 884744 | tf_op jit(solution)/shard_map/ppermute | solution.py:33
  17.4 26.8 %collective-permute-start.9 = (f32[2,96,384]{2,1,0:T(8,128)S(1)}, f32[2,96,384]{2,1,0:T(8,128)S(1)}, u32[]{:S(2)}, u32[]{:S(2)}) collective-permute-start(f32[2,96,384]{2,1,0:T(8,128)S(1)} %get-tuple-element.67), channel_id=1, source_target_pairs={{0,1},{1,0},{2,3},{3,2},{4,5},{5,4},{6,7},{7,6},{8,9},{9,8},{10,11... | collective-permute-start | bytes 884744 | tf_op jit(solution)/shard_map/ppermute | solution.py:33
  18.9 26.8 %collective-permute-start.11 = (f32[2,96,384]{2,1,0:T(8,128)S(1)}, f32[2,96,384]{2,1,0:T(8,128)S(1)}, u32[]{:S(2)}, u32[]{:S(2)}) collective-permute-start(f32[2,96,384]{2,1,0:T(8,128)S(1)} %get-tuple-element.69), channel_id=1, source_target_pairs={{0,3},{1,2},{2,1},{3,0},{4,7},{5,6},{6,5},{7,4},{8,11},{9,10},{10,... | collective-permute-start | bytes 884744 | tf_op jit(solution)/shard_map/ppermute | solution.py:33
  22.6 19.8 %collective-permute-start.5 = (f32[2,128,128]{2,1,0:T(8,128)S(1)}, f32[2,128,128]{2,1,0:T(8,128)S(1)}, u32[]{:S(2)}, u32[]{:S(2)}) collective-permute-start(f32[2,128,128]{2,1,0:T(8,128)S(1)} %get-tuple-element.62), channel_id=1, source_target_pairs={{0,16},{4,20},{8,24},{12,28},{16,0},{20,4},{24,8},{28,12},{1,17},{... | collective-permute-start | bytes 393224 | tf_op jit(solution)/shard_map/ppermute | solution.py:33
  26.6 5.6 %collective-permute-start.1 = (f32[8,128]{1,0:T(8,128)S(1)}, f32[8,128]{1,0:T(8,128)S(1)}, u32[]{:S(2)}, u32[]{:S(2)}) collective-permute-start(f32[8,128]{1,0:T(8,128)S(1)} %broadcast_in_dim.6.refs_0_), channel_id=1, source_target_pairs={{0,1},{1,0},{2,3},{3,2},{4,5},{5,4},{6,7},{7,6},{8,9},{9,8},{10,11... | collective-permute-start | bytes 12296 | tf_op jit(solution)/shard_map/ppermute | solution.py:33
  32.2 3.6 %collective-permute-start.2 = (f32[8,128]{1,0:T(8,128)S(1)}, f32[8,128]{1,0:T(8,128)S(1)}, u32[]{:S(2)}, u32[]{:S(2)}) collective-permute-start(f32[8,128]{1,0:T(8,128)S(1)} %broadcast_in_dim.6.refs_0_), channel_id=1, source_target_pairs={{0,2},{1,3},{2,0},{3,1},{4,6},{5,7},{6,4},{7,5},{8,10},{9,11},{10,... | collective-permute-start | bytes 12296 | tf_op jit(solution)/shard_map/ppermute | solution.py:33
  35.8 4.5 %collective-permute-start.3 = (f32[8,128]{1,0:T(8,128)S(1)}, f32[8,128]{1,0:T(8,128)S(1)}, u32[]{:S(2)}, u32[]{:S(2)}) collective-permute-start(f32[8,128]{1,0:T(8,128)S(1)} %broadcast_in_dim.6.refs_0_), channel_id=1, source_target_pairs={{0,3},{1,2},{2,1},{3,0},{4,7},{5,6},{6,5},{7,4},{8,11},{9,10},{10,... | collective-permute-start | bytes 12296 | tf_op jit(solution)/shard_map/ppermute | solution.py:33
  40.4 7.6 %collective-permute-start.12 = (f32[2,96,256]{2,1,0:T(8,128)S(1)}, f32[2,96,256]{2,1,0:T(8,128)S(1)}, u32[]{:S(2)}, u32[]{:S(2)}) collective-permute-start(f32[2,96,256]{2,1,0:T(8,128)S(1)} %get-tuple-element.72), channel_id=1, source_target_pairs={{0,1},{1,0},{2,3},{3,2},{4,5},{5,4},{6,7},{7,6},{8,9},{9,8},{10,11... | collective-permute-start | bytes 589832 | tf_op jit(solution)/shard_map/ppermute | solution.py:33
  41.9 9.1 %collective-permute-start.13 = (f32[2,96,256]{2,1,0:T(8,128)S(1)}, f32[2,96,256]{2,1,0:T(8,128)S(1)}, u32[]{:S(2)}, u32[]{:S(2)}) collective-permute-start(f32[2,96,256]{2,1,0:T(8,128)S(1)} %get-tuple-element.73), channel_id=1, source_target_pairs={{0,2},{1,3},{2,0},{3,1},{4,6},{5,7},{6,4},{7,5},{8,10},{9,11},{10,... | collective-permute-start | bytes 589832 | tf_op jit(solution)/shard_map/ppermute | solution.py:33
  42.4 8.6 %collective-permute-start.14 = (f32[2,96,256]{2,1,0:T(8,128)S(1)}, f32[2,96,256]{2,1,0:T(8,128)S(1)}, u32[]{:S(2)}, u32[]{:S(2)}) collective-permute-start(f32[2,96,256]{2,1,0:T(8,128)S(1)} %get-tuple-element.74), channel_id=1, source_target_pairs={{0,3},{1,2},{2,1},{3,0},{4,7},{5,6},{6,5},{7,4},{8,11},{9,10},{10,... | collective-permute-start | bytes 589832 | tf_op jit(solution)/shard_map/ppermute | solution.py:33
  44.2 8.3 %collective-permute-start.6 = (f32[2,96,128]{2,1,0:T(8,128)S(1)}, f32[2,96,128]{2,1,0:T(8,128)S(1)}, u32[]{:S(2)}, u32[]{:S(2)}) collective-permute-start(f32[2,96,128]{2,1,0:T(8,128)S(1)} %get-tuple-element.64), channel_id=1, source_target_pairs={{0,1},{1,0},{2,3},{3,2},{4,5},{5,4},{6,7},{7,6},{8,9},{9,8},{10,11... | collective-permute-start | bytes 294920 | tf_op jit(solution)/shard_map/ppermute | solution.py:33
  45.8 6.7 %collective-permute-start.7 = (f32[2,96,128]{2,1,0:T(8,128)S(1)}, f32[2,96,128]{2,1,0:T(8,128)S(1)}, u32[]{:S(2)}, u32[]{:S(2)}) collective-permute-start(f32[2,96,128]{2,1,0:T(8,128)S(1)} %get-tuple-element.65), channel_id=1, source_target_pairs={{0,2},{1,3},{2,0},{3,1},{4,6},{5,7},{6,4},{7,5},{8,10},{9,11},{10,... | collective-permute-start | bytes 294920 | tf_op jit(solution)/shard_map/ppermute | solution.py:33
  48.0 5.5 %collective-permute-start.8 = (f32[2,96,128]{2,1,0:T(8,128)S(1)}, f32[2,96,128]{2,1,0:T(8,128)S(1)}, u32[]{:S(2)}, u32[]{:S(2)}) collective-permute-start(f32[2,96,128]{2,1,0:T(8,128)S(1)} %get-tuple-element.66), channel_id=1, source_target_pairs={{0,3},{1,2},{2,1},{3,0},{4,7},{5,6},{6,5},{7,4},{8,11},{9,10},{10,... | collective-permute-start | bytes 294920 | tf_op jit(solution)/shard_map/ppermute | solution.py:33

commit v3 on v2

--- a/solution.py
+++ b/solution.py
@@ -54,17 +54,22 @@
 
 def matmul(left, right):
     dot = functools.partial(jnp.dot, preferred_element_type=jnp.float32)
-    return dot(left[0], right[0]) + (dot(left[1], right[0]) + dot(left[0], right[1]))
-
-
-def embed(real, imag):
-    top = jnp.concatenate([real, imag], axis=1)
-    return halves(jnp.concatenate([top, jnp.concatenate([-imag, real], axis=1)], axis=0))
-
-
-def split_embed(x):
-    half = x.shape[1] // 2
-    return embed(x[:, :half], x[:, half:])
+    rows = left[0].shape[0]
+    both = dot(jnp.concatenate(left, axis=0), right[0])
+    return both[:rows] + (both[rows:] + dot(left[0], right[1]))
+
+
+def expand(rows):
+    half = rows.shape[1] // 2
+    return jnp.concatenate([rows, jnp.concatenate([-rows[:, half:], rows[:, :half]], axis=1)], axis=0)
+
+
+def times(left, right):
+    return matmul(left, [expand(x) for x in right])
+
+
+def joined(ref, rows, cols):
+    return jnp.concatenate([ref[0, rows, cols], ref[1, rows, cols]], axis=1)
 
 
 def panel_of(owner_ref, dest, groups):
@@ -98,8 +103,8 @@
     for (lo, hi), part in zip(cuts, parts):
         others.append(fetch(iti_ref.at[:, ext:, lo:hi], part))
     shared.wait()
-    rss_high[...], rss_low[...] = embed(shared_ref[0, :, ext:], shared_ref[1, :, ext:])
-    rse_high[...], rse_low[...] = embed(shared_ref[0, :, :ext], shared_ref[1, :, :ext])
+    rss_high[...], rss_low[...] = halves(joined(shared_ref, slice(None), slice(ext, None)))
+    rse_high[...], rse_low[...] = halves(joined(shared_ref, slice(None), slice(0, ext)))
     for copy in blocks:
         copy.wait()
     res_high[...], res_low[...] = halves(res_ref[...])
@@ -109,24 +114,23 @@
 
 def factor_kernel(edge, ext, rows, qss_ref, base_ref, res_ref, res_high, res_low, rss_high, rss_low, rse_high, rse_low, *refs):
     pow_high, pow_low, cols_high, cols_low, far_high, far_low, out_ref = refs
-    qss = halves(jnp.concatenate([qss_ref[0], qss_ref[1]], axis=1))
-    power = matmul(qss, (rss_high[...], rss_low[...]))
+    qss = halves(joined(qss_ref, slice(None), slice(None)))
+    power = halves(times(qss, (rss_high[...], rss_low[...])))
+    cols_high[...], cols_low[...] = halves(times(qss, (rse_high[...], rse_low[...])))
     total = res_ref[ext - rows :]
     left = res_high[ext - rows :], res_low[ext - rows :]
     for level in range(LEVELS):
-        right = split_embed(power)
-        pow_high[level], pow_low[level] = right
+        pow_high[level], pow_low[level] = power
         if level + 1 < LEVELS:
-            both = matmul([jnp.concatenate(pair, axis=0) for pair in zip(halves(power), left)], right)
-            power = both[:edge]
+            both = times([jnp.concatenate(pair, axis=0) for pair in zip(power, left)], power)
+            power = halves(both[:edge])
             total = total + both[edge:]
         else:
-            total = total + matmul(left, right)
+            total = total + times(left, power)
         left = halves(total)
     far_high[...], far_low[...] = left
-    cols = split_embed(matmul(qss, (rse_high[...], rse_low[...])))
-    cols_high[...], cols_low[...] = cols
-    finish(edge, ext, [out_ref], matmul(left, cols), base_ref, ext - rows)
+    cols = cols_high[...], cols_low[...]
+    finish(edge, ext, [out_ref], times(left, cols), base_ref, ext - rows)
 
 
 def finish(edge, ext, out_refs, half, base_ref, start):
@@ -143,24 +147,26 @@
     total = res_ref[: ext - rows]
     left = res_high[: ext - rows], res_low[: ext - rows]
     for level in range(LEVELS):
-        total = total + matmul(left, (pow_high[level], pow_low[level]))
+        total = total + times(left, (pow_high[level], pow_low[level]))
         left = halves(total)
     high_ref[...], low_ref[...] = left
     if out_refs:
-        finish(edge, ext, out_refs, matmul([x[rows:] for x in left], (cols_high[...], cols_low[...])), base_ref, rows)
+        finish(edge, ext, out_refs, times([x[rows:] for x in left], (cols_high[...], cols_low[...])), base_ref, rows)
 
 
 def mine_kernel(edge, ext, rows, base_ref, high_ref, low_ref, cols_high, cols_low, out_ref):
-    half = matmul((high_ref[:rows], low_ref[:rows]), (cols_high[...], cols_low[...]))
+    half = times((high_ref[:rows], low_ref[:rows]), (cols_high[...], cols_low[...]))
     finish(edge, ext, [out_ref], half, base_ref, 0)
 
 
-def other_half_kernel(edge, groups, high_ref, low_ref, far_high, far_low, qse_ref, *out_refs):
+def other_half_kernel(edge, groups, high_ref, low_ref, far_high, far_low, *refs):
+    qse_refs, out_refs = refs[:-groups], refs[-groups:]
     weight = math.sqrt(edge)
     rows = far_high.shape[0]
-    cols = qse_ref.shape[-1]
+    cols = qse_refs[0].shape[-1]
+    qse = sum((joined(x, slice(None), slice(None)) for x in qse_refs[1:]), joined(qse_refs[0], slice(None), slice(None)))
     left = [jnp.concatenate([a[...], b[...]], axis=0) for a, b in ((high_ref, far_high), (low_ref, far_low))]
-    half = matmul(left, embed(qse_ref[0], qse_ref[1]))
+    half = times(left, halves(qse))
     for k in range(groups):
         for c in range(2):
             out_refs[k][c] = half[k * rows : (k + 1) * rows, c * cols : (c + 1) * cols] * weight
@@ -214,30 +220,32 @@
         functools.partial(prepare_kernel, edge, ext, groups, cuts),
         out_shape=[f32(2, edge, hi - lo) for lo, hi in cuts]
         + [f32(2, ext, ext), f32(ext, 2 * edge), bf16(ext, 2 * edge), bf16(ext, 2 * edge)]
-        + [bf16(2 * edge, 2 * edge)] * 2
-        + [bf16(2 * edge, 2 * ext)] * 2,
+        + [bf16(edge, 2 * edge)] * 2
+        + [bf16(edge, 2 * ext)] * 2,
         in_specs=[SMEM, HBM],
         out_specs=[VMEM] * (8 + len(cuts)),
         scratch_shapes=[pltpu.VMEM((2, edge, 4 * edge), jnp.float32), pltpu.SemaphoreType.DMA((1 + 4 * groups + len(cuts),))],
         compiler_params=limit(12),
     )(owner[0, 0], ownmap)
+    inner = [i for i in range(2 * across) if (i // across ^ i // (across // 2)) & 1]
+    first = [(i, i ^ across) for i in inner]
+    last = [(i ^ across // 2, i ^ across ^ across // 2) for i in inner]
+    early = lax.ppermute(pieces[0], "gx", first)
     pow_high, pow_low, cols_high, cols_low, far_high, far_low, farthest = call(
         functools.partial(factor_kernel, edge, ext, rows_each),
-        out_shape=[bf16(LEVELS, 2 * edge, 2 * edge)] * 2
-        + [bf16(2 * edge, 2 * ext)] * 2
+        out_shape=[bf16(LEVELS, edge, 2 * edge)] * 2
+        + [bf16(edge, 2 * ext)] * 2
         + [bf16(rows_each, 2 * edge)] * 2
         + [f32(2, rows_each, ext)],
         in_specs=[VMEM] * 9,
         out_specs=[VMEM] * 7,
         compiler_params=limit(16),
     )(qss, base, res, res_high, res_low, rss_high, rss_low, rse_high, rse_low)
-    qse = []
-    for piece in pieces:
-        if qse:
-            piece, qse[-1] = lax.optimization_barrier((piece, qse[-1]))
-        else:
-            piece, far_high = lax.optimization_barrier((piece, far_high))
-        qse.append(permute(piece, "gx", across))
+    piece, far_high = lax.optimization_barrier((pieces[0], far_high))
+    qse = [[early, lax.ppermute(piece, "gx", last)]]
+    for piece in pieces[1:]:
+        piece, qse[-1] = lax.optimization_barrier((piece, qse[-1]))
+        qse.append([permute(piece, "gx", across)])
     high, low, *own = call(
         functools.partial(own_half_kernel, edge, ext, rows_each),
         out_shape=[bf16(ext - rows_each, 2 * edge)] * 2 + [f32(2, rows_each, ext)] * (groups - 2),
@@ -262,10 +270,10 @@
         blocks = call(
             functools.partial(other_half_kernel, edge, groups),
             out_shape=[f32(2, rows_each, hi - lo)] * groups,
-            in_specs=[VMEM] * 5,
+            in_specs=[VMEM] * (4 + len(part)),
             out_specs=[VMEM] * groups,
             compiler_params=limit(12),
-        )(high, low, far_high, far_low, part)
+        )(high, low, far_high, far_low, *part)
         parts.append((lo, exchange(blocks)))
     out = store(sides, [(None, own), *parts[:-1]], ext)
     out = store(sides, parts[-1:], ext, out)

time: 54.6 us -> 54.9 us (level)
  the two profiles are of different devices: /device:TPU:8 before, /device:TPU:0 now
where the time goes in v3:
time: 54.9 us; the launch traced here: 54.7 us
  starting transfers between devices  24.6 us (45%)
  waiting for transfers between devices  18.1 us (33%)
  Pallas kernels  7.94 us (14%)
  local copies, waits for them, and re-layouts  3.17 us (6%)
  between operations  0.77 us (1%)
    ppermute x14, starting transfers between devices, permute(): lax.ppermute(x, axis, [(i, i ^ offset) for i in range(lax.axis_size(axis))])  19.4 us
    ppermute x14, waiting for transfers between devices, permute(): lax.ppermute(x, axis, [(i, i ^ offset) for i in range(lax.axis_size(axis))])  15.4 us
    pallas_call x8, Pallas kernels, run(): return pl.pallas_call(kernel, **options)(*args)  7.94 us
    ppermute x1, starting transfers between devices, on_device(): qse = [[early, lax.ppermute(piece, 'gx', last)]]  3.98 us
    ppermute x1, waiting for transfers between devices, on_device(): early = lax.ppermute(pieces[0], 'gx', first)  2.78 us
    unnamed x4, local copies, waits for them, and re-layouts  2.25 us
    ppermute x1, starting transfers between devices, on_device(): early = lax.ppermute(pieces[0], 'gx', first)  1.29 us
  transfers between devices with their start and end apart: 16, of which 8 were waited for; matrix products, arithmetic and copies ran while one was open for 0% of the time, Pallas kernels for 13%

profile of v3, /device:TPU:0, one launch (start us, length us, event | category | flops | bytes accessed | tf_op | source)
XLA Modules:
  0.0 54.7 jit_solution(17002962088201651570)
XLA Ops:
  0.0 0.9 %slice.4 = f32[2,128,128]{2,1,0:T(8,128)S(1)} slice(f32[2,512,512]{2,1,0:T(8,128)} %bitcast.4), slice={[0:2], [384:512], [384:512]} | slice | bytes 262144 | tf_op jit(solution)/shard_map/slice | solution.py:218
  0.9 4.1 %collective-permute-start = (f32[2,128,128]{2,1,0:T(8,128)S(1)}, f32[2,128,128]{2,1,0:T(8,128)S(1)}, u32[]{:S(2)}, u32[]{:S(2)}) collective-permute-start(f32[2,128,128]{2,1,0:T(8,128)S(1)} %slice.4), channel_id=1, source_target_pairs={{0,16},{4,20},{8,24},{12,28},{16,0},{20,4},{24,8},{28,12},{1,17},{... | collective-permute-start | bytes 393224 | tf_op jit(solution)/shard_map/ppermute | solution.py:33
  5.1 0.0 copy-start
  5.1 1.6 %copy-done = f32[1,1,2,512,512]{4,3,2,1,0:T(8,128)S(1)} copy-done((f32[1,1,2,512,512]{4,3,2,1,0:T(8,128)S(1)}, f32[1,1,2,512,512]{4,3,2,1,0:T(8,128)}, u32[]{:S(2)}) %copy-start) | copy-done | bytes 2097176
  6.6 0.0 copy-start.1
  6.6 0.7 %copy-done.1 = s32[1,1,4]{2,1,0:T(1,128)S(1)} copy-done((s32[1,1,4]{2,1,0:T(1,128)S(1)}, s32[1,1,4]{2,1,0:T(1,128)}, u32[]{:S(2)}) %copy-start.1) | copy-done | bytes 40
  7.3 1.2 %shard_map.37 = (f32[2,128,256]{2,1,0:T(8,128)S(1)}, f32[2,128,128]{2,1,0:T(8,128)S(1)}, f32[2,384,384]{2,1,0:T(8,128)S(1)}, f32[384,256]{1,0:T(8,128)S(1)}, bf1...) custom-call(s32[4]{0:T(128)S(1)} %bitcast.6, ...), custom_call_target="tpu_custom_call" | custom-call | tf_op jit(solution)/shard_map/pallas_call | solution.py:45
  8.5 1.3 %collective-permute-start.4 = (f32[2,128,256]{2,1,0:T(8,128)S(1)}, f32[2,128,256]{2,1,0:T(8,128)S(1)}, u32[]{:S(2)}, u32[]{:S(2)}) collective-permute-start(f32[2,128,256]{2,1,0:T(8,128)S(1)} %get-tuple-element.62), channel_id=1, source_target_pairs={{8,24},{12,28},{16,0},{20,4},{9,25},{13,29},{17,1},{21,5},{10,26},... | collective-permute-start | bytes 786440 | tf_op jit(solution)/shard_map/ppermute | solution.py:233
  9.8 1.5 %collective-permute-done.qss_ref = f32[2,128,128]{2,1,0:T(8,128)S(1)} collective-permute-done((f32[2,128,128]{2,1,0:T(8,128)S(1)}, f32[2,128,128]{2,1,0:T(8,128)S(1)}, u32[]{:S(2)}, u32[]{:S(2)}) %collective-permute-start) | collective-permute-done | bytes 131104 | tf_op jit(solution)/shard_map/ppermute | solution.py:33
  11.4 1.6 %shard_map.38 = (bf16[4,128,256]{2,1,0:T(8,128)(2,1)S(1)}, bf16[4,128,256]{2,1,0:T(8,128)(2,1)S(1)}, bf16[128,768]{1,0:T(8,128)(2,1)S(1)}, bf16[128,768]{1,0:T(8...) custom-call(f32[2,128,128]{2,1,0:T(8,128)S(1)} %collective-permute-done.qss_ref,, ...), custom_call_target="tpu_custom_call" | custom-call | tf_op jit(solution)/shard_map/pallas_call | solution.py:45
  13.0 4.0 %collective-permute-start.5 = (f32[2,128,256]{2,1,0:T(8,128)S(1)}, f32[2,128,256]{2,1,0:T(8,128)S(1)}, u32[]{:S(2)}, u32[]{:S(2)}) collective-permute-start(f32[2,128,256]{2,1,0:T(8,128)S(1)} %get-tuple-element.62), channel_id=1, source_target_pairs={{0,16},{4,20},{24,8},{28,12},{1,17},{5,21},{25,9},{29,13},{2,18},{... | collective-permute-start | bytes 786440 | tf_op jit(solution)/shard_map/ppermute | solution.py:245
  17.0 1.5 %shard_map.39 = (bf16[288,256]{1,0:T(8,128)(2,1)S(1)}, bf16[288,256]{1,0:T(8,128)(2,1)S(1)}, f32[2,96,384]{2,1,0:T(8,128)S(1)}, f32[2,96,384]{2,1,0:T(8,128)S(1)}) custom-call(f32[2,384,384]{2,1,0:T(8,128)S(1)} %get-tuple-element.41.base_ref, f32[384,256]{1,0:T(8,128)S(1)} %get-tuple-element.42.res_ref, bf16[384,256]{1,0:T(8,128)(2,1)S(1)} %get-tuple-element.43.res_high, ...), custom_call_target="tpu_custom_call" | custom-call | tf_op jit(solution)/shard_map/pallas_call | solution.py:45
  18.5 1.6 %collective-permute-start.10 = (f32[2,96,384]{2,1,0:T(8,128)S(1)}, f32[2,96,384]{2,1,0:T(8,128)S(1)}, u32[]{:S(2)}, u32[]{:S(2)}) collective-permute-start(f32[2,96,384]{2,1,0:T(8,128)S(1)} %get-tuple-element.68), channel_id=1, source_target_pairs={{0,1},{1,0},{2,3},{3,2},{4,5},{5,4},{6,7},{7,6},{8,9},{9,8},{10,11... | collective-permute-start | bytes 884744 | tf_op jit(solution)/shard_map/ppermute | solution.py:33
  20.1 1.5 %collective-permute-start.11 = (f32[2,96,384]{2,1,0:T(8,128)S(1)}, f32[2,96,384]{2,1,0:T(8,128)S(1)}, u32[]{:S(2)}, u32[]{:S(2)}) collective-permute-start(f32[2,96,384]{2,1,0:T(8,128)S(1)} %get-tuple-element.69), channel_id=1, source_target_pairs={{0,2},{1,3},{2,0},{3,1},{4,6},{5,7},{6,4},{7,5},{8,10},{9,11},{10,... | collective-permute-start | bytes 884744 | tf_op jit(solution)/shard_map/ppermute | solution.py:33
  21.6 0.5 collective-permute-start.12
  22.1 2.8 %collective-permute-done.4.refs_0_ = f32[2,128,256]{2,1,0:T(8,128)S(1)} collective-permute-done((f32[2,128,256]{2,1,0:T(8,128)S(1)}, f32[2,128,256]{2,1,0:T(8,128)S(1)}, u32[]{:S(2)}, u32[]{:S(2)}) %collective-permute-start.4) | collective-permute-done | bytes 262176 | tf_op jit(solution)/shard_map/ppermute | solution.py:233
  24.9 0.0 collective-permute-done.5.refs_1_
  24.9 0.5 collective-permute-start.6
  26.0 2.5 %collective-permute-start.3 = (f32[8,128]{1,0:T(8,128)S(1)}, f32[8,128]{1,0:T(8,128)S(1)}, u32[]{:S(2)}, u32[]{:S(2)}) collective-permute-start(f32[8,128]{1,0:T(8,128)S(1)} %broadcast_in_dim.6.refs_0_), channel_id=1, source_target_pairs={{0,3},{1,2},{2,1},{3,0},{4,7},{5,6},{6,5},{7,4},{8,11},{9,10},{10,... | collective-permute-start | bytes 12296 | tf_op jit(solution)/shard_map/ppermute | solution.py:33
  28.5 5.5 %collective-permute-done.3.refs_3_ = f32[8,128]{1,0:T(8,128)S(1)} collective-permute-done((f32[8,128]{1,0:T(8,128)S(1)}, f32[8,128]{1,0:T(8,128)S(1)}, u32[]{:S(2)}, u32[]{:S(2)}) %collective-permute-start.3) | collective-permute-done | bytes 4128 | tf_op jit(solution)/shard_map/ppermute | solution.py:33
  34.0 0.5 collective-permute-start.2
  34.5 3.1 %collective-permute-done.2.refs_2_ = f32[8,128]{1,0:T(8,128)S(1)} collective-permute-done((f32[8,128]{1,0:T(8,128)S(1)}, f32[8,128]{1,0:T(8,128)S(1)}, u32[]{:S(2)}, u32[]{:S(2)}) %collective-permute-start.2) | collective-permute-done | bytes 4128 | tf_op jit(solution)/shard_map/ppermute | solution.py:33
  37.6 1.4 %collective-permute-start.1 = (f32[8,128]{1,0:T(8,128)S(1)}, f32[8,128]{1,0:T(8,128)S(1)}, u32[]{:S(2)}, u32[]{:S(2)}) collective-permute-start(f32[8,128]{1,0:T(8,128)S(1)} %broadcast_in_dim.6.refs_0_), channel_id=1, source_target_pairs={{0,1},{1,0},{2,3},{3,2},{4,5},{5,4},{6,7},{7,6},{8,9},{9,8},{10,11... | collective-permute-start | bytes 12296 | tf_op jit(solution)/shard_map/ppermute | solution.py:33
  39.0 0.5 shard_map.42
  39.4 1.8 %collective-permute-done.1.refs_1_ = f32[8,128]{1,0:T(8,128)S(1)} collective-permute-done((f32[8,128]{1,0:T(8,128)S(1)}, f32[8,128]{1,0:T(8,128)S(1)}, u32[]{:S(2)}, u32[]{:S(2)}) %collective-permute-start.1) | collective-permute-done | bytes 4128 | tf_op jit(solution)/shard_map/ppermute | solution.py:33
  41.2 1.4 %collective-permute-start.13 = (f32[2,96,256]{2,1,0:T(8,128)S(1)}, f32[2,96,256]{2,1,0:T(8,128)S(1)}, u32[]{:S(2)}, u32[]{:S(2)}) collective-permute-start(f32[2,96,256]{2,1,0:T(8,128)S(1)} %get-tuple-element.74), channel_id=1, source_target_pairs={{0,1},{1,0},{2,3},{3,2},{4,5},{5,4},{6,7},{7,6},{8,9},{9,8},{10,11... | collective-permute-start | bytes 589832 | tf_op jit(solution)/shard_map/ppermute | solution.py:33
  42.6 0.0 collective-permute-done.10.refs_5_
  42.6 0.6 %collective-permute-start.14 = (f32[2,96,256]{2,1,0:T(8,128)S(1)}, f32[2,96,256]{2,1,0:T(8,128)S(1)}, u32[]{:S(2)}, u32[]{:S(2)}) collective-permute-start(f32[2,96,256]{2,1,0:T(8,128)S(1)} %get-tuple-element.75), channel_id=1, source_target_pairs={{0,2},{1,3},{2,0},{3,1},{4,6},{5,7},{6,4},{7,5},{8,10},{9,11},{10,... | collective-permute-start | bytes 589832 | tf_op jit(solution)/shard_map/ppermute | solution.py:33
  43.2 0.0 collective-permute-done.6.refs_0_
  43.2 1.5 %collective-permute-start.15 = (f32[2,96,256]{2,1,0:T(8,128)S(1)}, f32[2,96,256]{2,1,0:T(8,128)S(1)}, u32[]{:S(2)}, u32[]{:S(2)}) collective-permute-start(f32[2,96,256]{2,1,0:T(8,128)S(1)} %get-tuple-element.76), channel_id=1, source_target_pairs={{0,3},{1,2},{2,1},{3,0},{4,7},{5,6},{6,5},{7,4},{8,11},{9,10},{10,... | collective-permute-start | bytes 589832 | tf_op jit(solution)/shard_map/ppermute | solution.py:33
  44.7 0.3 shard_map.40
  45.0 0.0 collective-permute-done.11.refs_6_
  45.0 1.5 %collective-permute-start.7 = (f32[2,96,128]{2,1,0:T(8,128)S(1)}, f32[2,96,128]{2,1,0:T(8,128)S(1)}, u32[]{:S(2)}, u32[]{:S(2)}) collective-permute-start(f32[2,96,128]{2,1,0:T(8,128)S(1)} %get-tuple-element.65), channel_id=1, source_target_pairs={{0,1},{1,0},{2,3},{3,2},{4,5},{5,4},{6,7},{7,6},{8,9},{9,8},{10,11... | collective-permute-start | bytes 294920 | tf_op jit(solution)/shard_map/ppermute | solution.py:33
  46.5 0.0 collective-permute-done.12.refs_7_
  46.5 0.6 %collective-permute-start.8 = (f32[2,96,128]{2,1,0:T(8,128)S(1)}, f32[2,96,128]{2,1,0:T(8,128)S(1)}, u32[]{:S(2)}, u32[]{:S(2)}) collective-permute-start(f32[2,96,128]{2,1,0:T(8,128)S(1)} %get-tuple-element.66), channel_id=1, source_target_pairs={{0,2},{1,3},{2,0},{3,1},{4,6},{5,7},{6,4},{7,5},{8,10},{9,11},{10,... | collective-permute-start | bytes 294920 | tf_op jit(solution)/shard_map/ppermute | solution.py:33
  47.1 1.1 %collective-permute-done.13.refs_9_ = f32[2,96,256]{2,1,0:T(8,128)S(1)} collective-permute-done((f32[2,96,256]{2,1,0:T(8,128)S(1)}, f32[2,96,256]{2,1,0:T(8,128)S(1)}, u32[]{:S(2)}, u32[]{:S(2)}) %collective-permute-start.13) | collective-permute-done | bytes 196640 | tf_op jit(solution)/shard_map/ppermute | solution.py:33
  48.2 1.3 %collective-permute-start.9 = (f32[2,96,128]{2,1,0:T(8,128)S(1)}, f32[2,96,128]{2,1,0:T(8,128)S(1)}, u32[]{:S(2)}, u32[]{:S(2)}) collective-permute-start(f32[2,96,128]{2,1,0:T(8,128)S(1)} %get-tuple-element.67), channel_id=1, source_target_pairs={{0,3},{1,2},{2,1},{3,0},{4,7},{5,6},{6,5},{7,4},{8,11},{9,10},{10,... | collective-permute-start | bytes 294920 | tf_op jit(solution)/shard_map/ppermute | solution.py:33
  49.5 0.3 shard_map.41.refs_4_
  49.8 1.5 %collective-permute-done.14.refs_10_ = f32[2,96,256]{2,1,0:T(8,128)S(1)} collective-permute-done((f32[2,96,256]{2,1,0:T(8,128)S(1)}, f32[2,96,256]{2,1,0:T(8,128)S(1)}, u32[]{:S(2)}, u32[]{:S(2)}) %collective-permute-start.14) | collective-permute-done | bytes 196640 | tf_op jit(solution)/shard_map/ppermute | solution.py:33
  51.2 0.0 collective-permute-done.15.refs_11_
  51.2 1.5 %shard_map.43.refs_8_ = f32[2,4,96,768]{3,2,1,0:T(8,128)} custom-call(f32[8,128]{1,0:T(8,128)S(1)} %broadcast_in_dim.6.refs_0_, f32[8,128]{1,0:T(8,128)S(1)} %collective-permute-done.1.refs_1_, f32[8,128]{1,0:T(8,128)S(1)} %collective-permute-done.2.refs_2_, f32[8,128]{1,0:T(8,128)S(1)} %collective-permute-done.3.refs_3_, ...), custom_call_target="tpu_custom_call" | custom-call | tf_op jit(solution)/shard_map/pallas_call | solution.py:45
  52.8 0.0 collective-permute-done.7.refs_5_
  52.8 0.0 collective-permute-done.8.refs_6_
  52.8 0.9 %collective-permute-done.9.refs_7_ = f32[2,96,128]{2,1,0:T(8,128)S(1)} collective-permute-done((f32[2,96,128]{2,1,0:T(8,128)S(1)}, f32[2,96,128]{2,1,0:T(8,128)S(1)}, u32[]{:S(2)}, u32[]{:S(2)}) %collective-permute-start.9) | collective-permute-done | bytes 98336 | tf_op jit(solution)/shard_map/ppermute | solution.py:33
  53.7 0.9 %shard_map.44 = f32[2,4,96,768]{3,2,1,0:T(8,128)} custom-call(f32[8,128]{1,0:T(8,128)S(1)} %broadcast_in_dim.6.refs_0_, f32[8,128]{1,0:T(8,128)S(1)} %collective-permute-done.1.refs_1_, f32[8,128]{1,0:T(8,128)S(1)} %collective-permute-done.2.refs_2_, f32[8,128]{1,0:T(8,128)S(1)} %collective-permute-done.3.refs_3_, ...), custom_call_target="tpu_custom_call", output_to_operand_aliasing={{}: (8, {})} | custom-call | tf_op jit(solution)/shard_map/pallas_call | solution.py:45
  (1 shorter events, 0.0 us)
Async XLA Ops:
  0.9 10.4 %collective-permute-start = (f32[2,128,128]{2,1,0:T(8,128)S(1)}, f32[2,128,128]{2,1,0:T(8,128)S(1)}, u32[]{:S(2)}, u32[]{:S(2)}) collective-permute-start(f32[2,128,128]{2,1,0:T(8,128)S(1)} %slice.4), channel_id=1, source_target_pairs={{0,16},{4,20},{8,24},{12,28},{16,0},{20,4},{24,8},{28,12},{1,17},{... | collective-permute-start | bytes 393224 | tf_op jit(solution)/shard_map/ppermute | solution.py:33
  5.1 1.6 %copy-start = (f32[1,1,2,512,512]{4,3,2,1,0:T(8,128)S(1)}, f32[1,1,2,512,512]{4,3,2,1,0:T(8,128)}, u32[]{:S(2)}) copy-start(f32[1,1,2,512,512]{4,3,2,1,0:T(8,128)} %param.3) | copy-start | bytes 6291460
  6.6 0.7 %copy-start.1 = (s32[1,1,4]{2,1,0:T(1,128)S(1)}, s32[1,1,4]{2,1,0:T(1,128)}, u32[]{:S(2)}) copy-start(s32[1,1,4]{2,1,0:T(1,128)} %param.5) | copy-start | bytes 52
  8.5 16.3 %collective-permute-start.4 = (f32[2,128,256]{2,1,0:T(8,128)S(1)}, f32[2,128,256]{2,1,0:T(8,128)S(1)}, u32[]{:S(2)}, u32[]{:S(2)}) collective-permute-start(f32[2,128,256]{2,1,0:T(8,128)S(1)} %get-tuple-element.62), channel_id=1, source_target_pairs={{8,24},{12,28},{16,0},{20,4},{9,25},{13,29},{17,1},{21,5},{10,26},... | collective-permute-start | bytes 786440 | tf_op jit(solution)/shard_map/ppermute | solution.py:233
  13.0 11.9 %collective-permute-start.5 = (f32[2,128,256]{2,1,0:T(8,128)S(1)}, f32[2,128,256]{2,1,0:T(8,128)S(1)}, u32[]{:S(2)}, u32[]{:S(2)}) collective-permute-start(f32[2,128,256]{2,1,0:T(8,128)S(1)} %get-tuple-element.62), channel_id=1, source_target_pairs={{0,16},{4,20},{24,8},{28,12},{1,17},{5,21},{25,9},{29,13},{2,18},{... | collective-permute-start | bytes 786440 | tf_op jit(solution)/shard_map/ppermute | solution.py:245
  18.5 24.1 %collective-permute-start.10 = (f32[2,96,384]{2,1,0:T(8,128)S(1)}, f32[2,96,384]{2,1,0:T(8,128)S(1)}, u32[]{:S(2)}, u32[]{:S(2)}) collective-permute-start(f32[2,96,384]{2,1,0:T(8,128)S(1)} %get-tuple-element.68), channel_id=1, source_target_pairs={{0,1},{1,0},{2,3},{3,2},{4,5},{5,4},{6,7},{7,6},{8,9},{9,8},{10,11... | collective-permute-start | bytes 884744 | tf_op jit(solution)/shard_map/ppermute | solution.py:33
  20.1 25.0 %collective-permute-start.11 = (f32[2,96,384]{2,1,0:T(8,128)S(1)}, f32[2,96,384]{2,1,0:T(8,128)S(1)}, u32[]{:S(2)}, u32[]{:S(2)}) collective-permute-start(f32[2,96,384]{2,1,0:T(8,128)S(1)} %get-tuple-element.69), channel_id=1, source_target_pairs={{0,2},{1,3},{2,0},{3,1},{4,6},{5,7},{6,4},{7,5},{8,10},{9,11},{10,... | collective-permute-start | bytes 884744 | tf_op jit(solution)/shard_map/ppermute | solution.py:33
  21.6 24.9 %collective-permute-start.12 = (f32[2,96,384]{2,1,0:T(8,128)S(1)}, f32[2,96,384]{2,1,0:T(8,128)S(1)}, u32[]{:S(2)}, u32[]{:S(2)}) collective-permute-start(f32[2,96,384]{2,1,0:T(8,128)S(1)} %get-tuple-element.70), channel_id=1, source_target_pairs={{0,3},{1,2},{2,1},{3,0},{4,7},{5,6},{6,5},{7,4},{8,11},{9,10},{10,... | collective-permute-start | bytes 884744 | tf_op jit(solution)/shard_map/ppermute | solution.py:33
  24.9 18.4 %collective-permute-start.6 = (f32[2,128,128]{2,1,0:T(8,128)S(1)}, f32[2,128,128]{2,1,0:T(8,128)S(1)}, u32[]{:S(2)}, u32[]{:S(2)}) collective-permute-start(f32[2,128,128]{2,1,0:T(8,128)S(1)} %get-tuple-element.63), channel_id=1, source_target_pairs={{0,16},{4,20},{8,24},{12,28},{16,0},{20,4},{24,8},{28,12},{1,17},{... | collective-permute-start | bytes 393224 | tf_op jit(solution)/shard_map/ppermute | solution.py:33
  26.0 8.0 %collective-permute-start.3 = (f32[8,128]{1,0:T(8,128)S(1)}, f32[8,128]{1,0:T(8,128)S(1)}, u32[]{:S(2)}, u32[]{:S(2)}) collective-permute-start(f32[8,128]{1,0:T(8,128)S(1)} %broadcast_in_dim.6.refs_0_), channel_id=1, source_target_pairs={{0,3},{1,2},{2,1},{3,0},{4,7},{5,6},{6,5},{7,4},{8,11},{9,10},{10,... | collective-permute-start | bytes 12296 | tf_op jit(solution)/shard_map/ppermute | solution.py:33
  34.0 3.6 %collective-permute-start.2 = (f32[8,128]{1,0:T(8,128)S(1)}, f32[8,128]{1,0:T(8,128)S(1)}, u32[]{:S(2)}, u32[]{:S(2)}) collective-permute-start(f32[8,128]{1,0:T(8,128)S(1)} %broadcast_in_dim.6.refs_0_), channel_id=1, source_target_pairs={{0,2},{1,3},{2,0},{3,1},{4,6},{5,7},{6,4},{7,5},{8,10},{9,11},{10,... | collective-permute-start | bytes 12296 | tf_op jit(solution)/shard_map/ppermute | solution.py:33
  37.6 3.6 %collective-permute-start.1 = (f32[8,128]{1,0:T(8,128)S(1)}, f32[8,128]{1,0:T(8,128)S(1)}, u32[]{:S(2)}, u32[]{:S(2)}) collective-permute-start(f32[8,128]{1,0:T(8,128)S(1)} %broadcast_in_dim.6.refs_0_), channel_id=1, source_target_pairs={{0,1},{1,0},{2,3},{3,2},{4,5},{5,4},{6,7},{7,6},{8,9},{9,8},{10,11... | collective-permute-start | bytes 12296 | tf_op jit(solution)/shard_map/ppermute | solution.py:33
  41.2 7.0 %collective-permute-start.13 = (f32[2,96,256]{2,1,0:T(8,128)S(1)}, f32[2,96,256]{2,1,0:T(8,128)S(1)}, u32[]{:S(2)}, u32[]{:S(2)}) collective-permute-start(f32[2,96,256]{2,1,0:T(8,128)S(1)} %get-tuple-element.74), channel_id=1, source_target_pairs={{0,1},{1,0},{2,3},{3,2},{4,5},{5,4},{6,7},{7,6},{8,9},{9,8},{10,11... | collective-permute-start | bytes 589832 | tf_op jit(solution)/shard_map/ppermute | solution.py:33
  42.6 8.6 %collective-permute-start.14 = (f32[2,96,256]{2,1,0:T(8,128)S(1)}, f32[2,96,256]{2,1,0:T(8,128)S(1)}, u32[]{:S(2)}, u32[]{:S(2)}) collective-permute-start(f32[2,96,256]{2,1,0:T(8,128)S(1)} %get-tuple-element.75), channel_id=1, source_target_pairs={{0,2},{1,3},{2,0},{3,1},{4,6},{5,7},{6,4},{7,5},{8,10},{9,11},{10,... | collective-permute-start | bytes 589832 | tf_op jit(solution)/shard_map/ppermute | solution.py:33
  43.2 8.0 %collective-permute-start.15 = (f32[2,96,256]{2,1,0:T(8,128)S(1)}, f32[2,96,256]{2,1,0:T(8,128)S(1)}, u32[]{:S(2)}, u32[]{:S(2)}) collective-permute-start(f32[2,96,256]{2,1,0:T(8,128)S(1)} %get-tuple-element.76), channel_id=1, source_target_pairs={{0,3},{1,2},{2,1},{3,0},{4,7},{5,6},{6,5},{7,4},{8,11},{9,10},{10,... | collective-permute-start | bytes 589832 | tf_op jit(solution)/shard_map/ppermute | solution.py:33
  45.0 7.7 %collective-permute-start.7 = (f32[2,96,128]{2,1,0:T(8,128)S(1)}, f32[2,96,128]{2,1,0:T(8,128)S(1)}, u32[]{:S(2)}, u32[]{:S(2)}) collective-permute-start(f32[2,96,128]{2,1,0:T(8,128)S(1)} %get-tuple-element.65), channel_id=1, source_target_pairs={{0,1},{1,0},{2,3},{3,2},{4,5},{5,4},{6,7},{7,6},{8,9},{9,8},{10,11... | collective-permute-start | bytes 294920 | tf_op jit(solution)/shard_map/ppermute | solution.py:33
  46.5 6.3 %collective-permute-start.8 = (f32[2,96,128]{2,1,0:T(8,128)S(1)}, f32[2,96,128]{2,1,0:T(8,128)S(1)}, u32[]{:S(2)}, u32[]{:S(2)}) collective-permute-start(f32[2,96,128]{2,1,0:T(8,128)S(1)} %get-tuple-element.66), channel_id=1, source_target_pairs={{0,2},{1,3},{2,0},{3,1},{4,6},{5,7},{6,4},{7,5},{8,10},{9,11},{10,... | collective-permute-start | bytes 294920 | tf_op jit(solution)/shard_map/ppermute | solution.py:33
  48.2 5.5 %collective-permute-start.9 = (f32[2,96,128]{2,1,0:T(8,128)S(1)}, f32[2,96,128]{2,1,0:T(8,128)S(1)}, u32[]{:S(2)}, u32[]{:S(2)}) collective-permute-start(f32[2,96,128]{2,1,0:T(8,128)S(1)} %get-tuple-element.67), channel_id=1, source_target_pairs={{0,3},{1,2},{2,1},{3,0},{4,7},{5,6},{6,5},{7,4},{8,11},{9,10},{10,... | collective-permute-start | bytes 294920 | tf_op jit(solution)/shard_map/ppermute | solution.py:33

commit v4 on v3

--- a/solution.py
+++ b/solution.py
@@ -77,6 +77,12 @@
     for p in range(groups):
         index = jnp.where(owner_ref[p] == dest, jnp.int32(p), index)
     return index
+
+
+def corner_kernel(ext, iti_ref, out_ref, sem):
+    copy = pltpu.make_async_copy(iti_ref.at[:, ext:, ext:], out_ref, sem)
+    copy.start()
+    copy.wait()
 
 
 def prepare_kernel(edge, ext, groups, cuts, owner_ref, iti_ref, *refs):
@@ -215,7 +221,15 @@
     across = lax.axis_size("gx") // 2
     cuts = [(0 * edge, 2 * edge), (2 * edge, 3 * edge)]
     assert len(cuts) == PIECES
-    qss = permute(ownmap[:, ext:, ext:], "gx", across)
+    corner = pl.pallas_call(
+        functools.partial(corner_kernel, ext),
+        out_shape=f32(2, edge, edge),
+        in_specs=[HBM],
+        out_specs=VMEM,
+        scratch_shapes=[pltpu.SemaphoreType.DMA],
+        compiler_params=limit(52),
+    )(ownmap)
+    qss = permute(corner, "gx", across)
     *pieces, base, res, res_high, res_low, rss_high, rss_low, rse_high, rse_low = call(
         functools.partial(prepare_kernel, edge, ext, groups, cuts),
         out_shape=[f32(2, edge, hi - lo) for lo, hi in cuts]
@@ -244,7 +258,7 @@
     piece, far_high = lax.optimization_barrier((pieces[0], far_high))
     qse = [[early, lax.ppermute(piece, "gx", last)]]
     for piece in pieces[1:]:
-        piece, qse[-1] = lax.optimization_barrier((piece, qse[-1]))
+        piece, far_high = lax.optimization_barrier((piece, far_high))
         qse.append([permute(piece, "gx", across)])
     high, low, *own = call(
         functools.partial(own_half_kernel, edge, ext, rows_each),

time: 54.9 us -> 55.3 us (level)
  waiting for transfers between devices: 18.1 us -> 20.8 us
  local copies, waits for them, and re-layouts: 3.17 us -> 0.66 us
  Pallas kernels: 7.94 us -> 9 us
  starting transfers between devices: 24.6 us -> 23.9 us
    ppermute x14, waiting for transfers between devices: 15.4 us -> 20.8 us  [permute(): lax.ppermute(x, axis, [(i, i ^ offset) for i in range(lax.axis_size(axis))])]
    ppermute x1, waiting for transfers between devices: 2.78 us -> 0.01 us  [on_device(): early = lax.ppermute(pieces[0], 'gx', first)]
    ppermute x1, starting transfers between devices: 3.98 us -> 2.39 us  [on_device(): qse = [[early, lax.ppermute(piece, 'gx', last)]]]
    unnamed x4, local copies, waits for them, and re-layouts: 2.25 us -> 0.66 us
    pallas_call x0 -> x1, Pallas kernels: none -> 1.07 us  [on_device(): pl.pallas_call(functools.partial(corner_kernel, ext), out_shape=f32(2, ed...]
    slice x1 -> x0, local copies, waits for them, and re-layouts: 0.92 us -> none  [on_device(): qss = permute(ownmap[:, ext:, ext:], 'gx', across)]
    ppermute x14, starting transfers between devices: 19.4 us -> 20.2 us  [permute(): lax.ppermute(x, axis, [(i, i ^ offset) for i in range(lax.axis_size(axis))])]
  transfers between devices with their start and end apart: 16 -> 16, of which waited for: 8 -> 7; matrix products, arithmetic and copies ran while one was open for 0% -> 0% of each run, Pallas kernels for 13% -> 13%
where the time goes in v4:
time: 55.3 us; the launch traced here: 55.1 us
  starting transfers between devices  23.9 us (43%)
  waiting for transfers between devices  20.8 us (38%)
  Pallas kernels  9 us (16%)
  between operations  0.77 us (1%)
  local copies, waits for them, and re-layouts  0.66 us (1%)
    ppermute x14, waiting for transfers between devices, permute(): lax.ppermute(x, axis, [(i, i ^ offset) for i in range(lax.axis_size(axis))])  20.8 us
    ppermute x14, starting transfers between devices, permute(): lax.ppermute(x, axis, [(i, i ^ offset) for i in range(lax.axis_size(axis))])  20.2 us
    pallas_call x8, Pallas kernels, run(): return pl.pallas_call(kernel, **options)(*args)  7.94 us
    ppermute x1, starting transfers between devices, on_device(): qse = [[early, lax.ppermute(piece, 'gx', last)]]  2.39 us
    ppermute x1, starting transfers between devices, on_device(): early = lax.ppermute(pieces[0], 'gx', first)  1.29 us
  transfers between devices with their start and end apart: 16, of which 7 were waited for; matrix products, arithmetic and copies ran while one was open for 0% of the time, Pallas kernels for 13%

profile of v4, /device:TPU:0, one launch (start us, length us, event | category | flops | bytes accessed | tf_op | source)
XLA Modules:
  0.0 55.1 jit_solution(246275902155683921)
XLA Ops:
  0.0 0.0 copy-start
  0.0 1.1 %shard_map.38 = f32[2,128,128]{2,1,0:T(8,128)S(1)} custom-call(f32[2,512,512]{2,1,0:T(8,128)} %bitcast.4), custom_call_target="tpu_custom_call" | custom-call | tf_op jit(solution)/shard_map/pallas_call | solution.py:224
  1.1 4.1 %collective-permute-start = (f32[2,128,128]{2,1,0:T(8,128)S(1)}, f32[2,128,128]{2,1,0:T(8,128)S(1)}, u32[]{:S(2)}, u32[]{:S(2)}) collective-permute-start(f32[2,128,128]{2,1,0:T(8,128)S(1)} %shard_map.38), channel_id=1, source_target_pairs={{0,16},{4,20},{8,24},{12,28},{16,0},{20,4},{24,8},{28,12},{1,17},{... | collective-permute-start | bytes 393224 | tf_op jit(solution)/shard_map/ppermute | solution.py:33
  5.2 0.0 copy-done
  5.2 0.0 copy-start.1
  5.2 0.7 %copy-done.1 = s32[1,1,4]{2,1,0:T(1,128)S(1)} copy-done((s32[1,1,4]{2,1,0:T(1,128)S(1)}, s32[1,1,4]{2,1,0:T(1,128)}, u32[]{:S(2)}) %copy-start.1) | copy-done | bytes 40
  5.9 1.2 %shard_map.37 = (f32[2,128,256]{2,1,0:T(8,128)S(1)}, f32[2,128,128]{2,1,0:T(8,128)S(1)}, f32[2,384,384]{2,1,0:T(8,128)S(1)}, f32[384,256]{1,0:T(8,128)S(1)}, bf1...) custom-call(s32[4]{0:T(128)S(1)} %bitcast.6, ...), custom_call_target="tpu_custom_call" | custom-call | tf_op jit(solution)/shard_map/pallas_call | solution.py:45
  7.1 1.3 %collective-permute-start.11 = (f32[2,128,256]{2,1,0:T(8,128)S(1)}, f32[2,128,256]{2,1,0:T(8,128)S(1)}, u32[]{:S(2)}, u32[]{:S(2)}) collective-permute-start(f32[2,128,256]{2,1,0:T(8,128)S(1)} %get-tuple-element.70), channel_id=1, source_target_pairs={{8,24},{12,28},{16,0},{20,4},{9,25},{13,29},{17,1},{21,5},{10,26},... | collective-permute-start | bytes 786440 | tf_op jit(solution)/shard_map/ppermute | solution.py:247
  8.4 3.1 %collective-permute-done.qss_ref = f32[2,128,128]{2,1,0:T(8,128)S(1)} collective-permute-done((f32[2,128,128]{2,1,0:T(8,128)S(1)}, f32[2,128,128]{2,1,0:T(8,128)S(1)}, u32[]{:S(2)}, u32[]{:S(2)}) %collective-permute-start) | collective-permute-done | bytes 131104 | tf_op jit(solution)/shard_map/ppermute | solution.py:33
  11.5 1.6 %shard_map.39 = (bf16[4,128,256]{2,1,0:T(8,128)(2,1)S(1)}, bf16[4,128,256]{2,1,0:T(8,128)(2,1)S(1)}, bf16[128,768]{1,0:T(8,128)(2,1)S(1)}, bf16[128,768]{1,0:T(8...) custom-call(f32[2,128,128]{2,1,0:T(8,128)S(1)} %collective-permute-done.qss_ref,, ...), custom_call_target="tpu_custom_call" | custom-call | tf_op jit(solution)/shard_map/pallas_call | solution.py:45
  13.1 2.4 %collective-permute-start.12 = (f32[2,128,256]{2,1,0:T(8,128)S(1)}, f32[2,128,256]{2,1,0:T(8,128)S(1)}, u32[]{:S(2)}, u32[]{:S(2)}) collective-permute-start(f32[2,128,256]{2,1,0:T(8,128)S(1)} %get-tuple-element.70), channel_id=1, source_target_pairs={{0,16},{4,20},{24,8},{28,12},{1,17},{5,21},{25,9},{29,13},{2,18},{... | collective-permute-start | bytes 786440 | tf_op jit(solution)/shard_map/ppermute | solution.py:259
  15.5 1.5 %shard_map.40 = (bf16[288,256]{1,0:T(8,128)(2,1)S(1)}, bf16[288,256]{1,0:T(8,128)(2,1)S(1)}, f32[2,96,384]{2,1,0:T(8,128)S(1)}, f32[2,96,384]{2,1,0:T(8,128)S(1)}) custom-call(f32[2,384,384]{2,1,0:T(8,128)S(1)} %get-tuple-element.40.base_ref, f32[384,256]{1,0:T(8,128)S(1)} %get-tuple-element.41.res_ref, bf16[384,256]{1,0:T(8,128)(2,1)S(1)} %get-tuple-element.42.res_high, ...), custom_call_target="tpu_custom_call" | custom-call | tf_op jit(solution)/shard_map/pallas_call | solution.py:45
  17.1 1.6 %collective-permute-start.8 = (f32[2,96,384]{2,1,0:T(8,128)S(1)}, f32[2,96,384]{2,1,0:T(8,128)S(1)}, u32[]{:S(2)}, u32[]{:S(2)}) collective-permute-start(f32[2,96,384]{2,1,0:T(8,128)S(1)} %get-tuple-element.67), channel_id=1, source_target_pairs={{0,1},{1,0},{2,3},{3,2},{4,5},{5,4},{6,7},{7,6},{8,9},{9,8},{10,11... | collective-permute-start | bytes 884744 | tf_op jit(solution)/shard_map/ppermute | solution.py:33
  19.3 1.6 %collective-permute-start.3 = (f32[8,128]{1,0:T(8,128)S(1)}, f32[8,128]{1,0:T(8,128)S(1)}, u32[]{:S(2)}, u32[]{:S(2)}) collective-permute-start(f32[8,128]{1,0:T(8,128)S(1)} %broadcast_in_dim.6.refs_0_), channel_id=1, source_target_pairs={{0,3},{1,2},{2,1},{3,0},{4,7},{5,6},{6,5},{7,4},{8,11},{9,10},{10,... | collective-permute-start | bytes 12296 | tf_op jit(solution)/shard_map/ppermute | solution.py:33
  20.9 0.5 collective-permute-start.2
  21.4 4.7 %collective-permute-done.3.refs_3_ = f32[8,128]{1,0:T(8,128)S(1)} collective-permute-done((f32[8,128]{1,0:T(8,128)S(1)}, f32[8,128]{1,0:T(8,128)S(1)}, u32[]{:S(2)}, u32[]{:S(2)}) %collective-permute-start.3) | collective-permute-done | bytes 4128 | tf_op jit(solution)/shard_map/ppermute | solution.py:33
  26.1 0.5 collective-permute-start.9
  26.6 0.0 collective-permute-done.2.refs_2_
  26.6 2.4 %collective-permute-start.10 = (f32[2,96,384]{2,1,0:T(8,128)S(1)}, f32[2,96,384]{2,1,0:T(8,128)S(1)}, u32[]{:S(2)}, u32[]{:S(2)}) collective-permute-start(f32[2,96,384]{2,1,0:T(8,128)S(1)} %get-tuple-element.69), channel_id=1, source_target_pairs={{0,3},{1,2},{2,1},{3,0},{4,7},{5,6},{6,5},{7,4},{8,11},{9,10},{10,... | collective-permute-start | bytes 884744 | tf_op jit(solution)/shard_map/ppermute | solution.py:33
  29.1 0.0 collective-permute-done.11.refs_0_
  29.1 0.0 collective-permute-start.4
  29.1 0.0 collective-permute-done.12.refs_1_
  29.1 0.6 %collective-permute-start.1 = (f32[8,128]{1,0:T(8,128)S(1)}, f32[8,128]{1,0:T(8,128)S(1)}, u32[]{:S(2)}, u32[]{:S(2)}) collective-permute-start(f32[8,128]{1,0:T(8,128)S(1)} %broadcast_in_dim.6.refs_0_), channel_id=1, source_target_pairs={{0,1},{1,0},{2,3},{3,2},{4,5},{5,4},{6,7},{7,6},{8,9},{9,8},{10,11... | collective-permute-start | bytes 12296 | tf_op jit(solution)/shard_map/ppermute | solution.py:33
  29.7 0.5 shard_map.43
  30.2 4.8 %collective-permute-done.1.refs_1_ = f32[8,128]{1,0:T(8,128)S(1)} collective-permute-done((f32[8,128]{1,0:T(8,128)S(1)}, f32[8,128]{1,0:T(8,128)S(1)}, u32[]{:S(2)}, u32[]{:S(2)}) %collective-permute-start.1) | collective-permute-done | bytes 4128 | tf_op jit(solution)/shard_map/ppermute | solution.py:33
  35.0 1.5 %collective-permute-start.13 = (f32[2,96,256]{2,1,0:T(8,128)S(1)}, f32[2,96,256]{2,1,0:T(8,128)S(1)}, u32[]{:S(2)}, u32[]{:S(2)}) collective-permute-start(f32[2,96,256]{2,1,0:T(8,128)S(1)} %get-tuple-element.72), channel_id=1, source_target_pairs={{0,1},{1,0},{2,3},{3,2},{4,5},{5,4},{6,7},{7,6},{8,9},{9,8},{10,11... | collective-permute-start | bytes 589832 | tf_op jit(solution)/shard_map/ppermute | solution.py:33
  36.5 0.0 collective-permute-done.4.refs_0_
  36.5 0.8 %collective-permute-start.14 = (f32[2,96,256]{2,1,0:T(8,128)S(1)}, f32[2,96,256]{2,1,0:T(8,128)S(1)}, u32[]{:S(2)}, u32[]{:S(2)}) collective-permute-start(f32[2,96,256]{2,1,0:T(8,128)S(1)} %get-tuple-element.73), channel_id=1, source_target_pairs={{0,2},{1,3},{2,0},{3,1},{4,6},{5,7},{6,4},{7,5},{8,10},{9,11},{10,... | collective-permute-start | bytes 589832 | tf_op jit(solution)/shard_map/ppermute | solution.py:33
  37.3 0.0 collective-permute-done.8.refs_5_
  37.3 1.2 %collective-permute-start.15 = (f32[2,96,256]{2,1,0:T(8,128)S(1)}, f32[2,96,256]{2,1,0:T(8,128)S(1)}, u32[]{:S(2)}, u32[]{:S(2)}) collective-permute-start(f32[2,96,256]{2,1,0:T(8,128)S(1)} %get-tuple-element.74), channel_id=1, source_target_pairs={{0,3},{1,2},{2,1},{3,0},{4,7},{5,6},{6,5},{7,4},{8,11},{9,10},{10,... | collective-permute-start | bytes 589832 | tf_op jit(solution)/shard_map/ppermute | solution.py:33
  38.5 0.3 shard_map.41
  38.8 4.5 %collective-permute-done.9.refs_6_ = f32[2,96,384]{2,1,0:T(8,128)S(1)} collective-permute-done((f32[2,96,384]{2,1,0:T(8,128)S(1)}, f32[2,96,384]{2,1,0:T(8,128)S(1)}, u32[]{:S(2)}, u32[]{:S(2)}) %collective-permute-start.9) | collective-permute-done | bytes 294944 | tf_op jit(solution)/shard_map/ppermute | solution.py:33
  43.3 3.9 %collective-permute-start.5 = (f32[2,96,128]{2,1,0:T(8,128)S(1)}, f32[2,96,128]{2,1,0:T(8,128)S(1)}, u32[]{:S(2)}, u32[]{:S(2)}) collective-permute-start(f32[2,96,128]{2,1,0:T(8,128)S(1)} %get-tuple-element.64), channel_id=1, source_target_pairs={{0,1},{1,0},{2,3},{3,2},{4,5},{5,4},{6,7},{7,6},{8,9},{9,8},{10,11... | collective-permute-start | bytes 294920 | tf_op jit(solution)/shard_map/ppermute | solution.py:33
  47.2 0.0 collective-permute-done.10.refs_7_
  47.2 1.5 %collective-permute-start.6 = (f32[2,96,128]{2,1,0:T(8,128)S(1)}, f32[2,96,128]{2,1,0:T(8,128)S(1)}, u32[]{:S(2)}, u32[]{:S(2)}) collective-permute-start(f32[2,96,128]{2,1,0:T(8,128)S(1)} %get-tuple-element.65), channel_id=1, source_target_pairs={{0,2},{1,3},{2,0},{3,1},{4,6},{5,7},{6,4},{7,5},{8,10},{9,11},{10,... | collective-permute-start | bytes 294920 | tf_op jit(solution)/shard_map/ppermute | solution.py:33
  48.7 0.0 collective-permute-done.13.refs_9_
  48.7 0.0 collective-permute-start.7
  48.7 0.3 shard_map.42.refs_4_
  49.0 0.7 %collective-permute-done.14.refs_10_ = f32[2,96,256]{2,1,0:T(8,128)S(1)} collective-permute-done((f32[2,96,256]{2,1,0:T(8,128)S(1)}, f32[2,96,256]{2,1,0:T(8,128)S(1)}, u32[]{:S(2)}, u32[]{:S(2)}) %collective-permute-start.14) | collective-permute-done | bytes 196640 | tf_op jit(solution)/shard_map/ppermute | solution.py:33
  49.7 0.0 collective-permute-done.15.refs_11_
  49.7 1.5 %shard_map.44.refs_8_ = f32[2,4,96,768]{3,2,1,0:T(8,128)} custom-call(f32[8,128]{1,0:T(8,128)S(1)} %broadcast_in_dim.6.refs_0_, f32[8,128]{1,0:T(8,128)S(1)} %collective-permute-done.1.refs_1_, f32[8,128]{1,0:T(8,128)S(1)} %collective-permute-done.2.refs_2_, f32[8,128]{1,0:T(8,128)S(1)} %collective-permute-done.3.refs_3_, ...), custom_call_target="tpu_custom_call" | custom-call | tf_op jit(solution)/shard_map/pallas_call | solution.py:45
  51.2 0.0 collective-permute-done.5.refs_5_
  51.3 0.5 collective-permute-done.6.refs_6_
  51.8 2.4 %collective-permute-done.7.refs_7_ = f32[2,96,128]{2,1,0:T(8,128)S(1)} collective-permute-done((f32[2,96,128]{2,1,0:T(8,128)S(1)}, f32[2,96,128]{2,1,0:T(8,128)S(1)}, u32[]{:S(2)}, u32[]{:S(2)}) %collective-permute-start.7) | collective-permute-done | bytes 98336 | tf_op jit(solution)/shard_map/ppermute | solution.py:33
  54.2 0.9 %shard_map.45 = f32[2,4,96,768]{3,2,1,0:T(8,128)} custom-call(f32[8,128]{1,0:T(8,128)S(1)} %broadcast_in_dim.6.refs_0_, f32[8,128]{1,0:T(8,128)S(1)} %collective-permute-done.1.refs_1_, f32[8,128]{1,0:T(8,128)S(1)} %collective-permute-done.2.refs_2_, f32[8,128]{1,0:T(8,128)S(1)} %collective-permute-done.3.refs_3_, ...), custom_call_target="tpu_custom_call", output_to_operand_aliasing={{}: (8, {})} | custom-call | tf_op jit(solution)/shard_map/pallas_call | solution.py:45
  (1 shorter events, 0.0 us)
Async XLA Ops:
  0.0 5.2 %copy-start = (f32[1,1,2,512,512]{4,3,2,1,0:T(8,128)S(1)}, f32[1,1,2,512,512]{4,3,2,1,0:T(8,128)}, u32[]{:S(2)}) copy-start(f32[1,1,2,512,512]{4,3,2,1,0:T(8,128)} %param.3) | copy-start | bytes 6291460
  1.1 10.4 %collective-permute-start = (f32[2,128,128]{2,1,0:T(8,128)S(1)}, f32[2,128,128]{2,1,0:T(8,128)S(1)}, u32[]{:S(2)}, u32[]{:S(2)}) collective-permute-start(f32[2,128,128]{2,1,0:T(8,128)S(1)} %shard_map.38), channel_id=1, source_target_pairs={{0,16},{4,20},{8,24},{12,28},{16,0},{20,4},{24,8},{28,12},{1,17},{... | collective-permute-start | bytes 393224 | tf_op jit(solution)/shard_map/ppermute | solution.py:33
  5.2 0.7 %copy-start.1 = (s32[1,1,4]{2,1,0:T(1,128)S(1)}, s32[1,1,4]{2,1,0:T(1,128)}, u32[]{:S(2)}) copy-start(s32[1,1,4]{2,1,0:T(1,128)} %param.5) | copy-start | bytes 52
  7.1 21.9 %collective-permute-start.11 = (f32[2,128,256]{2,1,0:T(8,128)S(1)}, f32[2,128,256]{2,1,0:T(8,128)S(1)}, u32[]{:S(2)}, u32[]{:S(2)}) collective-permute-start(f32[2,128,256]{2,1,0:T(8,128)S(1)} %get-tuple-element.70), channel_id=1, source_target_pairs={{8,24},{12,28},{16,0},{20,4},{9,25},{13,29},{17,1},{21,5},{10,26},... | collective-permute-start | bytes 786440 | tf_op jit(solution)/shard_map/ppermute | solution.py:247
  13.1 15.9 %collective-permute-start.12 = (f32[2,128,256]{2,1,0:T(8,128)S(1)}, f32[2,128,256]{2,1,0:T(8,128)S(1)}, u32[]{:S(2)}, u32[]{:S(2)}) collective-permute-start(f32[2,128,256]{2,1,0:T(8,128)S(1)} %get-tuple-element.70), channel_id=1, source_target_pairs={{0,16},{4,20},{24,8},{28,12},{1,17},{5,21},{25,9},{29,13},{2,18},{... | collective-permute-start | bytes 786440 | tf_op jit(solution)/shard_map/ppermute | solution.py:259
  17.1 20.2 %collective-permute-start.8 = (f32[2,96,384]{2,1,0:T(8,128)S(1)}, f32[2,96,384]{2,1,0:T(8,128)S(1)}, u32[]{:S(2)}, u32[]{:S(2)}) collective-permute-start(f32[2,96,384]{2,1,0:T(8,128)S(1)} %get-tuple-element.67), channel_id=1, source_target_pairs={{0,1},{1,0},{2,3},{3,2},{4,5},{5,4},{6,7},{7,6},{8,9},{9,8},{10,11... | collective-permute-start | bytes 884744 | tf_op jit(solution)/shard_map/ppermute | solution.py:33
  19.3 6.8 %collective-permute-start.3 = (f32[8,128]{1,0:T(8,128)S(1)}, f32[8,128]{1,0:T(8,128)S(1)}, u32[]{:S(2)}, u32[]{:S(2)}) collective-permute-start(f32[8,128]{1,0:T(8,128)S(1)} %broadcast_in_dim.6.refs_0_), channel_id=1, source_target_pairs={{0,3},{1,2},{2,1},{3,0},{4,7},{5,6},{6,5},{7,4},{8,11},{9,10},{10,... | collective-permute-start | bytes 12296 | tf_op jit(solution)/shard_map/ppermute | solution.py:33
  20.9 5.8 %collective-permute-start.2 = (f32[8,128]{1,0:T(8,128)S(1)}, f32[8,128]{1,0:T(8,128)S(1)}, u32[]{:S(2)}, u32[]{:S(2)}) collective-permute-start(f32[8,128]{1,0:T(8,128)S(1)} %broadcast_in_dim.6.refs_0_), channel_id=1, source_target_pairs={{0,2},{1,3},{2,0},{3,1},{4,6},{5,7},{6,4},{7,5},{8,10},{9,11},{10,... | collective-permute-start | bytes 12296 | tf_op jit(solution)/shard_map/ppermute | solution.py:33
  26.1 17.2 %collective-permute-start.9 = (f32[2,96,384]{2,1,0:T(8,128)S(1)}, f32[2,96,384]{2,1,0:T(8,128)S(1)}, u32[]{:S(2)}, u32[]{:S(2)}) collective-permute-start(f32[2,96,384]{2,1,0:T(8,128)S(1)} %get-tuple-element.68), channel_id=1, source_target_pairs={{0,2},{1,3},{2,0},{3,1},{4,6},{5,7},{6,4},{7,5},{8,10},{9,11},{10,... | collective-permute-start | bytes 884744 | tf_op jit(solution)/shard_map/ppermute | solution.py:33
  26.6 20.6 %collective-permute-start.10 = (f32[2,96,384]{2,1,0:T(8,128)S(1)}, f32[2,96,384]{2,1,0:T(8,128)S(1)}, u32[]{:S(2)}, u32[]{:S(2)}) collective-permute-start(f32[2,96,384]{2,1,0:T(8,128)S(1)} %get-tuple-element.69), channel_id=1, source_target_pairs={{0,3},{1,2},{2,1},{3,0},{4,7},{5,6},{6,5},{7,4},{8,11},{9,10},{10,... | collective-permute-start | bytes 884744 | tf_op jit(solution)/shard_map/ppermute | solution.py:33
  29.1 7.4 %collective-permute-start.4 = (f32[2,128,128]{2,1,0:T(8,128)S(1)}, f32[2,128,128]{2,1,0:T(8,128)S(1)}, u32[]{:S(2)}, u32[]{:S(2)}) collective-permute-start(f32[2,128,128]{2,1,0:T(8,128)S(1)} %get-tuple-element.62), channel_id=1, source_target_pairs={{0,16},{4,20},{8,24},{12,28},{16,0},{20,4},{24,8},{28,12},{1,17},{... | collective-permute-start | bytes 393224 | tf_op jit(solution)/shard_map/ppermute | solution.py:33
  29.1 5.9 %collective-permute-start.1 = (f32[8,128]{1,0:T(8,128)S(1)}, f32[8,128]{1,0:T(8,128)S(1)}, u32[]{:S(2)}, u32[]{:S(2)}) collective-permute-start(f32[8,128]{1,0:T(8,128)S(1)} %broadcast_in_dim.6.refs_0_), channel_id=1, source_target_pairs={{0,1},{1,0},{2,3},{3,2},{4,5},{5,4},{6,7},{7,6},{8,9},{9,8},{10,11... | collective-permute-start | bytes 12296 | tf_op jit(solution)/shard_map/ppermute | solution.py:33
  35.0 13.7 %collective-permute-start.13 = (f32[2,96,256]{2,1,0:T(8,128)S(1)}, f32[2,96,256]{2,1,0:T(8,128)S(1)}, u32[]{:S(2)}, u32[]{:S(2)}) collective-permute-start(f32[2,96,256]{2,1,0:T(8,128)S(1)} %get-tuple-element.72), channel_id=1, source_target_pairs={{0,1},{1,0},{2,3},{3,2},{4,5},{5,4},{6,7},{7,6},{8,9},{9,8},{10,11... | collective-permute-start | bytes 589832 | tf_op jit(solution)/shard_map/ppermute | solution.py:33
  36.5 13.2 %collective-permute-start.14 = (f32[2,96,256]{2,1,0:T(8,128)S(1)}, f32[2,96,256]{2,1,0:T(8,128)S(1)}, u32[]{:S(2)}, u32[]{:S(2)}) collective-permute-start(f32[2,96,256]{2,1,0:T(8,128)S(1)} %get-tuple-element.73), channel_id=1, source_target_pairs={{0,2},{1,3},{2,0},{3,1},{4,6},{5,7},{6,4},{7,5},{8,10},{9,11},{10,... | collective-permute-start | bytes 589832 | tf_op jit(solution)/shard_map/ppermute | solution.py:33
  37.3 12.4 %collective-permute-start.15 = (f32[2,96,256]{2,1,0:T(8,128)S(1)}, f32[2,96,256]{2,1,0:T(8,128)S(1)}, u32[]{:S(2)}, u32[]{:S(2)}) collective-permute-start(f32[2,96,256]{2,1,0:T(8,128)S(1)} %get-tuple-element.74), channel_id=1, source_target_pairs={{0,3},{1,2},{2,1},{3,0},{4,7},{5,6},{6,5},{7,4},{8,11},{9,10},{10,... | collective-permute-start | bytes 589832 | tf_op jit(solution)/shard_map/ppermute | solution.py:33
  43.3 8.0 %collective-permute-start.5 = (f32[2,96,128]{2,1,0:T(8,128)S(1)}, f32[2,96,128]{2,1,0:T(8,128)S(1)}, u32[]{:S(2)}, u32[]{:S(2)}) collective-permute-start(f32[2,96,128]{2,1,0:T(8,128)S(1)} %get-tuple-element.64), channel_id=1, source_target_pairs={{0,1},{1,0},{2,3},{3,2},{4,5},{5,4},{6,7},{7,6},{8,9},{9,8},{10,11... | collective-permute-start | bytes 294920 | tf_op jit(solution)/shard_map/ppermute | solution.py:33
  47.2 4.6 %collective-permute-start.6 = (f32[2,96,128]{2,1,0:T(8,128)S(1)}, f32[2,96,128]{2,1,0:T(8,128)S(1)}, u32[]{:S(2)}, u32[]{:S(2)}) collective-permute-start(f32[2,96,128]{2,1,0:T(8,128)S(1)} %get-tuple-element.65), channel_id=1, source_target_pairs={{0,2},{1,3},{2,0},{3,1},{4,6},{5,7},{6,4},{7,5},{8,10},{9,11},{10,... | collective-permute-start | bytes 294920 | tf_op jit(solution)/shard_map/ppermute | solution.py:33
  48.7 5.5 %collective-permute-start.7 = (f32[2,96,128]{2,1,0:T(8,128)S(1)}, f32[2,96,128]{2,1,0:T(8,128)S(1)}, u32[]{:S(2)}, u32[]{:S(2)}) collective-permute-start(f32[2,96,128]{2,1,0:T(8,128)S(1)} %get-tuple-element.66), channel_id=1, source_target_pairs={{0,3},{1,2},{2,1},{3,0},{4,7},{5,6},{6,5},{7,4},{8,11},{9,10},{10,... | collective-permute-start | bytes 294920 | tf_op jit(solution)/shard_map/ppermute | solution.py:33

commit v5 on v4

--- a/solution.py
+++ b/solution.py
@@ -180,34 +180,34 @@
 
 def store(sides, parts, ext, out=None):
     groups = len(sides)
-    count = groups * len(parts)
-    rows = parts[0][1][0].shape[1]
+    blocks = [block for _, part in parts for block in part.values()]
+    places = [(first, k) for first, part in parts for k in part]
+    used = sorted({k for _, k in places})
+    rows = blocks[0].shape[1]
 
     def kernel(*refs):
         out_ref, sems = refs[-2:]
         me = lax.axis_index("gy")
+        own = {k: (jnp.max(refs[n][0:1, 0:1]) > 0.5).astype(jnp.int32) * ext for n, k in enumerate(used)}
         copies = []
-        for k in range(groups):
-            own = (jnp.max(refs[k][...]) > 0.5).astype(jnp.int32) * ext
-            for n, (first, _) in enumerate(parts):
-                block = refs[groups + n * groups + k]
-                col = pl.multiple_of(own if first is None else ext - own + first, 128)
-                for c in range(2):
-                    dst = out_ref.at[c, me ^ k, :, pl.ds(col, block.shape[-1])]
-                    copy = pltpu.make_async_copy(block.at[c], dst, sems.at[2 * (n * groups + k) + c])
-                    copy.start()
-                    copies.append(copy)
+        for n, (first, k) in enumerate(places):
+            block = refs[len(used) + n]
+            col = pl.multiple_of(own[k] if first is None else ext - own[k] + first, 128)
+            for c in range(2):
+                dst = out_ref.at[c, me ^ k, :, pl.ds(col, block.shape[-1])]
+                copies.append(pltpu.make_async_copy(block.at[c], dst, sems.at[n, c]))
+                copies[-1].start()
         for copy in copies:
             copy.wait()
 
-    args = [*sides, *(b for _, blocks in parts for b in blocks)] + ([] if out is None else [out])
+    args = [*(sides[k] for k in used), *blocks] + ([] if out is None else [out])
     return call(
         kernel,
         out_shape=f32(2, groups, rows, 2 * ext),
-        in_specs=[VMEM] * (groups + count) + ([] if out is None else [HBM]),
+        in_specs=[VMEM] * (len(used) + len(blocks)) + ([] if out is None else [HBM]),
         out_specs=HBM,
-        scratch_shapes=[pltpu.SemaphoreType.DMA((2 * count,))],
-        input_output_aliases={} if out is None else {groups + count: 0},
+        scratch_shapes=[pltpu.SemaphoreType.DMA((len(blocks), 2))],
+        input_output_aliases={} if out is None else {len(used) + len(blocks): 0},
         compiler_params=limit(4),
     )(*args)
 
@@ -289,8 +289,11 @@
             compiler_params=limit(12),
         )(high, low, far_high, far_low, *part)
         parts.append((lo, exchange(blocks)))
-    out = store(sides, [(None, own), *parts[:-1]], ext)
-    out = store(sides, parts[-1:], ext, out)
+    parts = [(first, dict(enumerate(blocks))) for first, blocks in [(None, own), *parts]]
+    first, ahead = parts[-1]
+    behind = {k: ahead.pop(k) for k in range(1, groups)}
+    out = store(sides, parts, ext)
+    out = store(sides, [(first, behind)], ext, out)
     return out[None, None]
 
 

time: 55.3 us -> 55.2 us (level)
  no operation moved by 1% of the time
where the time goes in v5:
time: 55.2 us; the launch traced here: 55 us
  starting transfers between devices  23.9 us (43%)
  waiting for transfers between devices  20.8 us (38%)
  Pallas kernels  8.84 us (16%)
  between operations  0.77 us (1%)
  local copies, waits for them, and re-layouts  0.66 us (1%)
    ppermute x14, waiting for transfers between devices, permute(): lax.ppermute(x, axis, [(i, i ^ offset) for i in range(lax.axis_size(axis))])  20.8 us
    ppermute x14, starting transfers between devices, permute(): lax.ppermute(x, axis, [(i, i ^ offset) for i in range(lax.axis_size(axis))])  20.2 us
    pallas_call x8, Pallas kernels, run(): return pl.pallas_call(kernel, **options)(*args)  7.77 us
    ppermute x1, starting transfers between devices, on_device(): qse = [[early, lax.ppermute(piece, 'gx', last)]]  2.39 us
    ppermute x1, starting transfers between devices, on_device(): early = lax.ppermute(pieces[0], 'gx', first)  1.29 us
  transfers between devices with their start and end apart: 16, of which 7 were waited for; matrix products, arithmetic and copies ran while one was open for 0% of the time, Pallas kernels for 13%

profile of v5, /device:TPU:0, one launch (start us, length us, event | category | flops | bytes accessed | tf_op | source)
XLA Modules:
  0.0 55.0 jit_solution(15880889742921995395)
XLA Ops:
  0.0 0.0 copy-start
  0.0 1.1 %shard_map.38 = f32[2,128,128]{2,1,0:T(8,128)S(1)} custom-call(f32[2,512,512]{2,1,0:T(8,128)} %bitcast.4), custom_call_target="tpu_custom_call" | custom-call | tf_op jit(solution)/shard_map/pallas_call | solution.py:224
  1.1 4.1 %collective-permute-start = (f32[2,128,128]{2,1,0:T(8,128)S(1)}, f32[2,128,128]{2,1,0:T(8,128)S(1)}, u32[]{:S(2)}, u32[]{:S(2)}) collective-permute-start(f32[2,128,128]{2,1,0:T(8,128)S(1)} %shard_map.38), channel_id=1, source_target_pairs={{0,16},{4,20},{8,24},{12,28},{16,0},{20,4},{24,8},{28,12},{1,17},{... | collective-permute-start | bytes 393224 | tf_op jit(solution)/shard_map/ppermute | solution.py:33
  5.2 0.0 copy-done
  5.2 0.0 copy-start.1
  5.2 0.7 %copy-done.1 = s32[1,1,4]{2,1,0:T(1,128)S(1)} copy-done((s32[1,1,4]{2,1,0:T(1,128)S(1)}, s32[1,1,4]{2,1,0:T(1,128)}, u32[]{:S(2)}) %copy-start.1) | copy-done | bytes 40
  5.9 1.2 %shard_map.37 = (f32[2,128,256]{2,1,0:T(8,128)S(1)}, f32[2,128,128]{2,1,0:T(8,128)S(1)}, f32[2,384,384]{2,1,0:T(8,128)S(1)}, f32[384,256]{1,0:T(8,128)S(1)}, bf1...) custom-call(s32[4]{0:T(128)S(1)} %bitcast.6, ...), custom_call_target="tpu_custom_call" | custom-call | tf_op jit(solution)/shard_map/pallas_call | solution.py:45
  7.1 1.3 %collective-permute-start.11 = (f32[2,128,256]{2,1,0:T(8,128)S(1)}, f32[2,128,256]{2,1,0:T(8,128)S(1)}, u32[]{:S(2)}, u32[]{:S(2)}) collective-permute-start(f32[2,128,256]{2,1,0:T(8,128)S(1)} %get-tuple-element.69), channel_id=1, source_target_pairs={{8,24},{12,28},{16,0},{20,4},{9,25},{13,29},{17,1},{21,5},{10,26},... | collective-permute-start | bytes 786440 | tf_op jit(solution)/shard_map/ppermute | solution.py:247
  8.4 3.1 %collective-permute-done.qss_ref = f32[2,128,128]{2,1,0:T(8,128)S(1)} collective-permute-done((f32[2,128,128]{2,1,0:T(8,128)S(1)}, f32[2,128,128]{2,1,0:T(8,128)S(1)}, u32[]{:S(2)}, u32[]{:S(2)}) %collective-permute-start) | collective-permute-done | bytes 131104 | tf_op jit(solution)/shard_map/ppermute | solution.py:33
  11.5 1.6 %shard_map.39 = (bf16[4,128,256]{2,1,0:T(8,128)(2,1)S(1)}, bf16[4,128,256]{2,1,0:T(8,128)(2,1)S(1)}, bf16[128,768]{1,0:T(8,128)(2,1)S(1)}, bf16[128,768]{1,0:T(8...) custom-call(f32[2,128,128]{2,1,0:T(8,128)S(1)} %collective-permute-done.qss_ref,, ...), custom_call_target="tpu_custom_call" | custom-call | tf_op jit(solution)/shard_map/pallas_call | solution.py:45
  13.1 2.4 %collective-permute-start.12 = (f32[2,128,256]{2,1,0:T(8,128)S(1)}, f32[2,128,256]{2,1,0:T(8,128)S(1)}, u32[]{:S(2)}, u32[]{:S(2)}) collective-permute-start(f32[2,128,256]{2,1,0:T(8,128)S(1)} %get-tuple-element.69), channel_id=1, source_target_pairs={{0,16},{4,20},{24,8},{28,12},{1,17},{5,21},{25,9},{29,13},{2,18},{... | collective-permute-start | bytes 786440 | tf_op jit(solution)/shard_map/ppermute | solution.py:259
  15.5 1.5 %shard_map.40 = (bf16[288,256]{1,0:T(8,128)(2,1)S(1)}, bf16[288,256]{1,0:T(8,128)(2,1)S(1)}, f32[2,96,384]{2,1,0:T(8,128)S(1)}, f32[2,96,384]{2,1,0:T(8,128)S(1)}) custom-call(f32[2,384,384]{2,1,0:T(8,128)S(1)} %get-tuple-element.40.base_ref, f32[384,256]{1,0:T(8,128)S(1)} %get-tuple-element.41.res_ref, bf16[384,256]{1,0:T(8,128)(2,1)S(1)} %get-tuple-element.42.res_high, ...), custom_call_target="tpu_custom_call" | custom-call | tf_op jit(solution)/shard_map/pallas_call | solution.py:45
  17.1 1.6 %collective-permute-start.8 = (f32[2,96,384]{2,1,0:T(8,128)S(1)}, f32[2,96,384]{2,1,0:T(8,128)S(1)}, u32[]{:S(2)}, u32[]{:S(2)}) collective-permute-start(f32[2,96,384]{2,1,0:T(8,128)S(1)} %get-tuple-element.66), channel_id=1, source_target_pairs={{0,1},{1,0},{2,3},{3,2},{4,5},{5,4},{6,7},{7,6},{8,9},{9,8},{10,11... | collective-permute-start | bytes 884744 | tf_op jit(solution)/shard_map/ppermute | solution.py:33
  19.3 1.6 %collective-permute-start.3 = (f32[8,128]{1,0:T(8,128)S(1)}, f32[8,128]{1,0:T(8,128)S(1)}, u32[]{:S(2)}, u32[]{:S(2)}) collective-permute-start(f32[8,128]{1,0:T(8,128)S(1)} %broadcast_in_dim.6.refs_0_), channel_id=1, source_target_pairs={{0,3},{1,2},{2,1},{3,0},{4,7},{5,6},{6,5},{7,4},{8,11},{9,10},{10,... | collective-permute-start | bytes 12296 | tf_op jit(solution)/shard_map/ppermute | solution.py:33
  20.9 0.5 collective-permute-start.2
  21.4 4.7 %collective-permute-done.3.refs_3_.refs_2_ = f32[8,128]{1,0:T(8,128)S(1)} collective-permute-done((f32[8,128]{1,0:T(8,128)S(1)}, f32[8,128]{1,0:T(8,128)S(1)}, u32[]{:S(2)}, u32[]{:S(2)}) %collective-permute-start.3) | collective-permute-done | bytes 4128 | tf_op jit(solution)/shard_map/ppermute | solution.py:33
  26.1 0.5 collective-permute-start.9
  26.6 0.0 collective-permute-done.2.refs_2_.refs_1_
  26.6 2.4 %collective-permute-start.10 = (f32[2,96,384]{2,1,0:T(8,128)S(1)}, f32[2,96,384]{2,1,0:T(8,128)S(1)}, u32[]{:S(2)}, u32[]{:S(2)}) collective-permute-start(f32[2,96,384]{2,1,0:T(8,128)S(1)} %get-tuple-element.68), channel_id=1, source_target_pairs={{0,3},{1,2},{2,1},{3,0},{4,7},{5,6},{6,5},{7,4},{8,11},{9,10},{10,... | collective-permute-start | bytes 884744 | tf_op jit(solution)/shard_map/ppermute | solution.py:33
  29.1 0.0 collective-permute-done.11.refs_0_
  29.1 0.0 collective-permute-start.4
  29.1 0.0 collective-permute-done.12.refs_1_
  29.1 0.6 %collective-permute-start.1 = (f32[8,128]{1,0:T(8,128)S(1)}, f32[8,128]{1,0:T(8,128)S(1)}, u32[]{:S(2)}, u32[]{:S(2)}) collective-permute-start(f32[8,128]{1,0:T(8,128)S(1)} %broadcast_in_dim.6.refs_0_), channel_id=1, source_target_pairs={{0,1},{1,0},{2,3},{3,2},{4,5},{5,4},{6,7},{7,6},{8,9},{9,8},{10,11... | collective-permute-start | bytes 12296 | tf_op jit(solution)/shard_map/ppermute | solution.py:33
  29.7 0.5 shard_map.43
  30.2 4.8 %collective-permute-done.1.refs_1_.refs_0_ = f32[8,128]{1,0:T(8,128)S(1)} collective-permute-done((f32[8,128]{1,0:T(8,128)S(1)}, f32[8,128]{1,0:T(8,128)S(1)}, u32[]{:S(2)}, u32[]{:S(2)}) %collective-permute-start.1) | collective-permute-done | bytes 4128 | tf_op jit(solution)/shard_map/ppermute | solution.py:33
  35.0 1.5 %collective-permute-start.13 = (f32[2,96,256]{2,1,0:T(8,128)S(1)}, f32[2,96,256]{2,1,0:T(8,128)S(1)}, u32[]{:S(2)}, u32[]{:S(2)}) collective-permute-start(f32[2,96,256]{2,1,0:T(8,128)S(1)} %get-tuple-element.71), channel_id=1, source_target_pairs={{0,1},{1,0},{2,3},{3,2},{4,5},{5,4},{6,7},{7,6},{8,9},{9,8},{10,11... | collective-permute-start | bytes 589832 | tf_op jit(solution)/shard_map/ppermute | solution.py:33
  36.5 0.0 collective-permute-done.4.refs_0_
  36.5 0.8 %collective-permute-start.14 = (f32[2,96,256]{2,1,0:T(8,128)S(1)}, f32[2,96,256]{2,1,0:T(8,128)S(1)}, u32[]{:S(2)}, u32[]{:S(2)}) collective-permute-start(f32[2,96,256]{2,1,0:T(8,128)S(1)} %get-tuple-element.72), channel_id=1, source_target_pairs={{0,2},{1,3},{2,0},{3,1},{4,6},{5,7},{6,4},{7,5},{8,10},{9,11},{10,... | collective-permute-start | bytes 589832 | tf_op jit(solution)/shard_map/ppermute | solution.py:33
  37.3 0.0 collective-permute-done.8.refs_5_
  37.3 1.2 %collective-permute-start.15 = (f32[2,96,256]{2,1,0:T(8,128)S(1)}, f32[2,96,256]{2,1,0:T(8,128)S(1)}, u32[]{:S(2)}, u32[]{:S(2)}) collective-permute-start(f32[2,96,256]{2,1,0:T(8,128)S(1)} %get-tuple-element.73), channel_id=1, source_target_pairs={{0,3},{1,2},{2,1},{3,0},{4,7},{5,6},{6,5},{7,4},{8,11},{9,10},{10,... | collective-permute-start | bytes 589832 | tf_op jit(solution)/shard_map/ppermute | solution.py:33
  38.5 0.3 shard_map.41
  38.8 4.5 %collective-permute-done.9.refs_6_ = f32[2,96,384]{2,1,0:T(8,128)S(1)} collective-permute-done((f32[2,96,384]{2,1,0:T(8,128)S(1)}, f32[2,96,384]{2,1,0:T(8,128)S(1)}, u32[]{:S(2)}, u32[]{:S(2)}) %collective-permute-start.9) | collective-permute-done | bytes 294944 | tf_op jit(solution)/shard_map/ppermute | solution.py:33
  43.3 3.9 %collective-permute-start.5 = (f32[2,96,128]{2,1,0:T(8,128)S(1)}, f32[2,96,128]{2,1,0:T(8,128)S(1)}, u32[]{:S(2)}, u32[]{:S(2)}) collective-permute-start(f32[2,96,128]{2,1,0:T(8,128)S(1)} %get-tuple-element.63), channel_id=1, source_target_pairs={{0,1},{1,0},{2,3},{3,2},{4,5},{5,4},{6,7},{7,6},{8,9},{9,8},{10,11... | collective-permute-start | bytes 294920 | tf_op jit(solution)/shard_map/ppermute | solution.py:33
  47.2 0.0 collective-permute-done.10.refs_7_
  47.2 1.5 %collective-permute-start.6 = (f32[2,96,128]{2,1,0:T(8,128)S(1)}, f32[2,96,128]{2,1,0:T(8,128)S(1)}, u32[]{:S(2)}, u32[]{:S(2)}) collective-permute-start(f32[2,96,128]{2,1,0:T(8,128)S(1)} %get-tuple-element.64), channel_id=1, source_target_pairs={{0,2},{1,3},{2,0},{3,1},{4,6},{5,7},{6,4},{7,5},{8,10},{9,11},{10,... | collective-permute-start | bytes 294920 | tf_op jit(solution)/shard_map/ppermute | solution.py:33
  48.7 0.0 collective-permute-done.13.refs_9_
  48.7 0.0 collective-permute-start.7
  48.7 0.3 shard_map.42.refs_4_
  49.0 0.7 %collective-permute-done.14.refs_10_ = f32[2,96,256]{2,1,0:T(8,128)S(1)} collective-permute-done((f32[2,96,256]{2,1,0:T(8,128)S(1)}, f32[2,96,256]{2,1,0:T(8,128)S(1)}, u32[]{:S(2)}, u32[]{:S(2)}) %collective-permute-start.14) | collective-permute-done | bytes 196640 | tf_op jit(solution)/shard_map/ppermute | solution.py:33
  49.7 0.0 collective-permute-done.15.refs_11_
  49.7 1.5 %shard_map.44.refs_6_ = f32[2,4,96,768]{3,2,1,0:T(8,128)} custom-call(f32[8,128]{1,0:T(8,128)S(1)} %broadcast_in_dim.6.refs_0_, f32[8,128]{1,0:T(8,128)S(1)} %collective-permute-done.1.refs_1_.refs_0_, f32[8,128]{1,0:T(8,128)S(1)} %collective-permute-done.2.refs_2_.refs_1_, f32[8,128]{1,0:T(8,128)S(1)} %collective-permute-done.3.refs_3_.refs_2_, ...), custom_call_target="tpu_custom_call" | custom-call | tf_op jit(solution)/shard_map/pallas_call | solution.py:45
  51.2 0.0 collective-permute-done.5.refs_3_
  51.2 0.6 %collective-permute-done.6.refs_4_ = f32[2,96,128]{2,1,0:T(8,128)S(1)} collective-permute-done((f32[2,96,128]{2,1,0:T(8,128)S(1)}, f32[2,96,128]{2,1,0:T(8,128)S(1)}, u32[]{:S(2)}, u32[]{:S(2)}) %collective-permute-start.6) | collective-permute-done | bytes 98336 | tf_op jit(solution)/shard_map/ppermute | solution.py:33
  51.8 2.4 %collective-permute-done.7.refs_5_ = f32[2,96,128]{2,1,0:T(8,128)S(1)} collective-permute-done((f32[2,96,128]{2,1,0:T(8,128)S(1)}, f32[2,96,128]{2,1,0:T(8,128)S(1)}, u32[]{:S(2)}, u32[]{:S(2)}) %collective-permute-start.7) | collective-permute-done | bytes 98336 | tf_op jit(solution)/shard_map/ppermute | solution.py:33
  54.2 0.8 %shard_map.45 = f32[2,4,96,768]{3,2,1,0:T(8,128)} custom-call(f32[8,128]{1,0:T(8,128)S(1)} %collective-permute-done.1.refs_1_.refs_0_, f32[8,128]{1,0:T(8,128)S(1)} %collective-permute-done.2.refs_2_.refs_1_, f32[8,128]{1,0:T(8,128)S(1)} %collective-permute-done.3.refs_3_.refs_2_, ...), custom_call_target="tpu_custom_call", output_to_operand_aliasing={{}: (6, {})} | custom-call | tf_op jit(solution)/shard_map/pallas_call | solution.py:45
  (1 shorter events, 0.0 us)
Async XLA Ops:
  0.0 5.2 %copy-start = (f32[1,1,2,512,512]{4,3,2,1,0:T(8,128)S(1)}, f32[1,1,2,512,512]{4,3,2,1,0:T(8,128)}, u32[]{:S(2)}) copy-start(f32[1,1,2,512,512]{4,3,2,1,0:T(8,128)} %param.3) | copy-start | bytes 6291460
  1.1 10.4 %collective-permute-start = (f32[2,128,128]{2,1,0:T(8,128)S(1)}, f32[2,128,128]{2,1,0:T(8,128)S(1)}, u32[]{:S(2)}, u32[]{:S(2)}) collective-permute-start(f32[2,128,128]{2,1,0:T(8,128)S(1)} %shard_map.38), channel_id=1, source_target_pairs={{0,16},{4,20},{8,24},{12,28},{16,0},{20,4},{24,8},{28,12},{1,17},{... | collective-permute-start | bytes 393224 | tf_op jit(solution)/shard_map/ppermute | solution.py:33
  5.2 0.7 %copy-start.1 = (s32[1,1,4]{2,1,0:T(1,128)S(1)}, s32[1,1,4]{2,1,0:T(1,128)}, u32[]{:S(2)}) copy-start(s32[1,1,4]{2,1,0:T(1,128)} %param.5) | copy-start | bytes 52
  7.1 21.9 %collective-permute-start.11 = (f32[2,128,256]{2,1,0:T(8,128)S(1)}, f32[2,128,256]{2,1,0:T(8,128)S(1)}, u32[]{:S(2)}, u32[]{:S(2)}) collective-permute-start(f32[2,128,256]{2,1,0:T(8,128)S(1)} %get-tuple-element.69), channel_id=1, source_target_pairs={{8,24},{12,28},{16,0},{20,4},{9,25},{13,29},{17,1},{21,5},{10,26},... | collective-permute-start | bytes 786440 | tf_op jit(solution)/shard_map/ppermute | solution.py:247
  13.1 15.9 %collective-permute-start.12 = (f32[2,128,256]{2,1,0:T(8,128)S(1)}, f32[2,128,256]{2,1,0:T(8,128)S(1)}, u32[]{:S(2)}, u32[]{:S(2)}) collective-permute-start(f32[2,128,256]{2,1,0:T(8,128)S(1)} %get-tuple-element.69), channel_id=1, source_target_pairs={{0,16},{4,20},{24,8},{28,12},{1,17},{5,21},{25,9},{29,13},{2,18},{... | collective-permute-start | bytes 786440 | tf_op jit(solution)/shard_map/ppermute | solution.py:259
  17.1 20.2 %collective-permute-start.8 = (f32[2,96,384]{2,1,0:T(8,128)S(1)}, f32[2,96,384]{2,1,0:T(8,128)S(1)}, u32[]{:S(2)}, u32[]{:S(2)}) collective-permute-start(f32[2,96,384]{2,1,0:T(8,128)S(1)} %get-tuple-element.66), channel_id=1, source_target_pairs={{0,1},{1,0},{2,3},{3,2},{4,5},{5,4},{6,7},{7,6},{8,9},{9,8},{10,11... | collective-permute-start | bytes 884744 | tf_op jit(solution)/shard_map/ppermute | solution.py:33
  19.3 6.8 %collective-permute-start.3 = (f32[8,128]{1,0:T(8,128)S(1)}, f32[8,128]{1,0:T(8,128)S(1)}, u32[]{:S(2)}, u32[]{:S(2)}) collective-permute-start(f32[8,128]{1,0:T(8,128)S(1)} %broadcast_in_dim.6.refs_0_), channel_id=1, source_target_pairs={{0,3},{1,2},{2,1},{3,0},{4,7},{5,6},{6,5},{7,4},{8,11},{9,10},{10,... | collective-permute-start | bytes 12296 | tf_op jit(solution)/shard_map/ppermute | solution.py:33
  20.9 5.8 %collective-permute-start.2 = (f32[8,128]{1,0:T(8,128)S(1)}, f32[8,128]{1,0:T(8,128)S(1)}, u32[]{:S(2)}, u32[]{:S(2)}) collective-permute-start(f32[8,128]{1,0:T(8,128)S(1)} %broadcast_in_dim.6.refs_0_), channel_id=1, source_target_pairs={{0,2},{1,3},{2,0},{3,1},{4,6},{5,7},{6,4},{7,5},{8,10},{9,11},{10,... | collective-permute-start | bytes 12296 | tf_op jit(solution)/shard_map/ppermute | solution.py:33
  26.1 17.2 %collective-permute-start.9 = (f32[2,96,384]{2,1,0:T(8,128)S(1)}, f32[2,96,384]{2,1,0:T(8,128)S(1)}, u32[]{:S(2)}, u32[]{:S(2)}) collective-permute-start(f32[2,96,384]{2,1,0:T(8,128)S(1)} %get-tuple-element.67), channel_id=1, source_target_pairs={{0,2},{1,3},{2,0},{3,1},{4,6},{5,7},{6,4},{7,5},{8,10},{9,11},{10,... | collective-permute-start | bytes 884744 | tf_op jit(solution)/shard_map/ppermute | solution.py:33
  26.6 20.6 %collective-permute-start.10 = (f32[2,96,384]{2,1,0:T(8,128)S(1)}, f32[2,96,384]{2,1,0:T(8,128)S(1)}, u32[]{:S(2)}, u32[]{:S(2)}) collective-permute-start(f32[2,96,384]{2,1,0:T(8,128)S(1)} %get-tuple-element.68), channel_id=1, source_target_pairs={{0,3},{1,2},{2,1},{3,0},{4,7},{5,6},{6,5},{7,4},{8,11},{9,10},{10,... | collective-permute-start | bytes 884744 | tf_op jit(solution)/shard_map/ppermute | solution.py:33
  29.1 7.4 %collective-permute-start.4 = (f32[2,128,128]{2,1,0:T(8,128)S(1)}, f32[2,128,128]{2,1,0:T(8,128)S(1)}, u32[]{:S(2)}, u32[]{:S(2)}) collective-permute-start(f32[2,128,128]{2,1,0:T(8,128)S(1)} %get-tuple-element.62), channel_id=1, source_target_pairs={{0,16},{4,20},{8,24},{12,28},{16,0},{20,4},{24,8},{28,12},{1,17},{... | collective-permute-start | bytes 393224 | tf_op jit(solution)/shard_map/ppermute | solution.py:33
  29.1 5.9 %collective-permute-start.1 = (f32[8,128]{1,0:T(8,128)S(1)}, f32[8,128]{1,0:T(8,128)S(1)}, u32[]{:S(2)}, u32[]{:S(2)}) collective-permute-start(f32[8,128]{1,0:T(8,128)S(1)} %broadcast_in_dim.6.refs_0_), channel_id=1, source_target_pairs={{0,1},{1,0},{2,3},{3,2},{4,5},{5,4},{6,7},{7,6},{8,9},{9,8},{10,11... | collective-permute-start | bytes 12296 | tf_op jit(solution)/shard_map/ppermute | solution.py:33
  35.0 13.7 %collective-permute-start.13 = (f32[2,96,256]{2,1,0:T(8,128)S(1)}, f32[2,96,256]{2,1,0:T(8,128)S(1)}, u32[]{:S(2)}, u32[]{:S(2)}) collective-permute-start(f32[2,96,256]{2,1,0:T(8,128)S(1)} %get-tuple-element.71), channel_id=1, source_target_pairs={{0,1},{1,0},{2,3},{3,2},{4,5},{5,4},{6,7},{7,6},{8,9},{9,8},{10,11... | collective-permute-start | bytes 589832 | tf_op jit(solution)/shard_map/ppermute | solution.py:33
  36.5 13.2 %collective-permute-start.14 = (f32[2,96,256]{2,1,0:T(8,128)S(1)}, f32[2,96,256]{2,1,0:T(8,128)S(1)}, u32[]{:S(2)}, u32[]{:S(2)}) collective-permute-start(f32[2,96,256]{2,1,0:T(8,128)S(1)} %get-tuple-element.72), channel_id=1, source_target_pairs={{0,2},{1,3},{2,0},{3,1},{4,6},{5,7},{6,4},{7,5},{8,10},{9,11},{10,... | collective-permute-start | bytes 589832 | tf_op jit(solution)/shard_map/ppermute | solution.py:33
  37.3 12.4 %collective-permute-start.15 = (f32[2,96,256]{2,1,0:T(8,128)S(1)}, f32[2,96,256]{2,1,0:T(8,128)S(1)}, u32[]{:S(2)}, u32[]{:S(2)}) collective-permute-start(f32[2,96,256]{2,1,0:T(8,128)S(1)} %get-tuple-element.73), channel_id=1, source_target_pairs={{0,3},{1,2},{2,1},{3,0},{4,7},{5,6},{6,5},{7,4},{8,11},{9,10},{10,... | collective-permute-start | bytes 589832 | tf_op jit(solution)/shard_map/ppermute | solution.py:33
  43.3 7.9 %collective-permute-start.5 = (f32[2,96,128]{2,1,0:T(8,128)S(1)}, f32[2,96,128]{2,1,0:T(8,128)S(1)}, u32[]{:S(2)}, u32[]{:S(2)}) collective-permute-start(f32[2,96,128]{2,1,0:T(8,128)S(1)} %get-tuple-element.63), channel_id=1, source_target_pairs={{0,1},{1,0},{2,3},{3,2},{4,5},{5,4},{6,7},{7,6},{8,9},{9,8},{10,11... | collective-permute-start | bytes 294920 | tf_op jit(solution)/shard_map/ppermute | solution.py:33
  47.2 4.6 %collective-permute-start.6 = (f32[2,96,128]{2,1,0:T(8,128)S(1)}, f32[2,96,128]{2,1,0:T(8,128)S(1)}, u32[]{:S(2)}, u32[]{:S(2)}) collective-permute-start(f32[2,96,128]{2,1,0:T(8,128)S(1)} %get-tuple-element.64), channel_id=1, source_target_pairs={{0,2},{1,3},{2,0},{3,1},{4,6},{5,7},{6,4},{7,5},{8,10},{9,11},{10,... | collective-permute-start | bytes 294920 | tf_op jit(solution)/shard_map/ppermute | solution.py:33
  48.7 5.5 %collective-permute-start.7 = (f32[2,96,128]{2,1,0:T(8,128)S(1)}, f32[2,96,128]{2,1,0:T(8,128)S(1)}, u32[]{:S(2)}, u32[]{:S(2)}) collective-permute-start(f32[2,96,128]{2,1,0:T(8,128)S(1)} %get-tuple-element.65), channel_id=1, source_target_pairs={{0,3},{1,2},{2,1},{3,0},{4,7},{5,6},{6,5},{7,4},{8,11},{9,10},{10,... | collective-permute-start | bytes 294920 | tf_op jit(solution)/shard_map/ppermute | solution.py:33

commit v6 on v5

--- a/solution.py
+++ b/solution.py
@@ -12,6 +12,7 @@
 SWEEPS = 15
 LEVELS = (SWEEPS + 1).bit_length() - 1
 PIECES = 2
+CUTS = 4
 VMEM = pl.BlockSpec(memory_space=pltpu.VMEM)
 SMEM = pl.BlockSpec(memory_space=pltpu.SMEM)
 HBM = pl.BlockSpec(memory_space=pltpu.MemorySpace.HBM)
@@ -52,8 +53,10 @@
     return high, (x - high.astype(jnp.float32)).astype(jnp.bfloat16)
 
 
+dot = functools.partial(jnp.dot, preferred_element_type=jnp.float32)
+
+
 def matmul(left, right):
-    dot = functools.partial(jnp.dot, preferred_element_type=jnp.float32)
     rows = left[0].shape[0]
     both = dot(jnp.concatenate(left, axis=0), right[0])
     return both[:rows] + (both[rows:] + dot(left[0], right[1]))
@@ -79,10 +82,17 @@
     return index
 
 
-def corner_kernel(ext, iti_ref, out_ref, sem):
-    copy = pltpu.make_async_copy(iti_ref.at[:, ext:, ext:], out_ref, sem)
-    copy.start()
-    copy.wait()
+def corner_kernel(ext, iti_ref, out_ref, sems):
+    step = out_ref.shape[1] // CUTS
+    copies = []
+    for c in range(2):
+        for n in range(CUTS):
+            rows = pl.ds(n * step, step)
+            src = iti_ref.at[c, pl.ds(ext + n * step, step), ext:]
+            copies.append(pltpu.make_async_copy(src, out_ref.at[c, rows, :], sems.at[c, n]))
+            copies[-1].start()
+    for copy in copies:
+        copy.wait()
 
 
 def prepare_kernel(edge, ext, groups, cuts, owner_ref, iti_ref, *refs):
@@ -128,9 +138,12 @@
     for level in range(LEVELS):
         pow_high[level], pow_low[level] = power
         if level + 1 < LEVELS:
-            both = times([jnp.concatenate(pair, axis=0) for pair in zip(power, left)], power)
-            power = halves(both[:edge])
-            total = total + both[edge:]
+            right = [expand(x) for x in power]
+            high = dot(jnp.concatenate([*power, *left], axis=0), right[0])
+            low = dot(jnp.concatenate([power[0], left[0]], axis=0), right[1])
+            power = halves(high[:edge] + (high[edge : 2 * edge] + low[:edge]))
+            high = high[2 * edge :]
+            total = total + (high[:rows] + (high[rows:] + low[edge:]))
         else:
             total = total + times(left, power)
         left = halves(total)
@@ -226,7 +239,7 @@
         out_shape=f32(2, edge, edge),
         in_specs=[HBM],
         out_specs=VMEM,
-        scratch_shapes=[pltpu.SemaphoreType.DMA],
+        scratch_shapes=[pltpu.SemaphoreType.DMA((2, CUTS))],
         compiler_params=limit(52),
     )(ownmap)
     qss = permute(corner, "gx", across)
@@ -239,7 +252,7 @@
         in_specs=[SMEM, HBM],
         out_specs=[VMEM] * (8 + len(cuts)),
         scratch_shapes=[pltpu.VMEM((2, edge, 4 * edge), jnp.float32), pltpu.SemaphoreType.DMA((1 + 4 * groups + len(cuts),))],
-        compiler_params=limit(12),
+        compiler_params=limit(50),
     )(owner[0, 0], ownmap)
     inner = [i for i in range(2 * across) if (i // across ^ i // (across // 2)) & 1]
     first = [(i, i ^ across) for i in inner]
@@ -253,7 +266,7 @@
         + [f32(2, rows_each, ext)],
         in_specs=[VMEM] * 9,
         out_specs=[VMEM] * 7,
-        compiler_params=limit(16),
+        compiler_params=pltpu.CompilerParams(vmem_limit_bytes=16 << 20),
     )(qss, base, res, res_high, res_low, rss_high, rss_low, rse_high, rse_low)
     piece, far_high = lax.optimization_barrier((pieces[0], far_high))
     qse = [[early, lax.ppermute(piece, "gx", last)]]

time: 55.2 us -> 56.2 us (1.018)
  starting transfers between devices: 23.9 us -> 25 us
  waiting for transfers between devices: 20.8 us -> 19.7 us
  Pallas kernels: 8.84 us -> 9.79 us
    ppermute x14, waiting for transfers between devices: 20.8 us -> 19.7 us  [permute(): lax.ppermute(x, axis, [(i, i ^ offset) for i in range(lax.axis_size(axis))])]
    pallas_call x8, Pallas kernels: 7.77 us -> 8.88 us  [run(): return pl.pallas_call(kernel, **options)(*args)]
    ppermute x1, starting transfers between devices: 2.39 us -> 3.49 us  [on_device(): qse = [[early, lax.ppermute(piece, 'gx', last)]]]
  transfers between devices with their start and end apart: 16 -> 16, of which waited for: 7 -> 7; matrix products, arithmetic and copies ran while one was open for 0% -> 0% of each run, Pallas kernels for 13% -> 14%
where the time goes in v6:
time: 56.2 us; the launch traced here: 55.9 us
  starting transfers between devices  25 us (44%)
  waiting for transfers between devices  19.7 us (35%)
  Pallas kernels  9.79 us (17%)
  between operations  0.77 us (1%)
  local copies, waits for them, and re-layouts  0.66 us (1%)
    ppermute x14, starting transfers between devices, permute(): lax.ppermute(x, axis, [(i, i ^ offset) for i in range(lax.axis_size(axis))])  20.2 us
    ppermute x14, waiting for transfers between devices, permute(): lax.ppermute(x, axis, [(i, i ^ offset) for i in range(lax.axis_size(axis))])  19.7 us
    pallas_call x8, Pallas kernels, run(): return pl.pallas_call(kernel, **options)(*args)  8.88 us
    ppermute x1, starting transfers between devices, on_device(): qse = [[early, lax.ppermute(piece, 'gx', last)]]  3.49 us
    ppermute x1, starting transfers between devices, on_device(): early = lax.ppermute(pieces[0], 'gx', first)  1.29 us
  transfers between devices with their start and end apart: 16, of which 7 were waited for; matrix products, arithmetic and copies ran while one was open for 0% of the time, Pallas kernels for 14%

profile of v6, /device:TPU:0, one launch (start us, length us, event | category | flops | bytes accessed | tf_op | source)
XLA Modules:
  0.0 55.9 jit_solution(18107730472844204890)
XLA Ops:
  0.0 0.9 %shard_map.38 = f32[2,128,128]{2,1,0:T(8,128)S(1)} custom-call(f32[2,512,512]{2,1,0:T(8,128)} %bitcast.5), custom_call_target="tpu_custom_call" | custom-call | tf_op jit(solution)/shard_map/pallas_call | solution.py:237
  0.9 4.1 %collective-permute-start = (f32[2,128,128]{2,1,0:T(8,128)S(1)}, f32[2,128,128]{2,1,0:T(8,128)S(1)}, u32[]{:S(2)}, u32[]{:S(2)}) collective-permute-start(f32[2,128,128]{2,1,0:T(8,128)S(1)} %shard_map.38), channel_id=1, source_target_pairs={{0,16},{4,20},{8,24},{12,28},{16,0},{20,4},{24,8},{28,12},{1,17},{... | collective-permute-start | bytes 393224 | tf_op jit(solution)/shard_map/ppermute | solution.py:34
  5.0 0.0 copy-start
  5.0 0.7 %copy-done = s32[1,1,4]{2,1,0:T(1,128)S(1)} copy-done((s32[1,1,4]{2,1,0:T(1,128)S(1)}, s32[1,1,4]{2,1,0:T(1,128)}, u32[]{:S(2)}) %copy-start) | copy-done | bytes 40
  5.7 2.3 %shard_map.37 = (f32[2,128,256]{2,1,0:T(8,128)S(1)}, f32[2,128,128]{2,1,0:T(8,128)S(1)}, f32[2,384,384]{2,1,0:T(8,128)S(1)}, f32[384,256]{1,0:T(8,128)S(1)}, bf1...) custom-call(s32[4]{0:T(128)S(1)} %bitcast.4, ...), custom_call_target="tpu_custom_call" | custom-call | tf_op jit(solution)/shard_map/pallas_call | solution.py:46
  8.1 1.3 %collective-permute-start.11 = (f32[2,128,256]{2,1,0:T(8,128)S(1)}, f32[2,128,256]{2,1,0:T(8,128)S(1)}, u32[]{:S(2)}, u32[]{:S(2)}) collective-permute-start(f32[2,128,256]{2,1,0:T(8,128)S(1)} %get-tuple-element.69), channel_id=1, source_target_pairs={{8,24},{12,28},{16,0},{20,4},{9,25},{13,29},{17,1},{21,5},{10,26},... | collective-permute-start | bytes 786440 | tf_op jit(solution)/shard_map/ppermute | solution.py:260
  9.4 2.0 %collective-permute-done.qss_ref = f32[2,128,128]{2,1,0:T(8,128)S(1)} collective-permute-done((f32[2,128,128]{2,1,0:T(8,128)S(1)}, f32[2,128,128]{2,1,0:T(8,128)S(1)}, u32[]{:S(2)}, u32[]{:S(2)}) %collective-permute-start) | collective-permute-done | bytes 131104 | tf_op jit(solution)/shard_map/ppermute | solution.py:34
  11.3 1.6 %shard_map.39 = (bf16[4,128,256]{2,1,0:T(8,128)(2,1)S(1)}, bf16[4,128,256]{2,1,0:T(8,128)(2,1)S(1)}, bf16[128,768]{1,0:T(8,128)(2,1)S(1)}, bf16[128,768]{1,0:T(8...) custom-call(f32[2,128,128]{2,1,0:T(8,128)S(1)} %collective-permute-done.qss_ref,, ...), custom_call_target="tpu_custom_call" | custom-call | tf_op jit(solution)/shard_map/pallas_call | solution.py:46
  13.0 3.5 %collective-permute-start.12 = (f32[2,128,256]{2,1,0:T(8,128)S(1)}, f32[2,128,256]{2,1,0:T(8,128)S(1)}, u32[]{:S(2)}, u32[]{:S(2)}) collective-permute-start(f32[2,128,256]{2,1,0:T(8,128)S(1)} %get-tuple-element.69), channel_id=1, source_target_pairs={{0,16},{4,20},{24,8},{28,12},{1,17},{5,21},{25,9},{29,13},{2,18},{... | collective-permute-start | bytes 786440 | tf_op jit(solution)/shard_map/ppermute | solution.py:272
  16.5 1.5 %shard_map.40 = (bf16[288,256]{1,0:T(8,128)(2,1)S(1)}, bf16[288,256]{1,0:T(8,128)(2,1)S(1)}, f32[2,96,384]{2,1,0:T(8,128)S(1)}, f32[2,96,384]{2,1,0:T(8,128)S(1)}) custom-call(f32[2,384,384]{2,1,0:T(8,128)S(1)} %get-tuple-element.40.base_ref, f32[384,256]{1,0:T(8,128)S(1)} %get-tuple-element.41.res_ref, bf16[384,256]{1,0:T(8,128)(2,1)S(1)} %get-tuple-element.42.res_high, ...), custom_call_target="tpu_custom_call" | custom-call | tf_op jit(solution)/shard_map/pallas_call | solution.py:46
  18.0 1.6 %collective-permute-start.8 = (f32[2,96,384]{2,1,0:T(8,128)S(1)}, f32[2,96,384]{2,1,0:T(8,128)S(1)}, u32[]{:S(2)}, u32[]{:S(2)}) collective-permute-start(f32[2,96,384]{2,1,0:T(8,128)S(1)} %get-tuple-element.66), channel_id=1, source_target_pairs={{0,1},{1,0},{2,3},{3,2},{4,5},{5,4},{6,7},{7,6},{8,9},{9,8},{10,11... | collective-permute-start | bytes 884744 | tf_op jit(solution)/shard_map/ppermute | solution.py:34
  20.3 1.6 %collective-permute-start.3 = (f32[8,128]{1,0:T(8,128)S(1)}, f32[8,128]{1,0:T(8,128)S(1)}, u32[]{:S(2)}, u32[]{:S(2)}) collective-permute-start(f32[8,128]{1,0:T(8,128)S(1)} %broadcast_in_dim.6.refs_0_), channel_id=1, source_target_pairs={{0,3},{1,2},{2,1},{3,0},{4,7},{5,6},{6,5},{7,4},{8,11},{9,10},{10,... | collective-permute-start | bytes 12296 | tf_op jit(solution)/shard_map/ppermute | solution.py:34
  21.8 0.5 collective-permute-start.2
  22.3 4.7 %collective-permute-done.3.refs_3_.refs_2_ = f32[8,128]{1,0:T(8,128)S(1)} collective-permute-done((f32[8,128]{1,0:T(8,128)S(1)}, f32[8,128]{1,0:T(8,128)S(1)}, u32[]{:S(2)}, u32[]{:S(2)}) %collective-permute-start.3) | collective-permute-done | bytes 4128 | tf_op jit(solution)/shard_map/ppermute | solution.py:34
  27.1 0.5 collective-permute-start.9
  27.6 0.0 collective-permute-done.2.refs_2_.refs_1_
  27.6 2.4 %collective-permute-start.10 = (f32[2,96,384]{2,1,0:T(8,128)S(1)}, f32[2,96,384]{2,1,0:T(8,128)S(1)}, u32[]{:S(2)}, u32[]{:S(2)}) collective-permute-start(f32[2,96,384]{2,1,0:T(8,128)S(1)} %get-tuple-element.68), channel_id=1, source_target_pairs={{0,3},{1,2},{2,1},{3,0},{4,7},{5,6},{6,5},{7,4},{8,11},{9,10},{10,... | collective-permute-start | bytes 884744 | tf_op jit(solution)/shard_map/ppermute | solution.py:34
  30.0 0.0 collective-permute-done.11.refs_0_
  30.0 0.0 collective-permute-start.4
  30.0 0.0 collective-permute-done.12.refs_1_
  30.0 0.6 %collective-permute-start.1 = (f32[8,128]{1,0:T(8,128)S(1)}, f32[8,128]{1,0:T(8,128)S(1)}, u32[]{:S(2)}, u32[]{:S(2)}) collective-permute-start(f32[8,128]{1,0:T(8,128)S(1)} %broadcast_in_dim.6.refs_0_), channel_id=1, source_target_pairs={{0,1},{1,0},{2,3},{3,2},{4,5},{5,4},{6,7},{7,6},{8,9},{9,8},{10,11... | collective-permute-start | bytes 12296 | tf_op jit(solution)/shard_map/ppermute | solution.py:34
  30.6 0.5 shard_map.43
  31.1 4.8 %collective-permute-done.1.refs_1_.refs_0_ = f32[8,128]{1,0:T(8,128)S(1)} collective-permute-done((f32[8,128]{1,0:T(8,128)S(1)}, f32[8,128]{1,0:T(8,128)S(1)}, u32[]{:S(2)}, u32[]{:S(2)}) %collective-permute-start.1) | collective-permute-done | bytes 4128 | tf_op jit(solution)/shard_map/ppermute | solution.py:34
  35.9 1.5 %collective-permute-start.13 = (f32[2,96,256]{2,1,0:T(8,128)S(1)}, f32[2,96,256]{2,1,0:T(8,128)S(1)}, u32[]{:S(2)}, u32[]{:S(2)}) collective-permute-start(f32[2,96,256]{2,1,0:T(8,128)S(1)} %get-tuple-element.71), channel_id=1, source_target_pairs={{0,1},{1,0},{2,3},{3,2},{4,5},{5,4},{6,7},{7,6},{8,9},{9,8},{10,11... | collective-permute-start | bytes 589832 | tf_op jit(solution)/shard_map/ppermute | solution.py:34
  37.4 0.0 collective-permute-done.4.refs_0_
  37.4 0.8 %collective-permute-start.14 = (f32[2,96,256]{2,1,0:T(8,128)S(1)}, f32[2,96,256]{2,1,0:T(8,128)S(1)}, u32[]{:S(2)}, u32[]{:S(2)}) collective-permute-start(f32[2,96,256]{2,1,0:T(8,128)S(1)} %get-tuple-element.72), channel_id=1, source_target_pairs={{0,2},{1,3},{2,0},{3,1},{4,6},{5,7},{6,4},{7,5},{8,10},{9,11},{10,... | collective-permute-start | bytes 589832 | tf_op jit(solution)/shard_map/ppermute | solution.py:34
  38.2 0.0 collective-permute-done.8.refs_5_
  38.2 1.2 %collective-permute-start.15 = (f32[2,96,256]{2,1,0:T(8,128)S(1)}, f32[2,96,256]{2,1,0:T(8,128)S(1)}, u32[]{:S(2)}, u32[]{:S(2)}) collective-permute-start(f32[2,96,256]{2,1,0:T(8,128)S(1)} %get-tuple-element.73), channel_id=1, source_target_pairs={{0,3},{1,2},{2,1},{3,0},{4,7},{5,6},{6,5},{7,4},{8,11},{9,10},{10,... | collective-permute-start | bytes 589832 | tf_op jit(solution)/shard_map/ppermute | solution.py:34
  39.4 0.3 shard_map.41
  39.8 4.4 %collective-permute-done.9.refs_6_ = f32[2,96,384]{2,1,0:T(8,128)S(1)} collective-permute-done((f32[2,96,384]{2,1,0:T(8,128)S(1)}, f32[2,96,384]{2,1,0:T(8,128)S(1)}, u32[]{:S(2)}, u32[]{:S(2)}) %collective-permute-start.9) | collective-permute-done | bytes 294944 | tf_op jit(solution)/shard_map/ppermute | solution.py:34
  44.2 3.9 %collective-permute-start.5 = (f32[2,96,128]{2,1,0:T(8,128)S(1)}, f32[2,96,128]{2,1,0:T(8,128)S(1)}, u32[]{:S(2)}, u32[]{:S(2)}) collective-permute-start(f32[2,96,128]{2,1,0:T(8,128)S(1)} %get-tuple-element.63), channel_id=1, source_target_pairs={{0,1},{1,0},{2,3},{3,2},{4,5},{5,4},{6,7},{7,6},{8,9},{9,8},{10,11... | collective-permute-start | bytes 294920 | tf_op jit(solution)/shard_map/ppermute | solution.py:34
  48.1 0.0 collective-permute-done.10.refs_7_
  48.1 1.5 %collective-permute-start.6 = (f32[2,96,128]{2,1,0:T(8,128)S(1)}, f32[2,96,128]{2,1,0:T(8,128)S(1)}, u32[]{:S(2)}, u32[]{:S(2)}) collective-permute-start(f32[2,96,128]{2,1,0:T(8,128)S(1)} %get-tuple-element.64), channel_id=1, source_target_pairs={{0,2},{1,3},{2,0},{3,1},{4,6},{5,7},{6,4},{7,5},{8,10},{9,11},{10,... | collective-permute-start | bytes 294920 | tf_op jit(solution)/shard_map/ppermute | solution.py:34
  49.6 0.0 collective-permute-done.13.refs_9_
  49.6 0.0 collective-permute-start.7
  49.6 0.3 shard_map.42.refs_4_
  49.9 0.7 %collective-permute-done.14.refs_10_ = f32[2,96,256]{2,1,0:T(8,128)S(1)} collective-permute-done((f32[2,96,256]{2,1,0:T(8,128)S(1)}, f32[2,96,256]{2,1,0:T(8,128)S(1)}, u32[]{:S(2)}, u32[]{:S(2)}) %collective-permute-start.14) | collective-permute-done | bytes 196640 | tf_op jit(solution)/shard_map/ppermute | solution.py:34
  50.7 0.0 collective-permute-done.15.refs_11_
  50.7 1.5 %shard_map.44.refs_6_ = f32[2,4,96,768]{3,2,1,0:T(8,128)} custom-call(f32[8,128]{1,0:T(8,128)S(1)} %broadcast_in_dim.6.refs_0_, f32[8,128]{1,0:T(8,128)S(1)} %collective-permute-done.1.refs_1_.refs_0_, f32[8,128]{1,0:T(8,128)S(1)} %collective-permute-done.2.refs_2_.refs_1_, f32[8,128]{1,0:T(8,128)S(1)} %collective-permute-done.3.refs_3_.refs_2_, ...), custom_call_target="tpu_custom_call" | custom-call | tf_op jit(solution)/shard_map/pallas_call | solution.py:46
  52.2 0.0 collective-permute-done.5.refs_3_
  52.2 0.5 collective-permute-done.6.refs_4_
  52.7 2.4 %collective-permute-done.7.refs_5_ = f32[2,96,128]{2,1,0:T(8,128)S(1)} collective-permute-done((f32[2,96,128]{2,1,0:T(8,128)S(1)}, f32[2,96,128]{2,1,0:T(8,128)S(1)}, u32[]{:S(2)}, u32[]{:S(2)}) %collective-permute-start.7) | collective-permute-done | bytes 98336 | tf_op jit(solution)/shard_map/ppermute | solution.py:34
  55.1 0.8 %shard_map.45 = f32[2,4,96,768]{3,2,1,0:T(8,128)} custom-call(f32[8,128]{1,0:T(8,128)S(1)} %collective-permute-done.1.refs_1_.refs_0_, f32[8,128]{1,0:T(8,128)S(1)} %collective-permute-done.2.refs_2_.refs_1_, f32[8,128]{1,0:T(8,128)S(1)} %collective-permute-done.3.refs_3_.refs_2_, ...), custom_call_target="tpu_custom_call", output_to_operand_aliasing={{}: (6, {})} | custom-call | tf_op jit(solution)/shard_map/pallas_call | solution.py:46
  (1 shorter events, 0.0 us)
Async XLA Ops:
  0.9 10.4 %collective-permute-start = (f32[2,128,128]{2,1,0:T(8,128)S(1)}, f32[2,128,128]{2,1,0:T(8,128)S(1)}, u32[]{:S(2)}, u32[]{:S(2)}) collective-permute-start(f32[2,128,128]{2,1,0:T(8,128)S(1)} %shard_map.38), channel_id=1, source_target_pairs={{0,16},{4,20},{8,24},{12,28},{16,0},{20,4},{24,8},{28,12},{1,17},{... | collective-permute-start | bytes 393224 | tf_op jit(solution)/shard_map/ppermute | solution.py:34
  5.0 0.7 %copy-start = (s32[1,1,4]{2,1,0:T(1,128)S(1)}, s32[1,1,4]{2,1,0:T(1,128)}, u32[]{:S(2)}) copy-start(s32[1,1,4]{2,1,0:T(1,128)} %param.5) | copy-start | bytes 52
  8.1 22.0 %collective-permute-start.11 = (f32[2,128,256]{2,1,0:T(8,128)S(1)}, f32[2,128,256]{2,1,0:T(8,128)S(1)}, u32[]{:S(2)}, u32[]{:S(2)}) collective-permute-start(f32[2,128,256]{2,1,0:T(8,128)S(1)} %get-tuple-element.69), channel_id=1, source_target_pairs={{8,24},{12,28},{16,0},{20,4},{9,25},{13,29},{17,1},{21,5},{10,26},... | collective-permute-start | bytes 786440 | tf_op jit(solution)/shard_map/ppermute | solution.py:260
  13.0 17.0 %collective-permute-start.12 = (f32[2,128,256]{2,1,0:T(8,128)S(1)}, f32[2,128,256]{2,1,0:T(8,128)S(1)}, u32[]{:S(2)}, u32[]{:S(2)}) collective-permute-start(f32[2,128,256]{2,1,0:T(8,128)S(1)} %get-tuple-element.69), channel_id=1, source_target_pairs={{0,16},{4,20},{24,8},{28,12},{1,17},{5,21},{25,9},{29,13},{2,18},{... | collective-permute-start | bytes 786440 | tf_op jit(solution)/shard_map/ppermute | solution.py:272
  18.0 20.2 %collective-permute-start.8 = (f32[2,96,384]{2,1,0:T(8,128)S(1)}, f32[2,96,384]{2,1,0:T(8,128)S(1)}, u32[]{:S(2)}, u32[]{:S(2)}) collective-permute-start(f32[2,96,384]{2,1,0:T(8,128)S(1)} %get-tuple-element.66), channel_id=1, source_target_pairs={{0,1},{1,0},{2,3},{3,2},{4,5},{5,4},{6,7},{7,6},{8,9},{9,8},{10,11... | collective-permute-start | bytes 884744 | tf_op jit(solution)/shard_map/ppermute | solution.py:34
  20.3 6.8 %collective-permute-start.3 = (f32[8,128]{1,0:T(8,128)S(1)}, f32[8,128]{1,0:T(8,128)S(1)}, u32[]{:S(2)}, u32[]{:S(2)}) collective-permute-start(f32[8,128]{1,0:T(8,128)S(1)} %broadcast_in_dim.6.refs_0_), channel_id=1, source_target_pairs={{0,3},{1,2},{2,1},{3,0},{4,7},{5,6},{6,5},{7,4},{8,11},{9,10},{10,... | collective-permute-start | bytes 12296 | tf_op jit(solution)/shard_map/ppermute | solution.py:34
  21.8 5.8 %collective-permute-start.2 = (f32[8,128]{1,0:T(8,128)S(1)}, f32[8,128]{1,0:T(8,128)S(1)}, u32[]{:S(2)}, u32[]{:S(2)}) collective-permute-start(f32[8,128]{1,0:T(8,128)S(1)} %broadcast_in_dim.6.refs_0_), channel_id=1, source_target_pairs={{0,2},{1,3},{2,0},{3,1},{4,6},{5,7},{6,4},{7,5},{8,10},{9,11},{10,... | collective-permute-start | bytes 12296 | tf_op jit(solution)/shard_map/ppermute | solution.py:34
  27.1 17.2 %collective-permute-start.9 = (f32[2,96,384]{2,1,0:T(8,128)S(1)}, f32[2,96,384]{2,1,0:T(8,128)S(1)}, u32[]{:S(2)}, u32[]{:S(2)}) collective-permute-start(f32[2,96,384]{2,1,0:T(8,128)S(1)} %get-tuple-element.67), channel_id=1, source_target_pairs={{0,2},{1,3},{2,0},{3,1},{4,6},{5,7},{6,4},{7,5},{8,10},{9,11},{10,... | collective-permute-start | bytes 884744 | tf_op jit(solution)/shard_map/ppermute | solution.py:34
  27.6 20.5 %collective-permute-start.10 = (f32[2,96,384]{2,1,0:T(8,128)S(1)}, f32[2,96,384]{2,1,0:T(8,128)S(1)}, u32[]{:S(2)}, u32[]{:S(2)}) collective-permute-start(f32[2,96,384]{2,1,0:T(8,128)S(1)} %get-tuple-element.68), channel_id=1, source_target_pairs={{0,3},{1,2},{2,1},{3,0},{4,7},{5,6},{6,5},{7,4},{8,11},{9,10},{10,... | collective-permute-start | bytes 884744 | tf_op jit(solution)/shard_map/ppermute | solution.py:34
  30.0 7.4 %collective-permute-start.4 = (f32[2,128,128]{2,1,0:T(8,128)S(1)}, f32[2,128,128]{2,1,0:T(8,128)S(1)}, u32[]{:S(2)}, u32[]{:S(2)}) collective-permute-start(f32[2,128,128]{2,1,0:T(8,128)S(1)} %get-tuple-element.62), channel_id=1, source_target_pairs={{0,16},{4,20},{8,24},{12,28},{16,0},{20,4},{24,8},{28,12},{1,17},{... | collective-permute-start | bytes 393224 | tf_op jit(solution)/shard_map/ppermute | solution.py:34
  30.0 5.9 %collective-permute-start.1 = (f32[8,128]{1,0:T(8,128)S(1)}, f32[8,128]{1,0:T(8,128)S(1)}, u32[]{:S(2)}, u32[]{:S(2)}) collective-permute-start(f32[8,128]{1,0:T(8,128)S(1)} %broadcast_in_dim.6.refs_0_), channel_id=1, source_target_pairs={{0,1},{1,0},{2,3},{3,2},{4,5},{5,4},{6,7},{7,6},{8,9},{9,8},{10,11... | collective-permute-start | bytes 12296 | tf_op jit(solution)/shard_map/ppermute | solution.py:34
  35.9 13.7 %collective-permute-start.13 = (f32[2,96,256]{2,1,0:T(8,128)S(1)}, f32[2,96,256]{2,1,0:T(8,128)S(1)}, u32[]{:S(2)}, u32[]{:S(2)}) collective-permute-start(f32[2,96,256]{2,1,0:T(8,128)S(1)} %get-tuple-element.71), channel_id=1, source_target_pairs={{0,1},{1,0},{2,3},{3,2},{4,5},{5,4},{6,7},{7,6},{8,9},{9,8},{10,11... | collective-permute-start | bytes 589832 | tf_op jit(solution)/shard_map/ppermute | solution.py:34
  37.4 13.2 %collective-permute-start.14 = (f32[2,96,256]{2,1,0:T(8,128)S(1)}, f32[2,96,256]{2,1,0:T(8,128)S(1)}, u32[]{:S(2)}, u32[]{:S(2)}) collective-permute-start(f32[2,96,256]{2,1,0:T(8,128)S(1)} %get-tuple-element.72), channel_id=1, source_target_pairs={{0,2},{1,3},{2,0},{3,1},{4,6},{5,7},{6,4},{7,5},{8,10},{9,11},{10,... | collective-permute-start | bytes 589832 | tf_op jit(solution)/shard_map/ppermute | solution.py:34
  38.2 12.4 %collective-permute-start.15 = (f32[2,96,256]{2,1,0:T(8,128)S(1)}, f32[2,96,256]{2,1,0:T(8,128)S(1)}, u32[]{:S(2)}, u32[]{:S(2)}) collective-permute-start(f32[2,96,256]{2,1,0:T(8,128)S(1)} %get-tuple-element.73), channel_id=1, source_target_pairs={{0,3},{1,2},{2,1},{3,0},{4,7},{5,6},{6,5},{7,4},{8,11},{9,10},{10,... | collective-permute-start | bytes 589832 | tf_op jit(solution)/shard_map/ppermute | solution.py:34
  44.2 8.0 %collective-permute-start.5 = (f32[2,96,128]{2,1,0:T(8,128)S(1)}, f32[2,96,128]{2,1,0:T(8,128)S(1)}, u32[]{:S(2)}, u32[]{:S(2)}) collective-permute-start(f32[2,96,128]{2,1,0:T(8,128)S(1)} %get-tuple-element.63), channel_id=1, source_target_pairs={{0,1},{1,0},{2,3},{3,2},{4,5},{5,4},{6,7},{7,6},{8,9},{9,8},{10,11... | collective-permute-start | bytes 294920 | tf_op jit(solution)/shard_map/ppermute | solution.py:34
  48.1 4.6 %collective-permute-start.6 = (f32[2,96,128]{2,1,0:T(8,128)S(1)}, f32[2,96,128]{2,1,0:T(8,128)S(1)}, u32[]{:S(2)}, u32[]{:S(2)}) collective-permute-start(f32[2,96,128]{2,1,0:T(8,128)S(1)} %get-tuple-element.64), channel_id=1, source_target_pairs={{0,2},{1,3},{2,0},{3,1},{4,6},{5,7},{6,4},{7,5},{8,10},{9,11},{10,... | collective-permute-start | bytes 294920 | tf_op jit(solution)/shard_map/ppermute | solution.py:34
  49.6 5.5 %collective-permute-start.7 = (f32[2,96,128]{2,1,0:T(8,128)S(1)}, f32[2,96,128]{2,1,0:T(8,128)S(1)}, u32[]{:S(2)}, u32[]{:S(2)}) collective-permute-start(f32[2,96,128]{2,1,0:T(8,128)S(1)} %get-tuple-element.65), channel_id=1, source_target_pairs={{0,3},{1,2},{2,1},{3,0},{4,7},{5,6},{6,5},{7,4},{8,11},{9,10},{10,... | collective-permute-start | bytes 294920 | tf_op jit(solution)/shard_map/ppermute | solution.py:34

commit v7 on v6

--- a/solution.py
+++ b/solution.py
@@ -53,10 +53,8 @@
     return high, (x - high.astype(jnp.float32)).astype(jnp.bfloat16)
 
 
-dot = functools.partial(jnp.dot, preferred_element_type=jnp.float32)
-
-
 def matmul(left, right):
+    dot = functools.partial(jnp.dot, preferred_element_type=jnp.float32)
     rows = left[0].shape[0]
     both = dot(jnp.concatenate(left, axis=0), right[0])
     return both[:rows] + (both[rows:] + dot(left[0], right[1]))
@@ -138,12 +136,9 @@
     for level in range(LEVELS):
         pow_high[level], pow_low[level] = power
         if level + 1 < LEVELS:
-            right = [expand(x) for x in power]
-            high = dot(jnp.concatenate([*power, *left], axis=0), right[0])
-            low = dot(jnp.concatenate([power[0], left[0]], axis=0), right[1])
-            power = halves(high[:edge] + (high[edge : 2 * edge] + low[:edge]))
-            high = high[2 * edge :]
-            total = total + (high[:rows] + (high[rows:] + low[edge:]))
+            both = times([jnp.concatenate(pair, axis=0) for pair in zip(power, left)], power)
+            power = halves(both[:edge])
+            total = total + both[edge:]
         else:
             total = total + times(left, power)
         left = halves(total)

time: 56.2 us -> 56.2 us (level)
  no operation moved by 1% of the time
where the time goes in v7:
time: 56.2 us; the launch traced here: 55.9 us
  starting transfers between devices  25 us (44%)
  waiting for transfers between devices  19.7 us (35%)
  Pallas kernels  9.79 us (17%)
  between operations  0.77 us (1%)
  local copies, waits for them, and re-layouts  0.66 us (1%)
    ppermute x14, starting transfers between devices, permute(): lax.ppermute(x, axis, [(i, i ^ offset) for i in range(lax.axis_size(axis))])  20.2 us
    ppermute x14, waiting for transfers between devices, permute(): lax.ppermute(x, axis, [(i, i ^ offset) for i in range(lax.axis_size(axis))])  19.7 us
    pallas_call x8, Pallas kernels, run(): return pl.pallas_call(kernel, **options)(*args)  8.88 us
    ppermute x1, starting transfers between devices, on_device(): qse = [[early, lax.ppermute(piece, 'gx', last)]]  3.49 us
    ppermute x1, starting transfers between devices, on_device(): early = lax.ppermute(pieces[0], 'gx', first)  1.29 us
  transfers between devices with their start and end apart: 16, of which 7 were waited for; matrix products, arithmetic and copies ran while one was open for 0% of the time, Pallas kernels for 14%

profile of v7, /device:TPU:0, one launch (start us, length us, event | category | flops | bytes accessed | tf_op | source)
XLA Modules:
  0.0 55.9 jit_solution(624548373984244842)
XLA Ops:
  0.0 0.9 %shard_map.38 = f32[2,128,128]{2,1,0:T(8,128)S(1)} custom-call(f32[2,512,512]{2,1,0:T(8,128)} %bitcast.5), custom_call_target="tpu_custom_call" | custom-call | tf_op jit(solution)/shard_map/pallas_call | solution.py:232
  0.9 4.1 %collective-permute-start = (f32[2,128,128]{2,1,0:T(8,128)S(1)}, f32[2,128,128]{2,1,0:T(8,128)S(1)}, u32[]{:S(2)}, u32[]{:S(2)}) collective-permute-start(f32[2,128,128]{2,1,0:T(8,128)S(1)} %shard_map.38), channel_id=1, source_target_pairs={{0,16},{4,20},{8,24},{12,28},{16,0},{20,4},{24,8},{28,12},{1,17},{... | collective-permute-start | bytes 393224 | tf_op jit(solution)/shard_map/ppermute | solution.py:34
  5.0 0.0 copy-start
  5.0 0.7 %copy-done = s32[1,1,4]{2,1,0:T(1,128)S(1)} copy-done((s32[1,1,4]{2,1,0:T(1,128)S(1)}, s32[1,1,4]{2,1,0:T(1,128)}, u32[]{:S(2)}) %copy-start) | copy-done | bytes 40
  5.7 2.3 %shard_map.37 = (f32[2,128,256]{2,1,0:T(8,128)S(1)}, f32[2,128,128]{2,1,0:T(8,128)S(1)}, f32[2,384,384]{2,1,0:T(8,128)S(1)}, f32[384,256]{1,0:T(8,128)S(1)}, bf1...) custom-call(s32[4]{0:T(128)S(1)} %bitcast.4, ...), custom_call_target="tpu_custom_call" | custom-call | tf_op jit(solution)/shard_map/pallas_call | solution.py:46
  8.1 1.3 %collective-permute-start.11 = (f32[2,128,256]{2,1,0:T(8,128)S(1)}, f32[2,128,256]{2,1,0:T(8,128)S(1)}, u32[]{:S(2)}, u32[]{:S(2)}) collective-permute-start(f32[2,128,256]{2,1,0:T(8,128)S(1)} %get-tuple-element.69), channel_id=1, source_target_pairs={{8,24},{12,28},{16,0},{20,4},{9,25},{13,29},{17,1},{21,5},{10,26},... | collective-permute-start | bytes 786440 | tf_op jit(solution)/shard_map/ppermute | solution.py:255
  9.4 2.0 %collective-permute-done.qss_ref = f32[2,128,128]{2,1,0:T(8,128)S(1)} collective-permute-done((f32[2,128,128]{2,1,0:T(8,128)S(1)}, f32[2,128,128]{2,1,0:T(8,128)S(1)}, u32[]{:S(2)}, u32[]{:S(2)}) %collective-permute-start) | collective-permute-done | bytes 131104 | tf_op jit(solution)/shard_map/ppermute | solution.py:34
  11.3 1.6 %shard_map.39 = (bf16[4,128,256]{2,1,0:T(8,128)(2,1)S(1)}, bf16[4,128,256]{2,1,0:T(8,128)(2,1)S(1)}, bf16[128,768]{1,0:T(8,128)(2,1)S(1)}, bf16[128,768]{1,0:T(8...) custom-call(f32[2,128,128]{2,1,0:T(8,128)S(1)} %collective-permute-done.qss_ref,, ...), custom_call_target="tpu_custom_call" | custom-call | tf_op jit(solution)/shard_map/pallas_call | solution.py:46
  13.0 3.5 %collective-permute-start.12 = (f32[2,128,256]{2,1,0:T(8,128)S(1)}, f32[2,128,256]{2,1,0:T(8,128)S(1)}, u32[]{:S(2)}, u32[]{:S(2)}) collective-permute-start(f32[2,128,256]{2,1,0:T(8,128)S(1)} %get-tuple-element.69), channel_id=1, source_target_pairs={{0,16},{4,20},{24,8},{28,12},{1,17},{5,21},{25,9},{29,13},{2,18},{... | collective-permute-start | bytes 786440 | tf_op jit(solution)/shard_map/ppermute | solution.py:267
  16.5 1.5 %shard_map.40 = (bf16[288,256]{1,0:T(8,128)(2,1)S(1)}, bf16[288,256]{1,0:T(8,128)(2,1)S(1)}, f32[2,96,384]{2,1,0:T(8,128)S(1)}, f32[2,96,384]{2,1,0:T(8,128)S(1)}) custom-call(f32[2,384,384]{2,1,0:T(8,128)S(1)} %get-tuple-element.40.base_ref, f32[384,256]{1,0:T(8,128)S(1)} %get-tuple-element.41.res_ref, bf16[384,256]{1,0:T(8,128)(2,1)S(1)} %get-tuple-element.42.res_high, ...), custom_call_target="tpu_custom_call" | custom-call | tf_op jit(solution)/shard_map/pallas_call | solution.py:46
  18.0 1.6 %collective-permute-start.8 = (f32[2,96,384]{2,1,0:T(8,128)S(1)}, f32[2,96,384]{2,1,0:T(8,128)S(1)}, u32[]{:S(2)}, u32[]{:S(2)}) collective-permute-start(f32[2,96,384]{2,1,0:T(8,128)S(1)} %get-tuple-element.66), channel_id=1, source_target_pairs={{0,1},{1,0},{2,3},{3,2},{4,5},{5,4},{6,7},{7,6},{8,9},{9,8},{10,11... | collective-permute-start | bytes 884744 | tf_op jit(solution)/shard_map/ppermute | solution.py:34
  20.3 1.6 %collective-permute-start.3 = (f32[8,128]{1,0:T(8,128)S(1)}, f32[8,128]{1,0:T(8,128)S(1)}, u32[]{:S(2)}, u32[]{:S(2)}) collective-permute-start(f32[8,128]{1,0:T(8,128)S(1)} %broadcast_in_dim.6.refs_0_), channel_id=1, source_target_pairs={{0,3},{1,2},{2,1},{3,0},{4,7},{5,6},{6,5},{7,4},{8,11},{9,10},{10,... | collective-permute-start | bytes 12296 | tf_op jit(solution)/shard_map/ppermute | solution.py:34
  21.8 0.5 collective-permute-start.2
  22.3 4.7 %collective-permute-done.3.refs_3_.refs_2_ = f32[8,128]{1,0:T(8,128)S(1)} collective-permute-done((f32[8,128]{1,0:T(8,128)S(1)}, f32[8,128]{1,0:T(8,128)S(1)}, u32[]{:S(2)}, u32[]{:S(2)}) %collective-permute-start.3) | collective-permute-done | bytes 4128 | tf_op jit(solution)/shard_map/ppermute | solution.py:34
  27.0 0.5 collective-permute-start.9
  27.6 0.0 collective-permute-done.2.refs_2_.refs_1_
  27.6 2.4 %collective-permute-start.10 = (f32[2,96,384]{2,1,0:T(8,128)S(1)}, f32[2,96,384]{2,1,0:T(8,128)S(1)}, u32[]{:S(2)}, u32[]{:S(2)}) collective-permute-start(f32[2,96,384]{2,1,0:T(8,128)S(1)} %get-tuple-element.68), channel_id=1, source_target_pairs={{0,3},{1,2},{2,1},{3,0},{4,7},{5,6},{6,5},{7,4},{8,11},{9,10},{10,... | collective-permute-start | bytes 884744 | tf_op jit(solution)/shard_map/ppermute | solution.py:34
  30.0 0.0 collective-permute-done.11.refs_0_
  30.0 0.0 collective-permute-start.4
  30.0 0.0 collective-permute-done.12.refs_1_
  30.0 0.6 %collective-permute-start.1 = (f32[8,128]{1,0:T(8,128)S(1)}, f32[8,128]{1,0:T(8,128)S(1)}, u32[]{:S(2)}, u32[]{:S(2)}) collective-permute-start(f32[8,128]{1,0:T(8,128)S(1)} %broadcast_in_dim.6.refs_0_), channel_id=1, source_target_pairs={{0,1},{1,0},{2,3},{3,2},{4,5},{5,4},{6,7},{7,6},{8,9},{9,8},{10,11... | collective-permute-start | bytes 12296 | tf_op jit(solution)/shard_map/ppermute | solution.py:34
  30.6 0.5 shard_map.43
  31.1 4.8 %collective-permute-done.1.refs_1_.refs_0_ = f32[8,128]{1,0:T(8,128)S(1)} collective-permute-done((f32[8,128]{1,0:T(8,128)S(1)}, f32[8,128]{1,0:T(8,128)S(1)}, u32[]{:S(2)}, u32[]{:S(2)}) %collective-permute-start.1) | collective-permute-done | bytes 4128 | tf_op jit(solution)/shard_map/ppermute | solution.py:34
  35.9 1.5 %collective-permute-start.13 = (f32[2,96,256]{2,1,0:T(8,128)S(1)}, f32[2,96,256]{2,1,0:T(8,128)S(1)}, u32[]{:S(2)}, u32[]{:S(2)}) collective-permute-start(f32[2,96,256]{2,1,0:T(8,128)S(1)} %get-tuple-element.71), channel_id=1, source_target_pairs={{0,1},{1,0},{2,3},{3,2},{4,5},{5,4},{6,7},{7,6},{8,9},{9,8},{10,11... | collective-permute-start | bytes 589832 | tf_op jit(solution)/shard_map/ppermute | solution.py:34
  37.4 0.0 collective-permute-done.4.refs_0_
  37.4 0.8 %collective-permute-start.14 = (f32[2,96,256]{2,1,0:T(8,128)S(1)}, f32[2,96,256]{2,1,0:T(8,128)S(1)}, u32[]{:S(2)}, u32[]{:S(2)}) collective-permute-start(f32[2,96,256]{2,1,0:T(8,128)S(1)} %get-tuple-element.72), channel_id=1, source_target_pairs={{0,2},{1,3},{2,0},{3,1},{4,6},{5,7},{6,4},{7,5},{8,10},{9,11},{10,... | collective-permute-start | bytes 589832 | tf_op jit(solution)/shard_map/ppermute | solution.py:34
  38.2 0.0 collective-permute-done.8.refs_5_
  38.2 1.2 %collective-permute-start.15 = (f32[2,96,256]{2,1,0:T(8,128)S(1)}, f32[2,96,256]{2,1,0:T(8,128)S(1)}, u32[]{:S(2)}, u32[]{:S(2)}) collective-permute-start(f32[2,96,256]{2,1,0:T(8,128)S(1)} %get-tuple-element.73), channel_id=1, source_target_pairs={{0,3},{1,2},{2,1},{3,0},{4,7},{5,6},{6,5},{7,4},{8,11},{9,10},{10,... | collective-permute-start | bytes 589832 | tf_op jit(solution)/shard_map/ppermute | solution.py:34
  39.4 0.3 shard_map.41
  39.8 4.4 %collective-permute-done.9.refs_6_ = f32[2,96,384]{2,1,0:T(8,128)S(1)} collective-permute-done((f32[2,96,384]{2,1,0:T(8,128)S(1)}, f32[2,96,384]{2,1,0:T(8,128)S(1)}, u32[]{:S(2)}, u32[]{:S(2)}) %collective-permute-start.9) | collective-permute-done | bytes 294944 | tf_op jit(solution)/shard_map/ppermute | solution.py:34
  44.2 3.9 %collective-permute-start.5 = (f32[2,96,128]{2,1,0:T(8,128)S(1)}, f32[2,96,128]{2,1,0:T(8,128)S(1)}, u32[]{:S(2)}, u32[]{:S(2)}) collective-permute-start(f32[2,96,128]{2,1,0:T(8,128)S(1)} %get-tuple-element.63), channel_id=1, source_target_pairs={{0,1},{1,0},{2,3},{3,2},{4,5},{5,4},{6,7},{7,6},{8,9},{9,8},{10,11... | collective-permute-start | bytes 294920 | tf_op jit(solution)/shard_map/ppermute | solution.py:34
  48.1 0.0 collective-permute-done.10.refs_7_
  48.1 1.5 %collective-permute-start.6 = (f32[2,96,128]{2,1,0:T(8,128)S(1)}, f32[2,96,128]{2,1,0:T(8,128)S(1)}, u32[]{:S(2)}, u32[]{:S(2)}) collective-permute-start(f32[2,96,128]{2,1,0:T(8,128)S(1)} %get-tuple-element.64), channel_id=1, source_target_pairs={{0,2},{1,3},{2,0},{3,1},{4,6},{5,7},{6,4},{7,5},{8,10},{9,11},{10,... | collective-permute-start | bytes 294920 | tf_op jit(solution)/shard_map/ppermute | solution.py:34
  49.6 0.0 collective-permute-done.13.refs_9_
  49.6 0.0 collective-permute-start.7
  49.6 0.3 shard_map.42.refs_4_
  49.9 0.7 %collective-permute-done.14.refs_10_ = f32[2,96,256]{2,1,0:T(8,128)S(1)} collective-permute-done((f32[2,96,256]{2,1,0:T(8,128)S(1)}, f32[2,96,256]{2,1,0:T(8,128)S(1)}, u32[]{:S(2)}, u32[]{:S(2)}) %collective-permute-start.14) | collective-permute-done | bytes 196640 | tf_op jit(solution)/shard_map/ppermute | solution.py:34
  50.6 0.0 collective-permute-done.15.refs_11_
  50.6 1.5 %shard_map.44.refs_6_ = f32[2,4,96,768]{3,2,1,0:T(8,128)} custom-call(f32[8,128]{1,0:T(8,128)S(1)} %broadcast_in_dim.6.refs_0_, f32[8,128]{1,0:T(8,128)S(1)} %collective-permute-done.1.refs_1_.refs_0_, f32[8,128]{1,0:T(8,128)S(1)} %collective-permute-done.2.refs_2_.refs_1_, f32[8,128]{1,0:T(8,128)S(1)} %collective-permute-done.3.refs_3_.refs_2_, ...), custom_call_target="tpu_custom_call" | custom-call | tf_op jit(solution)/shard_map/pallas_call | solution.py:46
  52.1 0.0 collective-permute-done.5.refs_3_
  52.2 0.6 collective-permute-done.6.refs_4_
  52.7 2.4 %collective-permute-done.7.refs_5_ = f32[2,96,128]{2,1,0:T(8,128)S(1)} collective-permute-done((f32[2,96,128]{2,1,0:T(8,128)S(1)}, f32[2,96,128]{2,1,0:T(8,128)S(1)}, u32[]{:S(2)}, u32[]{:S(2)}) %collective-permute-start.7) | collective-permute-done | bytes 98336 | tf_op jit(solution)/shard_map/ppermute | solution.py:34
  55.1 0.8 %shard_map.45 = f32[2,4,96,768]{3,2,1,0:T(8,128)} custom-call(f32[8,128]{1,0:T(8,128)S(1)} %collective-permute-done.1.refs_1_.refs_0_, f32[8,128]{1,0:T(8,128)S(1)} %collective-permute-done.2.refs_2_.refs_1_, f32[8,128]{1,0:T(8,128)S(1)} %collective-permute-done.3.refs_3_.refs_2_, ...), custom_call_target="tpu_custom_call", output_to_operand_aliasing={{}: (6, {})} | custom-call | tf_op jit(solution)/shard_map/pallas_call | solution.py:46
  (1 shorter events, 0.0 us)
Async XLA Ops:
  0.9 10.4 %collective-permute-start = (f32[2,128,128]{2,1,0:T(8,128)S(1)}, f32[2,128,128]{2,1,0:T(8,128)S(1)}, u32[]{:S(2)}, u32[]{:S(2)}) collective-permute-start(f32[2,128,128]{2,1,0:T(8,128)S(1)} %shard_map.38), channel_id=1, source_target_pairs={{0,16},{4,20},{8,24},{12,28},{16,0},{20,4},{24,8},{28,12},{1,17},{... | collective-permute-start | bytes 393224 | tf_op jit(solution)/shard_map/ppermute | solution.py:34
  5.0 0.7 %copy-start = (s32[1,1,4]{2,1,0:T(1,128)S(1)}, s32[1,1,4]{2,1,0:T(1,128)}, u32[]{:S(2)}) copy-start(s32[1,1,4]{2,1,0:T(1,128)} %param.5) | copy-start | bytes 52
  8.1 22.0 %collective-permute-start.11 = (f32[2,128,256]{2,1,0:T(8,128)S(1)}, f32[2,128,256]{2,1,0:T(8,128)S(1)}, u32[]{:S(2)}, u32[]{:S(2)}) collective-permute-start(f32[2,128,256]{2,1,0:T(8,128)S(1)} %get-tuple-element.69), channel_id=1, source_target_pairs={{8,24},{12,28},{16,0},{20,4},{9,25},{13,29},{17,1},{21,5},{10,26},... | collective-permute-start | bytes 786440 | tf_op jit(solution)/shard_map/ppermute | solution.py:255
  13.0 17.0 %collective-permute-start.12 = (f32[2,128,256]{2,1,0:T(8,128)S(1)}, f32[2,128,256]{2,1,0:T(8,128)S(1)}, u32[]{:S(2)}, u32[]{:S(2)}) collective-permute-start(f32[2,128,256]{2,1,0:T(8,128)S(1)} %get-tuple-element.69), channel_id=1, source_target_pairs={{0,16},{4,20},{24,8},{28,12},{1,17},{5,21},{25,9},{29,13},{2,18},{... | collective-permute-start | bytes 786440 | tf_op jit(solution)/shard_map/ppermute | solution.py:267
  18.0 20.2 %collective-permute-start.8 = (f32[2,96,384]{2,1,0:T(8,128)S(1)}, f32[2,96,384]{2,1,0:T(8,128)S(1)}, u32[]{:S(2)}, u32[]{:S(2)}) collective-permute-start(f32[2,96,384]{2,1,0:T(8,128)S(1)} %get-tuple-element.66), channel_id=1, source_target_pairs={{0,1},{1,0},{2,3},{3,2},{4,5},{5,4},{6,7},{7,6},{8,9},{9,8},{10,11... | collective-permute-start | bytes 884744 | tf_op jit(solution)/shard_map/ppermute | solution.py:34
  20.3 6.8 %collective-permute-start.3 = (f32[8,128]{1,0:T(8,128)S(1)}, f32[8,128]{1,0:T(8,128)S(1)}, u32[]{:S(2)}, u32[]{:S(2)}) collective-permute-start(f32[8,128]{1,0:T(8,128)S(1)} %broadcast_in_dim.6.refs_0_), channel_id=1, source_target_pairs={{0,3},{1,2},{2,1},{3,0},{4,7},{5,6},{6,5},{7,4},{8,11},{9,10},{10,... | collective-permute-start | bytes 12296 | tf_op jit(solution)/shard_map/ppermute | solution.py:34
  21.8 5.7 %collective-permute-start.2 = (f32[8,128]{1,0:T(8,128)S(1)}, f32[8,128]{1,0:T(8,128)S(1)}, u32[]{:S(2)}, u32[]{:S(2)}) collective-permute-start(f32[8,128]{1,0:T(8,128)S(1)} %broadcast_in_dim.6.refs_0_), channel_id=1, source_target_pairs={{0,2},{1,3},{2,0},{3,1},{4,6},{5,7},{6,4},{7,5},{8,10},{9,11},{10,... | collective-permute-start | bytes 12296 | tf_op jit(solution)/shard_map/ppermute | solution.py:34
  27.0 17.2 %collective-permute-start.9 = (f32[2,96,384]{2,1,0:T(8,128)S(1)}, f32[2,96,384]{2,1,0:T(8,128)S(1)}, u32[]{:S(2)}, u32[]{:S(2)}) collective-permute-start(f32[2,96,384]{2,1,0:T(8,128)S(1)} %get-tuple-element.67), channel_id=1, source_target_pairs={{0,2},{1,3},{2,0},{3,1},{4,6},{5,7},{6,4},{7,5},{8,10},{9,11},{10,... | collective-permute-start | bytes 884744 | tf_op jit(solution)/shard_map/ppermute | solution.py:34
  27.6 20.5 %collective-permute-start.10 = (f32[2,96,384]{2,1,0:T(8,128)S(1)}, f32[2,96,384]{2,1,0:T(8,128)S(1)}, u32[]{:S(2)}, u32[]{:S(2)}) collective-permute-start(f32[2,96,384]{2,1,0:T(8,128)S(1)} %get-tuple-element.68), channel_id=1, source_target_pairs={{0,3},{1,2},{2,1},{3,0},{4,7},{5,6},{6,5},{7,4},{8,11},{9,10},{10,... | collective-permute-start | bytes 884744 | tf_op jit(solution)/shard_map/ppermute | solution.py:34
  30.0 7.4 %collective-permute-start.4 = (f32[2,128,128]{2,1,0:T(8,128)S(1)}, f32[2,128,128]{2,1,0:T(8,128)S(1)}, u32[]{:S(2)}, u32[]{:S(2)}) collective-permute-start(f32[2,128,128]{2,1,0:T(8,128)S(1)} %get-tuple-element.62), channel_id=1, source_target_pairs={{0,16},{4,20},{8,24},{12,28},{16,0},{20,4},{24,8},{28,12},{1,17},{... | collective-permute-start | bytes 393224 | tf_op jit(solution)/shard_map/ppermute | solution.py:34
  30.0 5.9 %collective-permute-start.1 = (f32[8,128]{1,0:T(8,128)S(1)}, f32[8,128]{1,0:T(8,128)S(1)}, u32[]{:S(2)}, u32[]{:S(2)}) collective-permute-start(f32[8,128]{1,0:T(8,128)S(1)} %broadcast_in_dim.6.refs_0_), channel_id=1, source_target_pairs={{0,1},{1,0},{2,3},{3,2},{4,5},{5,4},{6,7},{7,6},{8,9},{9,8},{10,11... | collective-permute-start | bytes 12296 | tf_op jit(solution)/shard_map/ppermute | solution.py:34
  35.9 13.7 %collective-permute-start.13 = (f32[2,96,256]{2,1,0:T(8,128)S(1)}, f32[2,96,256]{2,1,0:T(8,128)S(1)}, u32[]{:S(2)}, u32[]{:S(2)}) collective-permute-start(f32[2,96,256]{2,1,0:T(8,128)S(1)} %get-tuple-element.71), channel_id=1, source_target_pairs={{0,1},{1,0},{2,3},{3,2},{4,5},{5,4},{6,7},{7,6},{8,9},{9,8},{10,11... | collective-permute-start | bytes 589832 | tf_op jit(solution)/shard_map/ppermute | solution.py:34
  37.4 13.2 %collective-permute-start.14 = (f32[2,96,256]{2,1,0:T(8,128)S(1)}, f32[2,96,256]{2,1,0:T(8,128)S(1)}, u32[]{:S(2)}, u32[]{:S(2)}) collective-permute-start(f32[2,96,256]{2,1,0:T(8,128)S(1)} %get-tuple-element.72), channel_id=1, source_target_pairs={{0,2},{1,3},{2,0},{3,1},{4,6},{5,7},{6,4},{7,5},{8,10},{9,11},{10,... | collective-permute-start | bytes 589832 | tf_op jit(solution)/shard_map/ppermute | solution.py:34
  38.2 12.4 %collective-permute-start.15 = (f32[2,96,256]{2,1,0:T(8,128)S(1)}, f32[2,96,256]{2,1,0:T(8,128)S(1)}, u32[]{:S(2)}, u32[]{:S(2)}) collective-permute-start(f32[2,96,256]{2,1,0:T(8,128)S(1)} %get-tuple-element.73), channel_id=1, source_target_pairs={{0,3},{1,2},{2,1},{3,0},{4,7},{5,6},{6,5},{7,4},{8,11},{9,10},{10,... | collective-permute-start | bytes 589832 | tf_op jit(solution)/shard_map/ppermute | solution.py:34
  44.2 7.9 %collective-permute-start.5 = (f32[2,96,128]{2,1,0:T(8,128)S(1)}, f32[2,96,128]{2,1,0:T(8,128)S(1)}, u32[]{:S(2)}, u32[]{:S(2)}) collective-permute-start(f32[2,96,128]{2,1,0:T(8,128)S(1)} %get-tuple-element.63), channel_id=1, source_target_pairs={{0,1},{1,0},{2,3},{3,2},{4,5},{5,4},{6,7},{7,6},{8,9},{9,8},{10,11... | collective-permute-start | bytes 294920 | tf_op jit(solution)/shard_map/ppermute | solution.py:34
  48.1 4.6 %collective-permute-start.6 = (f32[2,96,128]{2,1,0:T(8,128)S(1)}, f32[2,96,128]{2,1,0:T(8,128)S(1)}, u32[]{:S(2)}, u32[]{:S(2)}) collective-permute-start(f32[2,96,128]{2,1,0:T(8,128)S(1)} %get-tuple-element.64), channel_id=1, source_target_pairs={{0,2},{1,3},{2,0},{3,1},{4,6},{5,7},{6,4},{7,5},{8,10},{9,11},{10,... | collective-permute-start | bytes 294920 | tf_op jit(solution)/shard_map/ppermute | solution.py:34
  49.6 5.5 %collective-permute-start.7 = (f32[2,96,128]{2,1,0:T(8,128)S(1)}, f32[2,96,128]{2,1,0:T(8,128)S(1)}, u32[]{:S(2)}, u32[]{:S(2)}) collective-permute-start(f32[2,96,128]{2,1,0:T(8,128)S(1)} %get-tuple-element.65), channel_id=1, source_target_pairs={{0,3},{1,2},{2,1},{3,0},{4,7},{5,6},{6,5},{7,4},{8,11},{9,10},{10,... | collective-permute-start | bytes 294920 | tf_op jit(solution)/shard_map/ppermute | solution.py:34
